TPU v7x, 32 devices: a whole 2x2x4 slice. The times are simulated.
32 devices in a mesh: dp: 2 (over core), bal: 16 (over z, y, x).
Axes of the slice: x: 2, y: 2, z: 4, core: 2. Of those that a mesh axis runs over, the one named last changes fastest.
Arguments:
- tokens: bfloat16 [64, 512, 768], P(('dp', 'bal')), may hold values from -6 to 6
- cotangent: bfloat16 [64, 512, 768], P(('dp', 'bal')), may hold values from -6 to 6
- seq_lengths: int32 [64], P(('dp', 'bal')), may hold values from 256 to 512, as said below
- token_mask: int32 [64, 512], P(('dp', 'bal')), may hold values from 0 to 1, as said below
- step_count: int32 [1], replicated, may hold values from 1 to 20
- attn_master: float32 [2, 4, 768, 768], P(None, None, 'bal')
- attn_first: float32 [2, 4, 768, 768], P(None, None, 'bal'), may hold values from -0.00018310547 to 0.00018310547
- attn_second: float32 [2, 4, 768, 768], P(None, None, 'bal'), may hold values from 7.0550676e-11 to 2.822027e-10
- up_master: float32 [2, 768, 3072], P(None, 'bal'), may hold values from -0.21875 to 0.21875
- up_first: float32 [2, 768, 3072], P(None, 'bal'), may hold values from -0.00018310547 to 0.00018310547
- up_second: float32 [2, 768, 3072], P(None, 'bal'), may hold values from 7.0550676e-11 to 2.822027e-10
- down_master: float32 [2, 3072, 768], P(None, 'bal'), may hold values from -0.109375 to 0.109375
- down_first: float32 [2, 3072, 768], P(None, 'bal'), may hold values from -0.00018310547 to 0.00018310547
- down_second: float32 [2, 3072, 768], P(None, 'bal'), may hold values from 7.0550676e-11 to 2.822027e-10
- small_master: float32 [2, 12, 768], P(None, None, 'bal')
- small_first: float32 [2, 12, 768], P(None, None, 'bal'), may hold values from -0.00048828125 to 0.00048828125
- small_second: float32 [2, 12, 768], P(None, None, 'bal'), may hold values from 6.349561e-10 to 2.5398244e-09
Outputs:
- output: bfloat16 [64, 512, 768], P(('dp', 'bal'))
- input_grad: bfloat16 [64, 512, 768], P(('dp', 'bal'))
- grad_norm: float32 [1], replicated
- attn_weight: float32 [2, 4, 768, 768], P(None, None, 'bal')
- attn_first_new: float32 [2, 4, 768, 768], P(None, None, 'bal')
- attn_second_new: float32 [2, 4, 768, 768], P(None, None, 'bal')
- attn_copy: bfloat16 [2, 4, 768, 768], P(None, None, 'bal')
- up_weight: float32 [2, 768, 3072], P(None, 'bal')
- up_first_new: float32 [2, 768, 3072], P(None, 'bal')
- up_second_new: float32 [2, 768, 3072], P(None, 'bal')
- up_copy: bfloat16 [2, 768, 3072], P(None, 'bal')
- down_weight: float32 [2, 3072, 768], P(None, 'bal')
- down_first_new: float32 [2, 3072, 768], P(None, 'bal')
- down_second_new: float32 [2, 3072, 768], P(None, 'bal')
- down_copy: bfloat16 [2, 3072, 768], P(None, 'bal')
- small_weight: float32 [2, 12, 768], P(None, None, 'bal')
- small_first_new: float32 [2, 12, 768], P(None, None, 'bal')
- small_second_new: float32 [2, 12, 768], P(None, None, 'bal')
- small_copy: bfloat16 [2, 12, 768], P(None, None, 'bal')
Inputs may be any that keep to these rules, and one draw needn't show every extreme that they name: `seq_lengths`: among the 2 sequences of each device one has length 512. `token_mask`: ones stand only at positions below the sequence's length. In every aligned run of 16 devices along bal one device holds exactly 384 ones among its 1024 positions and each other device holds at least 1 and at most 128.
All inputs are finite; a program needn't handle non-finite values.
Results may differ from a plain program's by a relative error of at most 0.019.
The roundings to bfloat16 on the way count: a program that leaves them out, or rounds other values in their place, can miss the bound.
Values may be sent and summed in bfloat16 or wider, within the bound.
No kernel may reach another device: no remote copies, remote signals or barrier semaphores. Data moves between devices by JAX's collectives and lax.ppermute only.
A program may use at most 384 MiB of HBM per device.

v0:
```python
import math

import jax
import jax.numpy as jnp
from jax import lax
from jax.sharding import PartitionSpec as P

HEADS = 12
HEAD_DIM = 64
MCAP = 384


LN_EPS = 1e-06
NEG_FILL = -1000000000.0
CLIP_NORM = 1.0
LEARN_RATE = 0.05
SMALL_RATE = 0.25
BETA_FIRST = 0.9
BETA_SECOND = 0.999
ADAM_EPS = 1e-08
WEIGHT_DECAY = 0.01


def forward_product(left_side, right_side):
    return jnp.dot(left_side, right_side, preferred_element_type=jnp.float32)


def weight_grad(left_side, right_side):
    return lax.dot_general(
        left_side, right_side, (((0,), (0,)), ((), ())), preferred_element_type=jnp.float32
    )


def back_product(left_side, right_side):
    return lax.dot_general(
        left_side, right_side, (((1,), (1,)), ((), ())), preferred_element_type=jnp.float32
    )


def norm_forward(residual, norm_gain, norm_shift):
    centered = residual - jnp.mean(residual, axis=-1, keepdims=True)
    variance = jnp.mean(centered * centered, axis=-1, keepdims=True)
    inv_std = lax.rsqrt(variance + LN_EPS)
    normal_part = centered * inv_std
    return (normal_part * norm_gain + norm_shift, normal_part, inv_std)


def norm_backward(d_out, normal_part, inv_std, norm_gain):
    d_normal = d_out * norm_gain
    d_resid = inv_std * (
        d_normal
        - jnp.mean(d_normal, axis=-1, keepdims=True)
        - normal_part * jnp.mean(d_normal * normal_part, axis=-1, keepdims=True)
    )
    return (d_resid, jnp.sum(d_out * normal_part, axis=0), jnp.sum(d_out, axis=0))


def gelu_slope(pre_act):
    return (
        0.5 * (1.0 + lax.erf(pre_act * 0.7071067811865476))
        + pre_act * jnp.exp(-0.5 * pre_act * pre_act) * 0.3989422804014327
    )


def head_split(flat_rows, seq_count):
    return flat_rows.reshape(seq_count, -1, HEADS, HEAD_DIM)


def key_mask(seq_lengths, length):
    return (jnp.arange(length)[None, :] < seq_lengths[:, None])[:, None, None, :]


def score_block(query_heads, key_heads, mask_keys):
    scores = jnp.einsum(
        "sqhd,skhd->shqk", query_heads, key_heads, preferred_element_type=jnp.float32
    ) * (1.0 / math.sqrt(HEAD_DIM))
    return jnp.where(mask_keys, scores, NEG_FILL)


def attend_forward(hidden, attn_layer, small_layer, seq_lengths):
    seq_count, length, model_width = hidden.shape
    flat_rows = hidden.reshape(seq_count * length, model_width)
    flat_low = flat_rows.astype(jnp.bfloat16)
    queries = (forward_product(flat_low, attn_layer[0]) + small_layer[0]).astype(jnp.bfloat16)
    key_rows = forward_product(flat_low, attn_layer[1]).astype(jnp.bfloat16)
    values = (forward_product(flat_low, attn_layer[2]) + small_layer[1]).astype(jnp.bfloat16)
    scores = score_block(
        head_split(queries, seq_count),
        head_split(key_rows, seq_count),
        key_mask(seq_lengths, length),
    )
    row_top = jnp.max(scores, axis=-1, keepdims=True)
    exp_scores = jnp.exp(scores - row_top)
    row_total = jnp.sum(exp_scores, axis=-1, keepdims=True)
    probs_low = (exp_scores / row_total).astype(jnp.bfloat16)
    log_total = row_top + jnp.log(row_total)
    mixed_heads = jnp.einsum(
        "shqk,skhd->sqhd",
        probs_low,
        head_split(values, seq_count),
        preferred_element_type=jnp.float32,
    )
    mixed_heads = mixed_heads.reshape(seq_count * length, model_width).astype(jnp.bfloat16)
    branch = forward_product(mixed_heads, attn_layer[3]) + small_layer[2]
    normed, normal_part, inv_std = norm_forward(flat_rows + branch, small_layer[3], small_layer[4])
    return (
        normed,
        (flat_low, queries, key_rows, values, log_total, mixed_heads, normal_part, inv_std),
    )


def attend_backward(d_normed, kept_state, attn_layer, small_layer, seq_lengths, seq_count, length):
    flat_low, queries, key_rows, values, log_total, mixed_heads, normal_part, inv_std = kept_state
    row_count, model_width = flat_low.shape
    d_resid, d_gain, d_shift = norm_backward(d_normed, normal_part, inv_std, small_layer[3])
    d_branch = d_resid.astype(jnp.bfloat16)
    d_out_bias = jnp.sum(d_branch.astype(jnp.float32), axis=0)
    d_out_weight = weight_grad(mixed_heads, d_branch)
    d_mixed = head_split(back_product(d_branch, attn_layer[3]).astype(jnp.bfloat16), seq_count)
    query_heads = head_split(queries, seq_count)
    key_heads = head_split(key_rows, seq_count)
    value_heads = head_split(values, seq_count)
    scores = score_block(query_heads, key_heads, key_mask(seq_lengths, length))
    attn_probs = jnp.exp(scores - log_total)
    d_values = jnp.einsum(
        "shqk,sqhd->skhd",
        attn_probs.astype(jnp.bfloat16),
        d_mixed,
        preferred_element_type=jnp.float32,
    )
    d_values = d_values.reshape(row_count, model_width).astype(jnp.bfloat16)
    d_probs = jnp.einsum(
        "sqhd,skhd->shqk", d_mixed, value_heads, preferred_element_type=jnp.float32
    )
    d_scores = (
        attn_probs * (d_probs - jnp.sum(attn_probs * d_probs, axis=-1, keepdims=True))
    ).astype(jnp.bfloat16)
    scale_factor = 1.0 / math.sqrt(HEAD_DIM)
    d_queries = (
        jnp.einsum("shqk,skhd->sqhd", d_scores, key_heads, preferred_element_type=jnp.float32)
        * scale_factor
    )
    d_queries = d_queries.reshape(row_count, model_width).astype(jnp.bfloat16)
    d_keys = (
        jnp.einsum("shqk,sqhd->skhd", d_scores, query_heads, preferred_element_type=jnp.float32)
        * scale_factor
    )
    d_keys = d_keys.reshape(row_count, model_width).astype(jnp.bfloat16)
    weight_set = jnp.stack(
        [
            weight_grad(flat_low, d_queries),
            weight_grad(flat_low, d_keys),
            weight_grad(flat_low, d_values),
            d_out_weight,
        ]
    )
    d_hidden = (
        d_resid
        + back_product(d_queries, attn_layer[0])
        + back_product(d_keys, attn_layer[1])
        + back_product(d_values, attn_layer[2])
    )
    small_rows = jnp.stack(
        [
            jnp.sum(d_queries.astype(jnp.float32), axis=0),
            jnp.sum(d_values.astype(jnp.float32), axis=0),
            d_out_bias,
            d_gain,
            d_shift,
        ]
    )
    return (d_hidden, weight_set, small_rows)


def feed_forward(rows_in, up_layer, down_layer, small_layer):
    rows_low = rows_in.astype(jnp.bfloat16)
    pre_act = forward_product(rows_low, up_layer) + small_layer[5:9].reshape(-1)
    act_low = jax.nn.gelu(pre_act, approximate=False).astype(jnp.bfloat16)
    branch = forward_product(act_low, down_layer) + small_layer[9]
    normed, normal_part, inv_std = norm_forward(rows_in + branch, small_layer[10], small_layer[11])
    return (normed, (rows_low, pre_act, act_low, normal_part, inv_std))


def feed_backward(d_normed, kept_state, up_layer, down_layer, small_layer):
    rows_low, pre_act, act_low, normal_part, inv_std = kept_state
    d_resid, d_gain, d_shift = norm_backward(d_normed, normal_part, inv_std, small_layer[10])
    d_branch = d_resid.astype(jnp.bfloat16)
    d_down = weight_grad(act_low, d_branch)
    d_pre = (back_product(d_branch, down_layer) * gelu_slope(pre_act)).astype(jnp.bfloat16)
    d_up = weight_grad(rows_low, d_pre)
    d_rows = d_resid + back_product(d_pre, up_layer)
    model_width = d_resid.shape[1]
    small_rows = jnp.concatenate(
        [
            jnp.sum(d_pre.astype(jnp.float32), axis=0).reshape(4, model_width),
            jnp.stack([jnp.sum(d_branch.astype(jnp.float32), axis=0), d_gain, d_shift]),
        ],
        axis=0,
    )
    return (d_rows, d_up, d_down, small_rows)


def masked_feed(rows_in, d_rows_out, live_rows, up_layer, down_layer, small_layer):
    capacity, model_width = rows_in.shape
    block_rows = math.gcd(capacity, 128)
    blocks_live = (live_rows + block_rows - 1) // block_rows
    start_state = (
        rows_in,
        jnp.zeros_like(rows_in),
        jnp.zeros(up_layer.shape, jnp.float32),
        jnp.zeros(down_layer.shape, jnp.float32),
        jnp.zeros((7, model_width), jnp.float32),
    )

    def one_block(number, loop_state):
        out_rows, d_in_rows, d_up, d_down, d_small = loop_state
        block_start = number * block_rows
        block_in = lax.dynamic_slice_in_dim(rows_in, block_start, block_rows, 0)
        d_block = lax.dynamic_slice_in_dim(d_rows_out, block_start, block_rows, 0)
        normed, kept_state = feed_forward(block_in, up_layer, down_layer, small_layer)
        d_part, up_part, down_part, small_part = feed_backward(
            d_block, kept_state, up_layer, down_layer, small_layer
        )
        return (
            lax.dynamic_update_slice_in_dim(out_rows, normed, block_start, 0),
            lax.dynamic_update_slice_in_dim(d_in_rows, d_part, block_start, 0),
            d_up + up_part,
            d_down + down_part,
            d_small + small_part,
        )

    return lax.fori_loop(0, blocks_live, one_block, start_state)


def adam_update(
    master, first_moment, second_moment, gradient, clip_scale, step_value, decay_rate, rate_value
):
    clipped = gradient * clip_scale
    first_new = BETA_FIRST * first_moment + (1.0 - BETA_FIRST) * clipped
    second_new = BETA_SECOND * second_moment + (1.0 - BETA_SECOND) * clipped * clipped
    first_hat = first_new / (1.0 - jnp.power(BETA_FIRST, step_value))
    second_hat = second_new / (1.0 - jnp.power(BETA_SECOND, step_value))
    master_new = master - rate_value * (
        first_hat / (jnp.sqrt(second_hat) + ADAM_EPS) + decay_rate * master
    )
    return (master_new, first_new, second_new, master_new.astype(jnp.bfloat16))


def per_device(
    tokens,
    cotangent,
    seq_lengths,
    token_mask,
    step_count,
    attn_master,
    attn_first,
    attn_second,
    up_master,
    up_first,
    up_second,
    down_master,
    down_first,
    down_second,
    small_master,
    small_first,
    small_second,
):
    attn_low, up_low, down_low, small_low = (
        lax.all_gather(attn_master.astype(jnp.bfloat16), "bal", axis=2, tiled=True),
        lax.all_gather(up_master.astype(jnp.bfloat16), "bal", axis=1, tiled=True),
        lax.all_gather(down_master.astype(jnp.bfloat16), "bal", axis=1, tiled=True),
        lax.all_gather(small_master.astype(jnp.bfloat16), "bal", axis=2, tiled=True),
    )
    small_vals = small_low.astype(jnp.float32)
    seq_count, length, model_width = tokens.shape
    rows_total = seq_count * length
    hidden = tokens.astype(jnp.float32)
    attended_one, kept_attend_one = attend_forward(hidden, attn_low[0], small_vals[0], seq_lengths)
    layer_one, kept_feed_one = feed_forward(attended_one, up_low[0], down_low[0], small_vals[0])
    attended_two, kept_attend_two = attend_forward(
        layer_one.reshape(seq_count, length, model_width), attn_low[1], small_vals[1], seq_lengths
    )
    cot_flat = cotangent.reshape(rows_total, model_width).astype(jnp.float32)
    flat_mask = token_mask.reshape(-1)
    live_rows = jnp.sum(flat_mask)
    positions = jnp.nonzero(flat_mask, size=MCAP, fill_value=0)[0].astype(jnp.int32)
    row_rank = jnp.arange(MCAP)
    row_used = row_rank < live_rows
    rows_in = attended_two[positions]
    d_rows_out = jnp.where(row_used[:, None], cot_flat[positions], 0.0)
    out_rows, d_in_rows, d_up_two, d_down_two, feed_small_two = masked_feed(
        rows_in, d_rows_out, live_rows, up_low[1], down_low[1], small_vals[1]
    )
    write_pos = jnp.where(row_used, positions, rows_total)
    output_flat = attended_two.at[write_pos].set(out_rows, mode="drop")
    d_attended_two = cot_flat.at[write_pos].set(d_in_rows, mode="drop")
    d_layer_one, d_attn_two, attn_small_two = attend_backward(
        d_attended_two, kept_attend_two, attn_low[1], small_vals[1], seq_lengths, seq_count, length
    )
    grads_two = (
        d_attn_two,
        d_up_two,
        d_down_two,
        jnp.concatenate([attn_small_two, feed_small_two], axis=0),
    )
    d_attended_one, d_up_one, d_down_one, feed_small_one = feed_backward(
        d_layer_one, kept_feed_one, up_low[0], down_low[0], small_vals[0]
    )
    d_tokens, d_attn_one, attn_small_one = attend_backward(
        d_attended_one, kept_attend_one, attn_low[0], small_vals[0], seq_lengths, seq_count, length
    )
    grads_one = (
        d_attn_one,
        d_up_one,
        d_down_one,
        jnp.concatenate([attn_small_one, feed_small_one], axis=0),
    )
    stacked = tuple((jnp.stack([grads_one[number], grads_two[number]]) for number in range(4)))
    shards = (
        lax.psum_scatter(stacked[0], "bal", scatter_dimension=2, tiled=True),
        lax.psum_scatter(stacked[1], "bal", scatter_dimension=1, tiled=True),
        lax.psum_scatter(stacked[2], "bal", scatter_dimension=1, tiled=True),
        lax.psum_scatter(stacked[3], "bal", scatter_dimension=2, tiled=True),
    )
    reduced = (
        lax.psum(shards[0].astype(jnp.bfloat16), "dp").astype(jnp.float32),
        lax.psum(shards[1].astype(jnp.bfloat16), "dp").astype(jnp.float32),
        lax.psum(shards[2].astype(jnp.bfloat16), "dp").astype(jnp.float32),
        lax.psum(shards[3].astype(jnp.bfloat16), "dp").astype(jnp.float32),
    )
    partial_squares = (
        jnp.sum(reduced[0] * reduced[0])
        + jnp.sum(reduced[1] * reduced[1])
        + jnp.sum(reduced[2] * reduced[2])
        + jnp.sum(reduced[3] * reduced[3])
    )
    square_total = lax.psum(partial_squares, "bal")
    grad_norm = jnp.sqrt(square_total).reshape(1)
    clip_scale = jnp.minimum(1.0, CLIP_NORM / (grad_norm[0] + 1e-06))
    step_value = step_count[0].astype(jnp.float32)
    attn_new = adam_update(
        attn_master,
        attn_first,
        attn_second,
        reduced[0],
        clip_scale,
        step_value,
        WEIGHT_DECAY,
        LEARN_RATE,
    )
    up_new = adam_update(
        up_master, up_first, up_second, reduced[1], clip_scale, step_value, WEIGHT_DECAY, LEARN_RATE
    )
    down_new = adam_update(
        down_master,
        down_first,
        down_second,
        reduced[2],
        clip_scale,
        step_value,
        WEIGHT_DECAY,
        LEARN_RATE,
    )
    small_new = adam_update(
        small_master, small_first, small_second, reduced[3], clip_scale, step_value, 0.0, SMALL_RATE
    )
    output = output_flat.reshape(seq_count, length, model_width).astype(jnp.bfloat16)
    input_grad = d_tokens.reshape(seq_count, length, model_width).astype(jnp.bfloat16)
    return (output, input_grad, grad_norm) + attn_new + up_new + down_new + small_new


def solution(mesh):
    return jax.shard_map(
        per_device,
        mesh=mesh,
        in_specs=(
            P(("dp", "bal"), None, None),
            P(("dp", "bal"), None, None),
            P(("dp", "bal")),
            P(("dp", "bal"), None),
            P(),
            P(None, None, "bal", None),
            P(None, None, "bal", None),
            P(None, None, "bal", None),
            P(None, "bal", None),
            P(None, "bal", None),
            P(None, "bal", None),
            P(None, "bal", None),
            P(None, "bal", None),
            P(None, "bal", None),
            P(None, None, "bal"),
            P(None, None, "bal"),
            P(None, None, "bal"),
        ),
        out_specs=(
            P(("dp", "bal"), None, None),
            P(("dp", "bal"), None, None),
            P(),
            P(None, None, "bal", None),
            P(None, None, "bal", None),
            P(None, None, "bal", None),
            P(None, None, "bal", None),
            P(None, "bal", None),
            P(None, "bal", None),
            P(None, "bal", None),
            P(None, "bal", None),
            P(None, "bal", None),
            P(None, "bal", None),
            P(None, "bal", None),
            P(None, "bal", None),
            P(None, None, "bal"),
            P(None, None, "bal"),
            P(None, None, "bal"),
            P(None, None, "bal"),
        ),
        check_vma=False,
    )
```

profile of v0, /device:TPU:0, one launch (start us, length us, event | category | flops | bytes accessed | tf_op | source)
XLA Modules:
  0.0 1914.2 jit_solution(17521250660093268286)
XLA Ops:
  11.7 46.7 %all_gather.13 = bf16[2,12,768]{1,0,2:T(2,128)(2,1)S(1)} all-gather(bf16[2,12,48]{1,0,2:T(2,128)(2,1)S(1)} %copy.265), channel_id=1, replica_groups=mesh['dp'=2,'bal'=16] {'bal'}, dimensions={2}, use_global_device_ids=true | all-gather | bytes 39168 | tf_op jit(solution)/shard_map/all_gather | solution.py:272
  81.2 39.7 %slice_reduce_fusion.4 = (f32[768]{0:T(1024)}, f32[768]{0:T(1024)}, f32[768]{0:T(1024)}, f32[768]{0:T(1024)}, f32[768]{0:T(1024)}, /*index=5*/f32[768]{0:T(1024)...) fusion(f32[2,12,768]{1,0,2:T(2,128)S(1)} %copy-done.9), kind=kLoop, calls=%fused_computation.254 | loop fusion | bytes 79872 | tf_op jit(solution)/shard_map/slice | solution.py:105
  121.0 17.4 all-gather.4.cloned.1.call-done
  163.1 11.5 fusion.51
  174.6 11.2 fusion.23
  185.9 11.5 fusion.77
  204.0 58.3 %all-gather.6.cloned.1.call-done = bf16[2,768,3072]{2,1,0:T(8,128)(2,1)} async-done(((bf16[2,48,3072]{2,1,0:T(8,128)(2,1)}), bf16[2,768,3072]{2,1,0:T(8,128)(2,1)}) %all-gather.6.cloned.1.call-update) | async-done | bytes 9437200 | tf_op jit(solution)/shard_map/all_gather | solution.py:270
  262.3 36.1 %fusion.29 = (bf16[1024,3072]{1,0:T(8,128)(2,1)}, f32[1024,3072]{1,0:T(8,128)}) fusion(f32[3072]{0:T(1024)S(1)} %add.420, bf16[2,768,3072]{2,1,0:T(8,128)(2,1)} %all-gather.6.cloned.1.call-done, f32[1024,768]{1,0:T(8,128)S(1)} %get-tuple-element.319, f32[768]{0:T(1024)S(1)} %get-tuple-element.249, f32[768]{0:T(1024)S(1)} %get-tuple-element.250, ...), kind=kOutput, calls=%fused_computation.84 | convolution fusion | flops 5043388416 | bytes 26765312 | tf_op jit(solution)/shard_map/dot_general | solution.py:25
  298.4 87.8 %all-gather.8.cloned.1.call-done = bf16[2,3072,768]{2,1,0:T(8,128)(2,1)} async-done(((bf16[2,192,768]{2,1,0:T(8,128)(2,1)}), bf16[2,3072,768]{2,1,0:T(8,128)(2,1)}) %all-gather.8.cloned.1.call-update) | async-done | bytes 9437200 | tf_op jit(solution)/shard_map/all_gather | solution.py:271
  430.2 13.0 fusion.52
  455.1 11.6 fusion.78
  500.2 33.3 %while.18 = (s32[]{:T(128)}, f32[384,768]{1,0:T(8,128)S(1)}, f32[384,768]{1,0:T(8,128)}, f32[768,3072]{1,0:T(8,128)}, f32[3072,768]{1,0:T(8,128)}, /*index=5*/f3...) while((s32[]{:T(128)}, f32[384,768]{1,0:T(8,128)S(1)}, ...), condition=%wide.region_26.27_spmd, body=%wide.region_17.26_spmd.sunk | while | flops 3687792640 | bytes 231457872 | solution.py:232
  552.5 13.3 convert_reduce_fusion.4
  565.8 19.6 %multiply_reduce_fusion.5 = (f32[2,12,512]{2,1,0:T(8,128)S(1)}, f32[2,12,512,512]{2,3,1,0:T(8,128)}) fusion(f32[2,12,512]{2,1,0:T(8,128)S(1)} %copy-done.67, f32[2,12,512,512]{2,3,1,0:T(8,128)} %get-tuple-element.325, pred[2,512]{1,0:T(4,128)(4,1)S(1)} %copy-done.70, bf16[2,512,12,64]{1,0,3,2:T(2,128)(2,1)S(1)} %copy-done.33, ...), kind=kOutput, calls=%fused_computation.65 | convolution fusion | flops 836751360 | bytes 53576704 | tf_op jit(solution)/shard_map/sqhd,skhd->shqk/dot_general | solution.py:132
  585.4 21.8 %multiply_convert_fusion.1 = bf16[2,12,512,512]{2,3,1,0:T(8,128)(2,1)} fusion(f32[2,12,512,512]{2,3,1,0:T(8,128)} %get-tuple-element.329, f32[2,12,512]{2,1,0:T(8,128)S(1)} %get-tuple-element.328, f32[2,12,512]{2,1,0:T(8,128)S(1)} %copy-done.67, f32[2,12,512,512]{2,3,1,0:T(8,128)} %get-tuple-element.325, pred[2,512]{1,0:T(4,128)(4,1)S(1)} %copy-done.70), kind=kLoop, calls=%fused_computation.64 | loop fusion | flops 37748736 | bytes 63013888 | tf_op jit(solution)/shard_map/convert_element_type | solution.py:137
  642.8 13.1 convert_reduce_fusion.2
  709.0 21.2 %multiply_reduce_fusion.4 = (f32[2,12,512]{2,1,0:T(8,128)S(1)}, f32[2,12,512,512]{2,3,1,0:T(8,128)}) fusion(f32[2,12,512]{2,1,0:T(8,128)S(1)} %log_add_fusion, f32[2,12,512,512]{2,3,1,0:T(8,128)} %get-tuple-element.317, pred[2,512]{1,0:T(4,128)(4,1)S(1)} %copy-done.70, bf16[2,512,12,64]{1,0,3,2:T(2,128)(2,1)S(1)} %copy-done.31, ...), kind=kOutput, calls=%fused_computation.62 | convolution fusion | flops 836751360 | bytes 53576704 | tf_op jit(solution)/shard_map/sqhd,skhd->shqk/dot_general | solution.py:132
  730.1 22.5 %multiply_convert_fusion = bf16[2,12,512,512]{2,3,1,0:T(8,128)(2,1)} fusion(f32[2,12,512,512]{2,3,1,0:T(8,128)} %get-tuple-element.333, f32[2,12,512]{2,1,0:T(8,128)S(1)} %get-tuple-element.332, f32[2,12,512]{2,1,0:T(8,128)S(1)} %log_add_fusion, f32[2,12,512,512]{2,3,1,0:T(8,128)} %get-tuple-element.317, pred[2,512]{1,0:T(4,128)(4,1)S(1)} %copy-done.70), kind=kLoop, calls=%fused_computation.61 | loop fusion | flops 37748736 | bytes 63013888 | tf_op jit(solution)/shard_map/convert_element_type | solution.py:137
  775.3 12.5 convert_reduce_fusion.8
  815.4 23.1 %copy.313 = f32[2,4,768,768]{3,1,0,2:T(4,128)} copy(f32[2,4,768,768]{2,3,1,0:T(8,128)} %pad_maximum_fusion) | data formatting | bytes 37748736 | tf_op jit(solution)/shard_map/stack | solution.py:318
  841.0 926.2 %all-reduce.6 = bf16[2,4,768,768]{3,1,0,2:T(4,128)(2,1)} all-reduce(f32[2,4,768,768]{3,1,0,2:T(4,128)} %copy.313), channel_id=2, replica_groups=mesh['dp'=2,'bal'=16] {'bal'}, use_global_device_ids=true, to_apply=%region_37.38.clone | all-reduce | flops 4718592 | bytes 28311552
  1788.8 26.6 %reduce-scatter.10.cloned.1.call-done = f32[48,24]{1,0:T(8,128)} async-done(((f32[768,24]{1,0:T(8,128)}), f32[48,24]{1,0:T(8,128)}) %reduce-scatter.10.cloned.1.call-update) | async-done | bytes 4624
  1819.4 19.8 %all-reduce.5.cloned.1.call-done = (bf16[2,4,48,768]{3,2,1,0:T(8,128)(2,1)}, bf16[2,48,3072]{2,1,0:T(8,128)(2,1)}, bf16[2,192,768]{2,1,0:T(8,128)(2,1)}) async-done(((bf16[2,4,48,768]{3,2,1,0:T(8,128)(2,1)}, bf16[2,48,3072]{2,1,0:T(8,128)(2,1)}, bf16[2,192,768]{2,1,0:T(8,128)(2,1)}), (bf16[2,4,48,768]{3,2,1,0:T(8,128)(2,1)}, bf16[2,48,3072]{2,1,0:T(8,128)(2,1)}, ...) | async-done | bytes 1769488 | tf_op jit(solution)/shard_map/psum | solution.py:326
  1849.1 42.6 %psum.39 = f32[]{:T(128)} all-reduce(f32[]{:T(128)S(6)} %add.463), channel_id=1, replica_groups=mesh['dp'=2,'bal'=16] {'bal'}, use_global_device_ids=true, to_apply=%region_63.64 | all-reduce | flops 1 | bytes 8 | tf_op jit(solution)/shard_map/psum | solution.py:337
  (489 shorter events, 384.0 us)
Async XLA Ops:
  7.2 131.2 %all-gather.4.cloned.1.call-start = ((), (), s32[]{:S(2)}) async-start(), calls=%async_computation.3 | async-start | bytes 10027008 | tf_op jit(solution)/shard_map/all_gather | solution.py:269
  9.6 252.7 %all-gather.6.cloned.1.call-start = ((), (), s32[]{:S(2)}) async-start(), calls=%async_computation.4 | async-start | bytes 10027008 | tf_op jit(solution)/shard_map/all_gather | solution.py:270
  10.6 49.4 %copy-start.101 = (s32[2,512]{1,0:T(2,128)S(1)}, s32[2,512]{1,0:T(2,128)}, u32[]{:S(2)}) copy-start(s32[2,512]{1,0:T(2,128)} %param.22) | copy-start | bytes 12292
  10.6 375.7 %all-gather.8.cloned.1.call-start = ((), (), s32[]{:S(2)}) async-start(), calls=%async_computation.5 | async-start | bytes 10027008 | tf_op jit(solution)/shard_map/all_gather | solution.py:271
  11.5 1757.8 %reduce-scatter.6.cloned.1.call-start = ((), (), s32[]{:S(2)}) async-start(), calls=%async_computation.6 | async-start | bytes 20054016 | tf_op jit(solution)/shard_map/reduce_scatter | solution.py:321
  62.7 199.6 %copy-start.110 = (f32[3072]{0:T(1024)}, f32[3072]{0:T(1024)S(1)}, u32[]{:S(2)}) copy-start(f32[3072]{0:T(1024)S(1)} %add.420) | copy-start | bytes 36868
  81.2 373.8 %copy-start.69 = (pred[2,512]{1,0:T(4,128)(4,1)}, pred[2,512]{1,0:T(4,128)(4,1)S(1)}, u32[]{:S(2)}) copy-start(pred[2,512]{1,0:T(4,128)(4,1)S(1)} %iota_compare_fusion) | copy-start | bytes 3076
  81.2 57.2 %copy-start.119 = (bf16[2,512,768]{2,1,0:T(8,128)(2,1)S(1)}, bf16[2,512,768]{2,1,0:T(8,128)(2,1)}, u32[]{:S(2)}) copy-start(bf16[2,512,768]{2,1,0:T(8,128)(2,1)} %param.19) | copy-start | bytes 4718596
  121.0 265.2 %copy-start.77 = (f32[768]{0:T(1024)}, f32[768]{0:T(1024)S(1)}, u32[]{:S(2)}) copy-start(f32[768]{0:T(1024)S(1)} %get-tuple-element.250) | copy-start | bytes 9220
  121.0 265.2 %copy-start.83 = (f32[768]{0:T(1024)}, f32[768]{0:T(1024)S(1)}, u32[]{:S(2)}) copy-start(f32[768]{0:T(1024)S(1)} %get-tuple-element.249) | copy-start | bytes 9220
  203.5 94.9 %copy-start.11 = (f32[1024,768]{1,0:T(8,128)}, f32[1024,768]{1,0:T(8,128)S(1)}, u32[]{:S(2)}) copy-start(f32[1024,768]{1,0:T(8,128)S(1)} %get-tuple-element.319) | copy-start | bytes 9437188
  203.5 182.7 %copy-start.71 = (f32[1024]{0:T(1024)}, f32[1024]{0:T(1024)S(1)}, u32[]{:S(2)}) copy-start(f32[1024]{0:T(1024)S(1)} %broadcast_multiply_fusion.11) | copy-start | bytes 12292
  204.0 182.2 %copy-start.73 = (f32[1024]{0:T(1024)}, f32[1024]{0:T(1024)S(1)}, u32[]{:S(2)}) copy-start(f32[1024]{0:T(1024)S(1)} %add_rsqrt_fusion.3) | copy-start | bytes 12292
  262.3 123.9 %copy-start.117 = (f32[768]{0:T(1024)S(1)}, f32[768]{0:T(1024)}, u32[]{:S(2)}) copy-start(f32[768]{0:T(1024)} %get-tuple-element.248) | copy-start | bytes 9220
  396.0 72.8 %copy-start.7 = (f32[1024,768]{1,0:T(8,128)}, f32[1024,768]{1,0:T(8,128)S(1)}, u32[]{:S(2)}) copy-start(f32[1024,768]{1,0:T(8,128)S(1)} %get-tuple-element.323) | copy-start | bytes 9437188
  396.0 72.7 %copy-start.81 = (f32[1024]{0:T(1024)}, f32[1024]{0:T(1024)S(1)}, u32[]{:S(2)}) copy-start(f32[1024]{0:T(1024)S(1)} %broadcast_multiply_fusion.10) | copy-start | bytes 12292
  396.5 72.2 %copy-start.89 = (f32[1024]{0:T(1024)}, f32[1024]{0:T(1024)S(1)}, u32[]{:S(2)}) copy-start(f32[1024]{0:T(1024)S(1)} %add_rsqrt_fusion.2) | copy-start | bytes 12292
  668.5 1103.2 %reduce-scatter.8.cloned.1.call-start = ((), (), s32[]{:S(2)}) async-start(), calls=%async_computation.7 | async-start | bytes 20054016 | tf_op jit(solution)/shard_map/reduce_scatter | solution.py:322
  688.3 1127.1 %reduce-scatter.10.cloned.1.call-start = ((), (), s32[]{:S(2)}) async-start(), calls=%async_computation.8 | async-start | bytes 417792
  764.5 33.4 %copy-start.50 = (bf16[96,8,2,512]{3,1,2,0:T(8,128)(2,1)}, bf16[96,8,2,512]{3,1,2,0:T(8,128)(2,1)S(1)}, u32[]{:S(2)}) copy-start(bf16[96,8,2,512]{3,1,2,0:T(8,128)(2,1)S(1)} %copy.345) | copy-start | bytes 4718596
  841.0 998.3 %all-reduce.5.cloned.1.call-start = ((), (), s32[]{:S(2)}) async-start(), calls=%async_computation.9 | async-start | bytes 3538944 | tf_op jit(solution)/shard_map/psum | solution.py:326
  1847.7 44.7 %copy-start.94 = (f32[2,12,48]{2,0,1:T(2,128)S(1)}, f32[2,12,48]{2,0,1:T(2,128)}, u32[]{:S(2)}) copy-start(f32[2,12,48]{2,0,1:T(2,128)} %param.33) | copy-start | bytes 13828
  1847.7 44.7 %copy-start.108 = (f32[2,12,48]{2,0,1:T(2,128)S(1)}, f32[2,12,48]{2,0,1:T(2,128)}, u32[]{:S(2)}) copy-start(f32[2,12,48]{2,0,1:T(2,128)} %param.35) | copy-start | bytes 13828
  1847.8 44.7 %copy-start.109 = (f32[2,12,48]{2,0,1:T(2,128)S(1)}, f32[2,12,48]{2,0,1:T(2,128)}, u32[]{:S(2)}) copy-start(f32[2,12,48]{2,0,1:T(2,128)} %param.34) | copy-start | bytes 13828
  (119 other events, 817.4 us)
Sparse Core Ops, SparseCore 0:
  11.3 127.0 all-gather.3
  141.7 120.5 all-gather.5
  265.6 120.5 all-gather.7
  668.6 499.9 reduce-scatter.5
  1174.2 504.8 reduce-scatter.7
  1684.2 131.1 reduce-scatter.9
  1819.2 19.9 all-reduce.4
where the time goes:
time: 1920 us; the launch traced here: 1910 us
  blocking collectives  1020 us (53%)
  matrix products  320 us (17%)
  waiting for transfers between devices  210 us (11%)
  local copies, waits for them, and re-layouts  192 us (10%)
  other arithmetic  150 us (8%)
  between operations  22.6 us (1%)
    unnamed x1, blocking collectives  926 us
    all_gather x1, waiting for transfers between devices, per_device(): lax.all_gather(down_master.astype(jnp.bfloat16), 'bal', axis=1, tiled=True)  87.8 us
    dot_general x12, matrix products, forward_product(): return jnp.dot(left_side, right_side, preferred_element_type=jnp.float32)  85.9 us
    all_gather x1, waiting for transfers between devices, per_device(): lax.all_gather(up_master.astype(jnp.bfloat16), 'bal', axis=1, tiled=True)  58.3 us
    dot_general x12, matrix products, back_product(): lax.dot_general(left_side, right_side, (((1,), (1,)), ((), ())), preferre...  54.9 us
    all_gather x1, blocking collectives, per_device(): lax.all_gather(small_master.astype(jnp.bfloat16), 'bal', axis=2, tiled=True)  46.7 us
    convert_element_type x2, other arithmetic, attend_backward(): d_scores = (attn_probs * (d_probs - jnp.sum(attn_probs * d_probs, axis=-1...  44.3 us
    psum x1, blocking collectives, per_device(): square_total = lax.psum(partial_squares, 'bal')  42.6 us
  transfers between devices with their start and end apart: 7, of which 5 were waited for; matrix products, arithmetic and copies ran while one was open for 18% of the time, Pallas kernels for 0%

commit v1 on v0

--- a/solution.py
+++ b/solution.py
@@ -3,6 +3,7 @@
 import jax
 import jax.numpy as jnp
 from jax import lax
+from jax.experimental.layout import Layout, with_layout_constraint
 from jax.sharding import PartitionSpec as P
 
 HEADS = 12
@@ -146,13 +147,14 @@
         * scale_factor
     )
     d_keys = d_keys.reshape(row_count, model_width).astype(jnp.bfloat16)
-    weight_set = jnp.stack(
+    weight_set = jnp.concatenate(
         [
             weight_grad(flat_low, d_queries),
             weight_grad(flat_low, d_keys),
             weight_grad(flat_low, d_values),
             d_out_weight,
-        ]
+        ],
+        axis=1,
     )
     d_hidden = (
         d_resid
@@ -200,36 +202,35 @@
     return (d_rows, d_up, d_down, small_rows)
 
 
-def masked_feed(rows_in, d_rows_out, live_rows, up_layer, down_layer, small_layer):
-    capacity, model_width = rows_in.shape
-    block_rows = math.gcd(capacity, 128)
-    blocks_live = (live_rows + block_rows - 1) // block_rows
-    start_state = (
-        rows_in,
-        jnp.zeros_like(rows_in),
-        jnp.zeros(up_layer.shape, jnp.float32),
-        jnp.zeros(down_layer.shape, jnp.float32),
-        jnp.zeros((7, model_width), jnp.float32),
-    )
-
-    def one_block(number, loop_state):
-        out_rows, d_in_rows, d_up, d_down, d_small = loop_state
-        block_start = number * block_rows
-        block_in = lax.dynamic_slice_in_dim(rows_in, block_start, block_rows, 0)
-        d_block = lax.dynamic_slice_in_dim(d_rows_out, block_start, block_rows, 0)
-        normed, kept_state = feed_forward(block_in, up_layer, down_layer, small_layer)
-        d_part, up_part, down_part, small_part = feed_backward(
-            d_block, kept_state, up_layer, down_layer, small_layer
-        )
-        return (
-            lax.dynamic_update_slice_in_dim(out_rows, normed, block_start, 0),
-            lax.dynamic_update_slice_in_dim(d_in_rows, d_part, block_start, 0),
-            d_up + up_part,
-            d_down + down_part,
-            d_small + small_part,
-        )
-
-    return lax.fori_loop(0, blocks_live, one_block, start_state)
+def row_select(token_mask, capacity):
+    flat_mask = token_mask.reshape(1, -1)
+    row_total = flat_mask.shape[1]
+    before = (
+        lax.broadcasted_iota(jnp.int32, (row_total, row_total), 0)
+        < lax.broadcasted_iota(jnp.int32, (row_total, row_total), 1)
+    ).astype(jnp.bfloat16)
+    rank = forward_product(flat_mask.astype(jnp.bfloat16), before).astype(jnp.int32)
+    slots = lax.broadcasted_iota(jnp.int32, (capacity, row_total), 0)
+    return ((slots == rank) & (flat_mask == 1)).astype(jnp.bfloat16)
+
+
+def split_low(wide, parts):
+    pieces = []
+    left = wide
+    for _ in range(parts - 1):
+        piece = lax.reduce_precision(left, 8, 7)
+        pieces.append(piece.astype(jnp.bfloat16))
+        left = left - piece
+    pieces.append(left.astype(jnp.bfloat16))
+    return jnp.concatenate(pieces, axis=1)
+
+
+def join_low(joined, parts):
+    width = joined.shape[1] // parts
+    total = joined[:, :width]
+    for number in range(1, parts):
+        total = total + joined[:, number * width : (number + 1) * width]
+    return total
 
 
 def adam_update(
@@ -244,6 +245,52 @@
         first_hat / (jnp.sqrt(second_hat) + ADAM_EPS) + decay_rate * master
     )
     return (master_new, first_new, second_new, master_new.astype(jnp.bfloat16))
+
+
+def gather_rows(rows, core):
+    half = rows.shape[0] // 2
+    mine = lax.dynamic_slice_in_dim(rows, core * half, half, 0)
+    return lax.all_gather(mine, ("bal", "dp"), axis=0, tiled=True)
+
+
+def scatter_rows(grads):
+    rows = with_layout_constraint(grads.astype(jnp.bfloat16), Layout(major_to_minor=(0, 1)))
+    return lax.psum_scatter(rows, ("bal", "dp"), scatter_dimension=0, tiled=True)
+
+
+def pair_rows(mine, core):
+    other = lax.ppermute(mine, "dp", [(0, 1), (1, 0)])
+    return jnp.where(
+        core == 0,
+        jnp.concatenate([mine, other], axis=0),
+        jnp.concatenate([other, mine], axis=0),
+    )
+
+
+def sum_all(value):
+    total = value.reshape(1, 1)
+    total = total + lax.ppermute(total, "dp", [(0, 1), (1, 0)])
+    peers = lax.axis_size("bal")
+    step = 1
+    while step < peers:
+        moved = []
+        for turn in range(1, 4):
+            pairs = [
+                (at, (at // (4 * step)) * 4 * step + (at + turn * step) % (4 * step))
+                for at in range(peers)
+            ]
+            moved.append(lax.ppermute(total, "bal", pairs))
+        place = (lax.axis_index("bal") // step) % 4
+        ring = jnp.concatenate([total] + moved, axis=1)
+        order = (place - jnp.arange(4)) % 4
+        total = jnp.sum(ring[:, order], axis=1, keepdims=True)
+        step *= 4
+    return total[0, 0]
+
+
+def attn_parts(joined):
+    width = joined.shape[0]
+    return [joined[:, number * width : (number + 1) * width] for number in range(4)]
 
 
 def per_device(
@@ -265,12 +312,22 @@
     small_first,
     small_second,
 ):
-    attn_low, up_low, down_low, small_low = (
-        lax.all_gather(attn_master.astype(jnp.bfloat16), "bal", axis=2, tiled=True),
-        lax.all_gather(up_master.astype(jnp.bfloat16), "bal", axis=1, tiled=True),
-        lax.all_gather(down_master.astype(jnp.bfloat16), "bal", axis=1, tiled=True),
-        lax.all_gather(small_master.astype(jnp.bfloat16), "bal", axis=2, tiled=True),
-    )
+    core = lax.axis_index("dp")
+    attn_rows = attn_master.astype(jnp.bfloat16).transpose(0, 2, 1, 3)
+    attn_rows = attn_rows.reshape(2, attn_rows.shape[1], -1)
+    small_cols = small_master.astype(jnp.bfloat16).reshape(24, -1).T
+    small_cols = jnp.pad(small_cols, ((0, 0), (0, 104)))
+    up_rows = up_master.astype(jnp.bfloat16)
+    down_rows = down_master.astype(jnp.bfloat16)
+    first_piece = gather_rows(jnp.concatenate([attn_rows[0], small_cols], axis=1), core)
+    wide = attn_rows.shape[2]
+    up_low, down_low = [None, None], [None, None]
+    up_low[0] = gather_rows(up_rows[0], core)
+    down_low[0] = gather_rows(down_rows[0], core)
+    attn_low = [attn_parts(first_piece[:, :wide]), attn_parts(gather_rows(attn_rows[1], core))]
+    up_low[1] = gather_rows(up_rows[1], core)
+    down_low[1] = gather_rows(down_rows[1], core)
+    small_low = first_piece[:, wide : wide + 24].T.reshape(2, 12, -1)
     small_vals = small_low.astype(jnp.float32)
     seq_count, length, model_width = tokens.shape
     rows_total = seq_count * length
@@ -281,19 +338,22 @@
         layer_one.reshape(seq_count, length, model_width), attn_low[1], small_vals[1], seq_lengths
     )
     cot_flat = cotangent.reshape(rows_total, model_width).astype(jnp.float32)
-    flat_mask = token_mask.reshape(-1)
-    live_rows = jnp.sum(flat_mask)
-    positions = jnp.nonzero(flat_mask, size=MCAP, fill_value=0)[0].astype(jnp.int32)
-    row_rank = jnp.arange(MCAP)
-    row_used = row_rank < live_rows
-    rows_in = attended_two[positions]
-    d_rows_out = jnp.where(row_used[:, None], cot_flat[positions], 0.0)
-    out_rows, d_in_rows, d_up_two, d_down_two, feed_small_two = masked_feed(
-        rows_in, d_rows_out, live_rows, up_low[1], down_low[1], small_vals[1]
-    )
-    write_pos = jnp.where(row_used, positions, rows_total)
-    output_flat = attended_two.at[write_pos].set(out_rows, mode="drop")
-    d_attended_two = cot_flat.at[write_pos].set(d_in_rows, mode="drop")
+    select_rows = row_select(token_mask, MCAP)
+    rows_in = join_low(forward_product(select_rows, split_low(attended_two, 3)), 3)
+    d_rows_out = forward_product(select_rows, cotangent.reshape(rows_total, model_width))
+    out_rows, kept_feed_two = feed_forward(rows_in, up_low[1], down_low[1], small_vals[1])
+    d_in_rows, d_up_two, d_down_two, feed_small_two = feed_backward(
+        d_rows_out, kept_feed_two, up_low[1], down_low[1], small_vals[1]
+    )
+    flat_mask = token_mask.reshape(-1, 1) == 1
+    output_flat = jnp.where(
+        flat_mask,
+        weight_grad(select_rows, out_rows.astype(jnp.bfloat16)),
+        attended_two,
+    )
+    d_attended_two = jnp.where(
+        flat_mask, join_low(weight_grad(select_rows, split_low(d_in_rows, 2)), 2), cot_flat
+    )
     d_layer_one, d_attn_two, attn_small_two = attend_backward(
         d_attended_two, kept_attend_two, attn_low[1], small_vals[1], seq_lengths, seq_count, length
     )
@@ -315,26 +375,25 @@
         d_down_one,
         jnp.concatenate([attn_small_one, feed_small_one], axis=0),
     )
-    stacked = tuple((jnp.stack([grads_one[number], grads_two[number]]) for number in range(4)))
-    shards = (
-        lax.psum_scatter(stacked[0], "bal", scatter_dimension=2, tiled=True),
-        lax.psum_scatter(stacked[1], "bal", scatter_dimension=1, tiled=True),
-        lax.psum_scatter(stacked[2], "bal", scatter_dimension=1, tiled=True),
-        lax.psum_scatter(stacked[3], "bal", scatter_dimension=2, tiled=True),
-    )
+    small_grads = jnp.stack([grads_one[3], grads_two[3]]).reshape(24, -1).T
+    small_grads = jnp.pad(small_grads, ((0, 0), (0, 104)))
+    owned = {}
+    owned["up1"] = scatter_rows(d_up_two)
+    owned["down1"] = scatter_rows(d_down_two)
+    owned["attn1"] = scatter_rows(d_attn_two)
+    owned["down0"] = scatter_rows(d_down_one)
+    owned["up0"] = scatter_rows(d_up_one)
+    owned["attn0"] = scatter_rows(jnp.concatenate([d_attn_one, small_grads], axis=1))
+    partial_squares = sum(jnp.sum(jnp.square(owned[name].astype(jnp.float32))) for name in owned)
+    square_total = sum_all(partial_squares)
+    both = {name: pair_rows(owned[name], core).astype(jnp.float32) for name in owned}
+    attn_both = jnp.stack([both["attn0"][:, :wide], both["attn1"]])
     reduced = (
-        lax.psum(shards[0].astype(jnp.bfloat16), "dp").astype(jnp.float32),
-        lax.psum(shards[1].astype(jnp.bfloat16), "dp").astype(jnp.float32),
-        lax.psum(shards[2].astype(jnp.bfloat16), "dp").astype(jnp.float32),
-        lax.psum(shards[3].astype(jnp.bfloat16), "dp").astype(jnp.float32),
-    )
-    partial_squares = (
-        jnp.sum(reduced[0] * reduced[0])
-        + jnp.sum(reduced[1] * reduced[1])
-        + jnp.sum(reduced[2] * reduced[2])
-        + jnp.sum(reduced[3] * reduced[3])
-    )
-    square_total = lax.psum(partial_squares, "bal")
+        attn_both.reshape(2, -1, 4, model_width).transpose(0, 2, 1, 3),
+        jnp.stack([both["up0"], both["up1"]]),
+        jnp.stack([both["down0"], both["down1"]]),
+        both["attn0"][:, wide : wide + 24].T.reshape(2, 12, -1),
+    )
     grad_norm = jnp.sqrt(square_total).reshape(1)
     clip_scale = jnp.minimum(1.0, CLIP_NORM / (grad_norm[0] + 1e-06))
     step_value = step_count[0].astype(jnp.float32)

time: 1920 us -> 1160 us (0.60)
  blocking collectives: 1020 us -> 0 us
  waiting for transfers between devices: 210 us -> 558 us
  local copies, waits for them, and re-layouts: 192 us -> 86.4 us
  other arithmetic: 150 us -> 114 us
  matrix products: 320 us -> 348 us
    unnamed x1 -> x0, blocking collectives: 926 us -> none
    reduce_scatter x2 -> x5, waiting for transfers between devices: 0.01 us -> 265 us  [scatter_rows(): lax.psum_scatter(rows, ('bal', 'dp'), scatter_dimension=0, tiled=True)]
    unnamed x8 -> x13, waiting for transfers between devices: 26.7 us -> 99.3 us
    all_gather x1 -> x0, blocking collectives: 46.7 us -> none  [per_device(): lax.all_gather(small_master.astype(jnp.bfloat16), 'bal', axis=2, tiled=True)]
    psum x2 -> x0, blocking collectives: 45.1 us -> none  [the longest x1 42.6 us: per_device(): square_total = lax.psum(partial_squares, 'bal')]
    slice x3 -> x6, local copies, waits for them, and re-layouts: 40.2 us -> 0.47 us  [the longest x2 0.19 us: per_device(): attn_rows[1]]
    another operation x11 -> x1, other arithmetic: 27.4 us -> 0.01 us  [per_device(): small_grads = jnp.stack([grads_one[3], grads_two[3]]).reshape(24, -1).T]
    another operation x4 -> x2, local copies, waits for them, and re-layouts: 23.4 us -> 0.41 us  [per_device(): attn_both = jnp.stack([both['attn0'][:, :wide], both['attn1']])]
  transfers between devices with their start and end apart: 7 -> 25, of which waited for: 5 -> 13; matrix products, arithmetic and copies ran while one was open for 18% -> 44% of each run, Pallas kernels for 0% -> 0%
where the time goes in v1:
time: 1160 us; the launch traced here: 1150 us
  waiting for transfers between devices  558 us (48%)
  matrix products  348 us (30%)
  other arithmetic  114 us (10%)
  local copies, waits for them, and re-layouts  86.4 us (7%)
  between operations  24 us (2%)
  starting transfers between devices  14.3 us (1%)
    reduce_scatter x5, waiting for transfers between devices, scatter_rows(): lax.psum_scatter(rows, ('bal', 'dp'), scatter_dimension=0, tiled=True)  265 us
    all_gather x6, waiting for transfers between devices, gather_rows(): return lax.all_gather(mine, ('bal', 'dp'), axis=0, tiled=True)  186 us
    dot_general x15, matrix products, forward_product(): return jnp.dot(left_side, right_side, preferred_element_type=jnp.float32)  102 us
    unnamed x13, waiting for transfers between devices  99.3 us
    dot_general x12, matrix products, back_product(): lax.dot_general(left_side, right_side, (((1,), (1,)), ((), ())), preferre...  62.5 us
    dot_general x14, matrix products, weight_grad(): lax.dot_general(left_side, right_side, (((0,), (0,)), ((), ())), preferre...  49.1 us
    dot_general x2, matrix products, attend_backward(): jnp.einsum('sqhd,skhd->shqk', d_mixed, value_heads, preferred_element_typ...  40.4 us
    convert_element_type x2, other arithmetic, attend_backward(): d_scores = (attn_probs * (d_probs - jnp.sum(attn_probs * d_probs, axis=-1...  36.5 us
  transfers between devices with their start and end apart: 25, of which 13 were waited for; matrix products, arithmetic and copies ran while one was open for 44% of the time, Pallas kernels for 0%

profile of v1, /device:TPU:0, one launch (start us, length us, event | category | flops | bytes accessed | tf_op | source)
XLA Modules:
  0.0 1145.1 jit_solution(2698200014164596145)
XLA Ops:
  16.4 62.3 %all-gather.11.cloned.1.call-done = bf16[768,3200]{1,0:T(8,128)(2,1)} async-done(((bf16[24,3200]{1,0:T(8,128)(2,1)}), bf16[768,3200]{1,0:T(8,128)(2,1)}) %all-gather.11.cloned.1.call-update) | async-done | bytes 4915216 | tf_op jit(solution)/shard_map/all_gather | solution.py:253
  99.0 11.2 fusion.28
  110.3 11.2 fusion
  121.6 12.4 %fusion.104 = bf16[2,512,12,64]{1,3,2,0:T(8,128)(2,1)S(1)} fusion(f32[2,12,512]{2,1,0:T(8,128)S(1)} %fusion, f32[2,12,512]{2,1,0:T(8,128)S(1)} %get-tuple-element.127, f32[2,12,512,512]{2,3,1,0:T(8,128)} %get-tuple-element.128, pred[2,512]{1,0:T(4,128)(4,1)S(1)} %iota_compare_fusion.4, bf16[2,512,12,64]{1,0,3,2:T(2,128)(2,1)S(1)} %copy-done.21), kind=kOutput, calls=%fused_computation.184 | convolution fusion | flops 837550080 | bytes 28410880 | tf_op jit(solution)/shard_map/shqk,skhd->sqhd/dot_general | solution.py:98
  144.6 36.9 %fusion.6 = (bf16[1024,3072]{1,0:T(8,128)(2,1)}, f32[1024,3072]{1,0:T(8,128)}) fusion(f32[3072]{0:T(1024)S(1)} %add.425, bf16[1,768,3072]{2,1,0:T(8,128)(2,1)} %all-gather.15.cloned.1.call-done, f32[1024,768]{1,0:T(8,128)S(1)} %get-tuple-element.130, f32[768]{0:T(1024)S(1)} %get-tuple-element.84, f32[768]{0:T(1024)S(1)} %get-tuple-element.85, ...), kind=kOutput, calls=%fused_computation.22 | convolution fusion | flops 5043388416 | bytes 26765312 | tf_op jit(solution)/shard_map/dot_general | solution.py:26
  181.5 29.1 %all-gather.17.cloned.1.call-done = bf16[1,3072,768]{2,1,0:T(8,128)(2,1)} async-done(((bf16[1,96,768]{2,1,0:T(8,128)(2,1)}), bf16[1,3072,768]{2,1,0:T(8,128)(2,1)}) %all-gather.17.cloned.1.call-update) | async-done | bytes 4718608 | tf_op jit(solution)/shard_map/all_gather | solution.py:253
  222.5 53.9 %all-gather.13.cloned.1.call-done = bf16[768,3072]{1,0:T(8,128)(2,1)} async-done(((bf16[24,3072]{1,0:T(8,128)(2,1)}), bf16[768,3072]{1,0:T(8,128)(2,1)}) %all-gather.13.cloned.1.call-update) | async-done | bytes 4718608 | tf_op jit(solution)/shard_map/all_gather | solution.py:253
  308.8 13.0 %fusion.29 = (f32[2,12,512]{2,1,0:T(8,128)S(1)}, f32[2,12,512,512]{2,3,1,0:T(8,128)}) fusion(pred[2,512]{1,0:T(4,128)(4,1)S(1)} %iota_compare_fusion.4, bf16[2,512,12,64]{1,0,3,2:T(2,128)(2,1)} %reshape.753, bf16[2,512,12,64]{1,0,3,2:T(2,128)(2,1)} %reshape.752), kind=kOutput, calls=%fused_computation.51 | convolution fusion | flops 824168448 | bytes 28361728 | tf_op jit(solution)/shard_map/sqhd,skhd->shqk/dot_general | solution.py:75
  321.7 11.8 %fusion.1 = f32[2,12,512]{2,1,0:T(8,128)S(1)} fusion(f32[2,12,512]{2,1,0:T(8,128)S(1)} %get-tuple-element.135, f32[2,12,512,512]{2,3,1,0:T(8,128)} %get-tuple-element.136, pred[2,512]{1,0:T(4,128)(4,1)S(1)} %iota_compare_fusion.4), kind=kLoop, calls=%fused_computation.15 | loop fusion | flops 25153536 | bytes 25265152 | tf_op jit(solution)/shard_map/reduce_sum | solution.py:95
  333.6 12.0 %fusion.105 = bf16[2,512,12,64]{1,3,2,0:T(8,128)(2,1)S(1)} fusion(f32[2,12,512]{2,1,0:T(8,128)S(1)} %fusion.1, f32[2,12,512]{2,1,0:T(8,128)S(1)} %get-tuple-element.135, f32[2,12,512,512]{2,3,1,0:T(8,128)} %get-tuple-element.136, pred[2,512]{1,0:T(4,128)(4,1)S(1)} %iota_compare_fusion.4, bf16[2,512,12,64]{1,0,3,2:T(2,128)(2,1)S(1)} %copy-done.23), kind=kOutput, calls=%fused_computation.185 | convolution fusion | flops 837550080 | bytes 28410880 | tf_op jit(solution)/shard_map/shqk,skhd->sqhd/dot_general | solution.py:98
  356.3 15.0 %fusion.32 = (bf16[384,3072]{1,0:T(8,128)(2,1)}, f32[384,3072]{1,0:T(8,128)}) fusion(f32[3072]{0:T(1024)S(1)} %copy-done.93, bf16[1,768,3072]{2,1,0:T(8,128)(2,1)} %all-gather.19.cloned.1.call-done, f32[384,768]{1,0:T(8,128)S(1)} %slice_add_fusion.1), kind=kOutput, calls=%fused_computation.60 | convolution fusion | flops 1890091008 | bytes 12988416 | tf_op jit(solution)/shard_map/dot_general | solution.py:26
  371.3 36.7 %all-gather.21.cloned.1.call-done = bf16[1,3072,768]{2,1,0:T(8,128)(2,1)} async-done(((bf16[1,96,768]{2,1,0:T(8,128)(2,1)}), bf16[1,3072,768]{2,1,0:T(8,128)(2,1)}) %all-gather.21.cloned.1.call-update) | async-done | bytes 4718608 | tf_op jit(solution)/shard_map/all_gather | solution.py:253
  457.3 20.5 %multiply_reduce_fusion.1 = (f32[2,12,512]{2,1,0:T(8,128)S(1)}, f32[2,12,512,512]{2,3,1,0:T(8,128)}) fusion(f32[2,12,512]{2,1,0:T(8,128)S(1)} %log_add_fusion.1, f32[2,12,512,512]{2,3,1,0:T(8,128)} %get-tuple-element.136, pred[2,512]{1,0:T(4,128)(4,1)S(1)} %iota_compare_fusion.4, bf16[2,512,12,64]{1,0,3,2:T(2,128)(2,1)} %reshape.751, ...), kind=kOutput, calls=%fused_computation.6 | convolution fusion | flops 836751360 | bytes 53576704 | tf_op jit(solution)/shard_map/sqhd,skhd->shqk/dot_general | solution.py:133
  477.7 11.7 %fusion.235 = (bf16[12,64]{1,0:T(8,128)(2,1)S(1)}, bf16[2,12,64,512]{3,2,1,0:T(8,128)(2,1)S(1)}) fusion(f32[2,12,512]{2,1,0:T(8,128)S(1)} %log_add_fusion.1, f32[2,12,512,512]{2,3,1,0:T(8,128)} %get-tuple-element.136, pred[2,512]{1,0:T(4,128)(4,1)S(1)} %iota_compare_fusion.4, bf16[2,512,12,64]{1,0,3,2:T(2,128)(2,1)} %reshape.755), kind=kOutput, calls=%fused_computation.404 | convolution fusion | flops 832044288 | bytes 28363264 | tf_op jit(solution)/shard_map/shqk,sqhd->skhd/dot_general | solution.py:126
  491.5 18.8 %multiply_convert_fusion.1 = bf16[2,12,512,512]{2,3,1,0:T(8,128)(2,1)S(1)} fusion(f32[2,12,512,512]{2,3,1,0:T(8,128)} %get-tuple-element.145, f32[2,12,512]{2,1,0:T(8,128)S(1)} %get-tuple-element.144, f32[2,12,512]{2,1,0:T(8,128)S(1)} %log_add_fusion.1, f32[2,12,512,512]{2,3,1,0:T(8,128)} %get-tuple-element.136, pred[2,512]{1,0:T(4,128)(4,1)S(1)} %iota_compare_fusion.4), kind=kLoop, calls=%fused_computation.5 | loop fusion | flops 37748736 | bytes 63013888 | tf_op jit(solution)/shard_map/convert_element_type | solution.py:138
  558.9 13.4 %fusion.239 = (bf16[3072]{0:T(1024)(128)(2,1)S(1)}, bf16[1024,3072]{1,0:T(8,128)(2,1)S(1)}) fusion(f32[1024,3072]{1,0:T(8,128)} %get-tuple-element.132, f32[3072]{0:T(1024)S(1)} %copy-done.92, bf16[1,3072,768]{2,1,0:T(8,128)(2,1)} %all-gather.17.cloned.1.call-done, f32[1024,768]{1,0:T(8,128)} %copy-done.32), kind=kOutput, calls=%fused_computation.408 | convolution fusion | flops 4870370304 | bytes 26757120 | tf_op jit(solution)/shard_map/dot_general | solution.py:36
  572.4 10.7 multiply_reduce_fusion.4
  608.1 20.0 %multiply_reduce_fusion = (f32[2,12,512]{2,1,0:T(8,128)S(1)}, f32[2,12,512,512]{2,3,1,0:T(8,128)}) fusion(f32[2,12,512]{2,1,0:T(8,128)S(1)} %log_add_fusion, f32[2,12,512,512]{2,3,1,0:T(8,128)} %get-tuple-element.128, pred[2,512]{1,0:T(4,128)(4,1)S(1)} %iota_compare_fusion.4, bf16[2,512,12,64]{1,0,3,2:T(2,128)(2,1)S(1)} %copy-done.22, ...), kind=kOutput, calls=%fused_computation.3 | convolution fusion | flops 836751360 | bytes 53576704 | tf_op jit(solution)/shard_map/sqhd,skhd->shqk/dot_general | solution.py:133
  628.1 11.5 %fusion.238 = (bf16[12,64]{1,0:T(8,128)(2,1)S(1)}, bf16[2,512,12,64]{1,3,2,0:T(8,128)(2,1)S(1)}) fusion(f32[2,12,512]{2,1,0:T(8,128)S(1)} %log_add_fusion, f32[2,12,512,512]{2,3,1,0:T(8,128)} %get-tuple-element.128, pred[2,512]{1,0:T(4,128)(4,1)S(1)} %iota_compare_fusion.4, bf16[2,512,12,64]{1,0,3,2:T(2,128)(2,1)S(1)} %copy-done.24), kind=kOutput, calls=%fused_computation.407 | convolution fusion | flops 832044288 | bytes 28363264 | tf_op jit(solution)/shard_map/shqk,sqhd->skhd/dot_general | solution.py:126
  643.4 17.7 %multiply_convert_fusion = bf16[2,12,512,512]{2,3,1,0:T(8,128)(2,1)S(1)} fusion(f32[2,12,512,512]{2,3,1,0:T(8,128)} %get-tuple-element.149, f32[2,12,512]{2,1,0:T(8,128)S(1)} %get-tuple-element.148, f32[2,12,512]{2,1,0:T(8,128)S(1)} %log_add_fusion, f32[2,12,512,512]{2,3,1,0:T(8,128)} %get-tuple-element.128, pred[2,512]{1,0:T(4,128)(4,1)S(1)} %iota_compare_fusion.4), kind=kLoop, calls=%fused_computation.2 | loop fusion | flops 37748736 | bytes 63013888 | tf_op jit(solution)/shard_map/convert_element_type | solution.py:138
  709.1 48.7 %reduce-scatter.13.cloned.1.call-done = bf16[24,3072]{1,0:T(8,128)(2,1)} async-done(((bf16[768,3072]{1,0:T(8,128)(2,1)}), bf16[24,3072]{1,0:T(8,128)(2,1)}) %reduce-scatter.13.cloned.1.call-update) | async-done | bytes 147472 | tf_op jit(solution)/shard_map/reduce_scatter | solution.py:258
  759.4 110.7 %reduce-scatter.15.cloned.1.call-done = bf16[96,768]{1,0:T(8,128)(2,1)} async-done(((bf16[3072,768]{1,0:T(8,128)(2,1)}), bf16[96,768]{1,0:T(8,128)(2,1)}) %reduce-scatter.15.cloned.1.call-update) | async-done | bytes 147472 | tf_op jit(solution)/shard_map/reduce_scatter | solution.py:258
  876.0 105.7 %reduce-scatter.17.cloned.1.call-done = bf16[24,3072]{1,0:T(8,128)(2,1)} async-done(((bf16[768,3072]{1,0:T(8,128)(2,1)}), bf16[24,3072]{1,0:T(8,128)(2,1)}) %reduce-scatter.17.cloned.1.call-update) | async-done | bytes 147472 | tf_op jit(solution)/shard_map/reduce_scatter | solution.py:258
  992.0 99.1 %reduce-scatter.19.cloned.1.call-done = bf16[24,3200]{1,0:T(8,128)(2,1)} async-done(((bf16[768,3200]{1,0:T(8,128)(2,1)}), bf16[24,3200]{1,0:T(8,128)(2,1)}) %reduce-scatter.19.cloned.1.call-update) | async-done | bytes 153616
  (495 shorter events, 327.0 us)
Async XLA Ops:
  7.2 71.4 %all-gather.11.cloned.1.call-start = ((), (), s32[]{:S(2)}) async-start(), calls=%async_computation.6 | async-start | bytes 5068800 | tf_op jit(solution)/shard_map/all_gather | solution.py:253
  10.5 134.1 %all-gather.15.cloned.1.call-start = ((), (), s32[]{:S(2)}) async-start(), calls=%async_computation.13 | async-start | bytes 4866048 | tf_op jit(solution)/shard_map/all_gather | solution.py:253
  11.4 199.2 %all-gather.17.cloned.1.call-start = ((), (), s32[]{:S(2)}) async-start(), calls=%async_computation.14 | async-start | bytes 4866048 | tf_op jit(solution)/shard_map/all_gather | solution.py:253
  12.3 264.2 %all-gather.13.cloned.1.call-start = ((), (), s32[]{:S(2)}) async-start(), calls=%async_computation.7 | async-start | bytes 4866048 | tf_op jit(solution)/shard_map/all_gather | solution.py:253
  13.2 342.7 %all-gather.19.cloned.1.call-start = ((), (), s32[]{:S(2)}) async-start(), calls=%async_computation.15 | async-start | bytes 4866048 | tf_op jit(solution)/shard_map/all_gather | solution.py:253
  14.0 394.1 %all-gather.21.cloned.1.call-start = ((), (), s32[]{:S(2)}) async-start(), calls=%async_computation.16 | async-start | bytes 4866048 | tf_op jit(solution)/shard_map/all_gather | solution.py:253
  14.7 690.8 %reduce-scatter.9.cloned.1.call-start = ((), (), s32[]{:S(2)}) async-start(), calls=%async_computation.8 | async-start | bytes 4866048 | tf_op jit(solution)/shard_map/reduce_scatter | solution.py:258
  427.8 279.5 %reduce-scatter.11.cloned.1.call-start = ((), (), s32[]{:S(2)}) async-start(), calls=%async_computation.9 | async-start | bytes 4866048 | tf_op jit(solution)/shard_map/reduce_scatter | solution.py:258
  457.0 300.9 %reduce-scatter.13.cloned.1.call-start = ((), (), s32[]{:S(2)}) async-start(), calls=%async_computation.10 | async-start | bytes 4866048 | tf_op jit(solution)/shard_map/reduce_scatter | solution.py:258
  537.4 332.8 %reduce-scatter.15.cloned.1.call-start = ((), (), s32[]{:S(2)}) async-start(), calls=%async_computation.11 | async-start | bytes 4866048 | tf_op jit(solution)/shard_map/reduce_scatter | solution.py:258
  558.2 423.5 %reduce-scatter.17.cloned.1.call-start = ((), (), s32[]{:S(2)}) async-start(), calls=%async_computation.12 | async-start | bytes 4866048 | tf_op jit(solution)/shard_map/reduce_scatter | solution.py:258
  606.3 484.9 %reduce-scatter.19.cloned.1.call-start = ((), (), s32[]{:S(2)}) async-start(), calls=%async_computation.17 | async-start | bytes 5068800
  705.6 279.5 %collective-permute-start.10 = (bf16[24,3072]{1,0:T(8,128)(2,1)}, bf16[24,3072]{1,0:T(8,128)(2,1)S(1)}, u32[]{:S(2)}, u32[]{:S(2)}) collective-permute-start(bf16[24,3072]{1,0:T(8,128)(2,1)} %reduce-scatter.9.cloned.1.call-done), channel_id=1, source_target_pairs={{0,16},{16,0},{1,17},{17,1},{2,18},{18,2},{3,19},{19,3},{4,20},{20... | collective-permute-start | bytes 442376 | tf_op jit(solution)/shard_map/ppermute | solution.py:262
  984.0 2.1 collective-permute-start.12
  984.0 4.9 collective-permute-start.8
  984.5 5.6 collective-permute-start.9
  984.6 2.6 collective-permute-start.11
  1094.3 34.0 %collective-permute-start.7 = (bf16[24,3200]{1,0:T(8,128)(2,1)}, bf16[24,3200]{1,0:T(8,128)(2,1)}, u32[]{:S(2)}, u32[]{:S(2)}) collective-permute-start(bf16[24,3200]{1,0:T(8,128)(2,1)} %reduce-scatter.19.cloned.1.call-done), channel_id=1, source_target_pairs={{0,16},{16,0},{1,17},{17,1},{2,18},{18,2},{3,19},{19,3},{4,20},{20... | collective-permute-start | bytes 460808 | tf_op jit(solution)/shard_map/ppermute | solution.py:262
  1095.5 7.4 collective-permute-start.3
  1098.8 4.1 collective-permute-start.2
  1101.0 4.5 collective-permute-start.1
  1108.8 3.8 collective-permute-start.6
  1111.1 4.7 collective-permute-start.5
  1111.4 5.6 collective-permute-start.4
  (122 other events, 2686.8 us)
Sparse Core Ops, SparseCore 0:
  11.5 67.0 all-gather.10
  82.1 62.4 all-gather.14
  148.1 62.4 all-gather.16
  213.9 62.4 all-gather.12
  279.8 62.4 all-gather.18
  345.6 62.4 all-gather.20
  427.9 105.7 reduce-scatter.8
  540.1 106.0 reduce-scatter.10
  651.7 106.0 reduce-scatter.12
  764.1 106.0 reduce-scatter.14
  875.7 106.0 reduce-scatter.16
  988.2 102.8 reduce-scatter.18

commit v2 on v1

v2 whole, which is shorter than its diff:
```python
import math

import jax
import jax.numpy as jnp
import numpy as np
from jax import lax
from jax.experimental import pallas as pl
from jax.experimental.pallas import tpu as pltpu
from jax.sharding import PartitionSpec as P

HEADS = 12
HEAD_DIM = 64
MCAP = 384
LANES = 128
QUERY_BLOCK = 256


LN_EPS = 1e-06
NEG_FILL = -1000000000.0
CLIP_NORM = 1.0
LEARN_RATE = 0.05
SMALL_RATE = 0.25
BETA_FIRST = 0.9
BETA_SECOND = 0.999
ADAM_EPS = 1e-08
WEIGHT_DECAY = 0.01


def forward_product(left_side, right_side):
    return jnp.dot(left_side, right_side, preferred_element_type=jnp.float32)


def weight_grad(left_side, right_side):
    return lax.dot_general(
        left_side, right_side, (((0,), (0,)), ((), ())), preferred_element_type=jnp.float32
    )


def back_product(left_side, right_side):
    return lax.dot_general(
        left_side, right_side, (((1,), (1,)), ((), ())), preferred_element_type=jnp.float32
    )


def norm_forward(residual, norm_gain, norm_shift):
    centered = residual - jnp.mean(residual, axis=-1, keepdims=True)
    variance = jnp.mean(centered * centered, axis=-1, keepdims=True)
    inv_std = lax.rsqrt(variance + LN_EPS)
    normal_part = centered * inv_std
    return (normal_part * norm_gain + norm_shift, normal_part, inv_std)


def norm_backward(d_out, normal_part, inv_std, norm_gain):
    d_normal = d_out * norm_gain
    d_resid = inv_std * (
        d_normal
        - jnp.mean(d_normal, axis=-1, keepdims=True)
        - normal_part * jnp.mean(d_normal * normal_part, axis=-1, keepdims=True)
    )
    return (d_resid, jnp.sum(d_out * normal_part, axis=0), jnp.sum(d_out, axis=0))


def gelu_slope(pre_act):
    return (
        0.5 * (1.0 + lax.erf(pre_act * 0.7071067811865476))
        + pre_act * jnp.exp(-0.5 * pre_act * pre_act) * 0.3989422804014327
    )


def key_side(keys, bias, lane, half):
    own = (lane < HEAD_DIM) if half == 0 else (lane >= HEAD_DIM)
    spare = HEAD_DIM if half == 0 else 0
    return jnp.where(own, keys, jnp.where(lane == spare, bias, 0.0)).astype(jnp.bfloat16)


def query_side(queries, lane, half):
    own = (lane < HEAD_DIM) if half == 0 else (lane >= HEAD_DIM)
    spare = HEAD_DIM if half == 0 else 0
    return jnp.where(own, queries, jnp.where(lane == spare, 1.0, 0.0)).astype(jnp.bfloat16)


def one_head(rows, lane, half):
    own = (lane < HEAD_DIM) if half == 0 else (lane >= HEAD_DIM)
    return jnp.where(own, rows, 0.0).astype(jnp.bfloat16)


def pair_of(ref, part, pair):
    width = ref.shape[1] // 3
    at = pl.multiple_of(part * width + pair * LANES, LANES)
    return ref[:, pl.ds(at, LANES)].astype(jnp.float32)


def attend_kernel(len_ref, qkv_lo, qkv_hi, mixed_ref, lse_ref, ot_ref):
    rows = mixed_ref.shape[0]
    width = qkv_lo.shape[1] // 3
    pairs = width // LANES
    real = len_ref[pl.program_id(0)]
    lane = lax.broadcasted_iota(jnp.int32, (rows, LANES), 1)
    place_key = lax.broadcasted_iota(jnp.int32, (rows, LANES), 0)
    bias = jnp.where(place_key < real, 0.0, NEG_FILL)
    for side, qkv_ref in enumerate((qkv_lo, qkv_hi)):

        def one_pair(pair, carry, side=side, qkv_ref=qkv_ref):
            queries = pair_of(qkv_ref, 0, pair) * (1.0 / math.sqrt(HEAD_DIM))
            keys = pair_of(qkv_ref, 1, pair)
            values_t = pair_of(qkv_ref, 2, pair).T.astype(jnp.bfloat16)
            for half in range(2):
                keys_one = key_side(keys, bias, lane, half)
                queries_one = query_side(queries, lane, half)
                lanes = slice(half * HEAD_DIM, (half + 1) * HEAD_DIM)
                head = side * 2 * pairs + 2 * pair + half
                for at in range(0, rows, QUERY_BLOCK):
                    cols = slice(at, at + QUERY_BLOCK)
                    scores = back_product(keys_one, queries_one[cols])
                    top = jnp.max(scores, axis=0, keepdims=True)
                    exps = jnp.exp(scores - top)
                    total = jnp.sum(exps, axis=0, keepdims=True)
                    mixed_t = forward_product(values_t[lanes], exps.astype(jnp.bfloat16))
                    ot_ref[lanes, cols] = mixed_t / total
                    lse_ref[pl.ds(head, 1), cols] = top + jnp.log(total)
            at = pl.multiple_of(side * width + pair * LANES, LANES)
            mixed_ref[:, pl.ds(at, LANES)] = ot_ref[...].T.astype(jnp.bfloat16)
            return carry

        lax.fori_loop(0, pairs, one_pair, 0)


def attend_core(qkv_lo, qkv_hi, seq_lengths):
    total, wide = qkv_lo.shape
    seqs = seq_lengths.shape[0]
    rows, width = total // seqs, 2 * wide // 3
    heads = width // HEAD_DIM
    lse_rows = -(-heads // 8) * 8
    side = pl.BlockSpec((rows, wide), lambda seq, lens: (seq, 0))
    return pl.pallas_call(
        attend_kernel,
        out_shape=(
            jax.ShapeDtypeStruct((total, width), jnp.bfloat16),
            jax.ShapeDtypeStruct((seqs, lse_rows, rows), jnp.float32),
        ),
        grid_spec=pltpu.PrefetchScalarGridSpec(
            num_scalar_prefetch=1,
            grid=(seqs,),
            in_specs=[side, side],
            out_specs=[
                pl.BlockSpec((rows, width), lambda seq, lens: (seq, 0)),
                pl.BlockSpec((None, lse_rows, rows), lambda seq, lens: (seq, 0, 0)),
            ],
            scratch_shapes=[pltpu.VMEM((LANES, rows), jnp.float32)],
        ),
        compiler_params=pltpu.CompilerParams(vmem_limit_bytes=32 << 20),
        cost_estimate=pl.CostEstimate(
            flops=16 * total * rows * width,
            bytes_accessed=8 * total * width,
            transcendentals=total * rows * heads,
        ),
        name="attend",
    )(seq_lengths, qkv_lo, qkv_hi)


def attend_back_kernel(
    len_ref, qkv_lo, qkv_hi, d_mixed_ref, lse_ref, d_qkv_ref, dqt_ref, dk_ref, dv_ref
):
    rows = d_mixed_ref.shape[0]
    width = qkv_lo.shape[1] // 3
    pairs = width // LANES
    scale = 1.0 / math.sqrt(HEAD_DIM)
    real = len_ref[pl.program_id(0)]
    lane = lax.broadcasted_iota(jnp.int32, (rows, LANES), 1)
    place_key = lax.broadcasted_iota(jnp.int32, (rows, LANES), 0)
    bias = jnp.where(place_key < real, 0.0, NEG_FILL)
    for side, qkv_ref in enumerate((qkv_lo, qkv_hi)):

        def one_pair(pair, carry, side=side, qkv_ref=qkv_ref):
            queries = pair_of(qkv_ref, 0, pair) * scale
            keys = pair_of(qkv_ref, 1, pair)
            values = pair_of(qkv_ref, 2, pair)
            at_mixed = pl.multiple_of(side * width + pair * LANES, LANES)
            d_mixed = d_mixed_ref[:, pl.ds(at_mixed, LANES)].astype(jnp.float32)
            keys_t = keys.T.astype(jnp.bfloat16)
            started = False
            for half in range(2):
                keys_one = key_side(keys, bias, lane, half)
                queries_one = query_side(queries, lane, half)
                values_only = one_head(values, lane, half)
                queries_only = one_head(queries, lane, half)
                d_mixed_only = one_head(d_mixed, lane, half)
                lanes = slice(half * HEAD_DIM, (half + 1) * HEAD_DIM)
                head = side * 2 * pairs + 2 * pair + half
                for at in range(0, rows, QUERY_BLOCK):
                    cols = slice(at, at + QUERY_BLOCK)
                    scores = back_product(keys_one, queries_one[cols])
                    d_probs = back_product(values_only, d_mixed_only[cols])
                    probs = jnp.exp(scores - lse_ref[pl.ds(head, 1), cols])
                    row_part = jnp.sum(probs * d_probs, axis=0, keepdims=True)
                    d_scores = (probs * (d_probs - row_part)).astype(jnp.bfloat16)
                    d_values = forward_product(probs.astype(jnp.bfloat16), d_mixed_only[cols])
                    d_keys = forward_product(d_scores, queries_only[cols])
                    if started:
                        dv_ref[...] += d_values
                        dk_ref[...] += d_keys
                    else:
                        dv_ref[...] = d_values
                        dk_ref[...] = d_keys
                        started = True
                    dqt_ref[lanes, cols] = forward_product(keys_t[lanes], d_scores)
            outs = ((dqt_ref[...].T * scale), dk_ref[...], dv_ref[...])
            for part, value in enumerate(outs):
                at = pl.multiple_of(part * width + pair * LANES, LANES)
                d_qkv_ref[side, :, pl.ds(at, LANES)] = value.astype(jnp.bfloat16)
            return carry

        lax.fori_loop(0, pairs, one_pair, 0)


def attend_core_back(qkv_lo, qkv_hi, d_mixed, lse, seq_lengths):
    total, wide = qkv_lo.shape
    seqs = seq_lengths.shape[0]
    rows, width = total // seqs, 2 * wide // 3
    heads = width // HEAD_DIM
    side = pl.BlockSpec((rows, wide), lambda seq, lens: (seq, 0))
    return pl.pallas_call(
        attend_back_kernel,
        out_shape=jax.ShapeDtypeStruct((2, total, wide), jnp.bfloat16),
        grid_spec=pltpu.PrefetchScalarGridSpec(
            num_scalar_prefetch=1,
            grid=(seqs,),
            in_specs=[
                side,
                side,
                pl.BlockSpec((rows, width), lambda seq, lens: (seq, 0)),
                pl.BlockSpec((None, lse.shape[1], rows), lambda seq, lens: (seq, 0, 0)),
            ],
            out_specs=pl.BlockSpec((2, rows, wide), lambda seq, lens: (0, seq, 0)),
            scratch_shapes=[
                pltpu.VMEM((LANES, rows), jnp.float32),
                pltpu.VMEM((rows, LANES), jnp.float32),
                pltpu.VMEM((rows, LANES), jnp.float32),
            ],
        ),
        compiler_params=pltpu.CompilerParams(vmem_limit_bytes=40 << 20),
        cost_estimate=pl.CostEstimate(
            flops=40 * total * rows * width,
            bytes_accessed=14 * total * width,
            transcendentals=total * rows * heads,
        ),
        name="attend_back",
    )(seq_lengths, qkv_lo, qkv_hi, d_mixed, lse)


def half_of(rows, side):
    width = rows.shape[1] // 2
    return lax.dynamic_slice_in_dim(rows, side * width, width, 1)


def attend_forward(flat_rows, flat_low, attn_layer, small_layer, seq_lengths):
    model_width = flat_rows.shape[1]
    third = model_width // 2
    qkv = []
    for side in range(2):
        cols = slice(side * third, (side + 1) * third)
        bias = jnp.concatenate(
            [small_layer[0, cols], jnp.zeros((third,), jnp.float32), small_layer[1, cols]]
        )
        part = forward_product(flat_low, attn_layer[side, :, : 3 * third]) + bias
        qkv.append(part.astype(jnp.bfloat16))
    mixed_heads, lse = attend_core(qkv[0], qkv[1], seq_lengths)
    branch = jnp.concatenate(
        [
            forward_product(mixed_heads, attn_layer[side, :, 3 * third : 4 * third])
            for side in range(2)
        ],
        axis=1,
    )
    normed, normal_part, inv_std = norm_forward(
        flat_rows + branch + small_layer[2], small_layer[3], small_layer[4]
    )
    return (normed, (flat_low, qkv, lse, mixed_heads, normal_part, inv_std))


def attend_backward(d_normed, kept_state, attn_layer, small_layer, seq_lengths, core):
    flat_low, qkv, lse, mixed_heads, normal_part, inv_std = kept_state
    row_count, model_width = flat_low.shape
    third = model_width // 2
    d_resid, d_gain, d_shift = norm_backward(d_normed, normal_part, inv_std, small_layer[3])
    d_branch = d_resid.astype(jnp.bfloat16)
    d_out_bias = jnp.sum(d_branch.astype(jnp.float32), axis=0)
    d_mixed = sum(
        back_product(
            d_branch[:, side * third : (side + 1) * third],
            attn_layer[side, :, 3 * third : 4 * third],
        )
        for side in range(2)
    ).astype(jnp.bfloat16)
    d_qkv = attend_core_back(qkv[0], qkv[1], d_mixed, lse, seq_lengths)

    def weights_of(side):
        return jnp.concatenate(
            [
                weight_grad(flat_low, lax.dynamic_index_in_dim(d_qkv, side, 0, False)),
                weight_grad(mixed_heads, half_of(d_branch, side)),
            ],
            axis=1,
        )

    far = weights_of(1 - core)
    own = weights_of(core)
    d_hidden = d_resid + sum(
        back_product(d_qkv[side], attn_layer[side, :, : 3 * third]) for side in range(2)
    )
    sums = jnp.sum(d_qkv.astype(jnp.float32), axis=1)
    small_rows = jnp.stack(
        [
            sums[:, :third].reshape(model_width),
            sums[:, 2 * third :].reshape(model_width),
            d_out_bias,
            d_gain,
            d_shift,
        ]
    )
    return (d_hidden, own, far, small_rows)


def feed_forward(rows_in, up_layer, down_layer, small_layer):
    rows_low = rows_in.astype(jnp.bfloat16)
    pre_act = forward_product(rows_low, up_layer) + small_layer[5:9].reshape(-1)
    act_low = jax.nn.gelu(pre_act, approximate=False).astype(jnp.bfloat16)
    branch = forward_product(act_low, down_layer) + small_layer[9]
    normed, normal_part, inv_std = norm_forward(rows_in + branch, small_layer[10], small_layer[11])
    return (normed, (rows_low, pre_act, act_low, normal_part, inv_std))


def feed_backward(d_normed, kept_state, up_layer, down_layer, small_layer, core):
    rows_low, pre_act, act_low, normal_part, inv_std = kept_state
    d_resid, d_gain, d_shift = norm_backward(d_normed, normal_part, inv_std, small_layer[10])
    d_branch = d_resid.astype(jnp.bfloat16)
    d_down = [weight_grad(act_low, half_of(d_branch, side)) for side in (1 - core, core)]
    d_pre = (back_product(d_branch, down_layer) * gelu_slope(pre_act)).astype(jnp.bfloat16)
    d_up = [weight_grad(rows_low, half_of(d_pre, side)) for side in (1 - core, core)]
    d_rows = d_resid + back_product(d_pre, up_layer)
    model_width = d_resid.shape[1]
    small_rows = jnp.concatenate(
        [
            jnp.sum(d_pre.astype(jnp.float32), axis=0).reshape(4, model_width),
            jnp.stack([jnp.sum(d_branch.astype(jnp.float32), axis=0), d_gain, d_shift]),
        ],
        axis=0,
    )
    return (d_rows, d_up, d_down, small_rows)


def row_select(token_mask, capacity):
    flat_mask = token_mask.reshape(1, -1)
    row_total = flat_mask.shape[1]
    before = (
        lax.broadcasted_iota(jnp.int32, (row_total, row_total), 0)
        < lax.broadcasted_iota(jnp.int32, (row_total, row_total), 1)
    ).astype(jnp.bfloat16)
    rank = forward_product(flat_mask.astype(jnp.bfloat16), before).astype(jnp.int32)
    slots = lax.broadcasted_iota(jnp.int32, (capacity, row_total), 0)
    return ((slots == rank) & (flat_mask == 1)).astype(jnp.bfloat16)


def split_low(wide, parts):
    pieces = []
    left = wide
    for _ in range(parts - 1):
        piece = lax.reduce_precision(left, 8, 7)
        pieces.append(piece.astype(jnp.bfloat16))
        left = left - piece
    pieces.append(left.astype(jnp.bfloat16))
    return jnp.concatenate(pieces, axis=1)


def join_low(joined, parts):
    width = joined.shape[1] // parts
    total = joined[:, :width]
    for number in range(1, parts):
        total = total + joined[:, number * width : (number + 1) * width]
    return total


def adam_update(
    master, first_moment, second_moment, gradient, clip_scale, step_value, decay_rate, rate_value
):
    clipped = gradient * clip_scale
    first_new = BETA_FIRST * first_moment + (1.0 - BETA_FIRST) * clipped
    second_new = BETA_SECOND * second_moment + (1.0 - BETA_SECOND) * clipped * clipped
    first_hat = first_new / (1.0 - jnp.power(BETA_FIRST, step_value))
    second_hat = second_new / (1.0 - jnp.power(BETA_SECOND, step_value))
    master_new = master - rate_value * (
        first_hat / (jnp.sqrt(second_hat) + ADAM_EPS) + decay_rate * master
    )
    return (master_new, first_new, second_new, master_new.astype(jnp.bfloat16))


def routes(peers):
    bits = peers.bit_length() - 1
    deep = min(2, bits)
    rest = bits - deep
    x_bits = [1 << at for at in range(rest - rest // 2)]
    y_bits = [1 << at for at in range(rest - rest // 2, rest)]
    z_bits = [1 << at for at in range(rest, bits)]
    first = z_bits + y_bits + x_bits
    second = z_bits + x_bits + y_bits
    return (first, second if len(x_bits) == len(y_bits) else first)


def shift(value, step, peers):
    pairs = []
    for core, path in enumerate(routes(peers)):
        pairs += [(core * peers + at, core * peers + (at ^ path[step])) for at in range(peers)]
    return lax.ppermute(value, ("dp", "bal"), pairs)


def swap(value):
    return lax.ppermute(value, "dp", [(0, 1), (1, 0)])


def place_table(peers, core):
    masks = [
        [sum(bit for at, bit in enumerate(path) if spot >> at & 1) for spot in range(peers)]
        for path in routes(peers)
    ]
    masks = jnp.asarray(np.array(masks, np.int32))
    mine = lax.axis_index("bal")
    own = jnp.where(core == 0, masks[0], masks[1])
    far = jnp.where(core == 0, masks[1], masks[0])
    return jnp.concatenate([mine ^ own, mine ^ far, core.reshape(1).astype(jnp.int32)])


def place_kernel(spots, own_lo, own_hi, far_lo, far_hi, out, held, in_sems, out_sems):
    half, rows, width = own_lo.shape
    core = spots[4 * half]
    loads = []
    for number, part in enumerate((own_lo, own_hi, far_lo, far_hi)):
        loads.append(pltpu.make_async_copy(part, held.at[number], in_sems.at[number]))
        loads[-1].start()
    stores = []
    for number, load in enumerate(loads):
        load.wait()
        side = core if number < 2 else 1 - core
        for at in range(half):
            spot = spots[number * half + at]
            if len(out.shape) == 4:
                target = out.at[side, spot]
            else:
                target = out.at[spot, :, pl.ds(pl.multiple_of(side * width, LANES), width)]
            stores.append(
                pltpu.make_async_copy(held.at[number, at], target, out_sems.at[number, at])
            )
            stores[-1].start()
    for store in stores:
        store.wait()


def place(spots, parts, stacked):
    half, rows, width = parts[0].shape
    peers = 2 * half
    shape = (2, peers, rows, width) if stacked else (peers, rows, 2 * width)
    return pl.pallas_call(
        place_kernel,
        out_shape=jax.ShapeDtypeStruct(shape, parts[0].dtype),
        grid_spec=pltpu.PrefetchScalarGridSpec(
            num_scalar_prefetch=1,
            grid=(),
            in_specs=[pl.BlockSpec(memory_space=pl.ANY)] * 4,
            out_specs=pl.BlockSpec(memory_space=pl.ANY),
            scratch_shapes=[
                pltpu.VMEM((4, half, rows, width), parts[0].dtype),
                pltpu.SemaphoreType.DMA((4,)),
                pltpu.SemaphoreType.DMA((4, half)),
            ],
        ),
        compiler_params=pltpu.CompilerParams(vmem_limit_bytes=16 << 20),
        cost_estimate=pl.CostEstimate(
            flops=0, bytes_accessed=8 * peers * rows * width, transcendentals=0
        ),
        name="place",
    )(spots, *parts)


def gather(mine, spots, peers, stacked):
    buffer = mine[None]
    steps = peers.bit_length() - 1
    for step in range(steps - 1):
        buffer = jnp.concatenate([buffer, shift(buffer, step, peers)], axis=0)
    moved = shift(buffer, steps - 1, peers)
    whole = place(spots, (buffer, moved, swap(buffer), swap(moved)), stacked)
    if stacked:
        return whole.reshape(2, -1, whole.shape[-1])
    return whole.reshape(-1, whole.shape[-1])


def fold_kernel(spots, own_a, far_a, own_b, far_b, keep, send):
    keep[...] = (own_a[...].astype(jnp.float32) + far_a[...].astype(jnp.float32)).astype(keep.dtype)
    send[...] = (own_b[...].astype(jnp.float32) + far_b[...].astype(jnp.float32)).astype(send.dtype)


def fold(spots, own, far):
    peers, rows, width = own.shape
    half = peers // 2
    near = pl.BlockSpec((1, rows, width), lambda at, spots: (spots[at], 0, 0))
    apart = pl.BlockSpec((1, rows, width), lambda at, spots: (spots[at + half], 0, 0))
    there = pl.BlockSpec((1, rows, width), lambda at, spots: (at, 0, 0))
    shape = jax.ShapeDtypeStruct((half, rows, width), own.dtype)
    return pl.pallas_call(
        fold_kernel,
        out_shape=(shape, shape),
        grid_spec=pltpu.PrefetchScalarGridSpec(
            num_scalar_prefetch=1,
            grid=(half,),
            in_specs=[near, near, apart, apart],
            out_specs=[there, there],
        ),
        cost_estimate=pl.CostEstimate(
            flops=peers * rows * width,
            bytes_accessed=6 * peers * rows * width,
            transcendentals=0,
        ),
        name="fold",
    )(spots, own, far, own, far)


def scatter(far, own, spots, peers):
    def blocks(grads):
        return grads.astype(jnp.bfloat16).reshape(peers, -1, grads.shape[1])

    keep, send = fold(spots, blocks(own), swap(blocks(far)))
    for step in range(peers.bit_length() - 2, -1, -1):
        total = keep.astype(jnp.float32) + shift(send, step, peers).astype(jnp.float32)
        half = total.shape[0] // 2
        if step == 0:
            return total[0].astype(jnp.bfloat16)
        keep = total[:half].astype(jnp.bfloat16)
        send = total[half:].astype(jnp.bfloat16)


def both_sides(own, core):
    other = swap(own)
    return (jnp.where(core == 0, own, other), jnp.where(core == 0, other, own))


def sum_all(value, peers):
    total = value.reshape(1, 1)
    total = total + swap(total)
    step = 1
    while step < peers:
        span = min(4, peers // step)
        moved = [
            lax.ppermute(total, "bal", [(at, at ^ (turn * step)) for at in range(peers)])
            for turn in range(1, span)
        ]
        if span == 4:
            total = (total + moved[0]) + (moved[1] + moved[2])
        else:
            total = total + moved[0]
        step *= span
    return total[0, 0]


def per_device(
    tokens,
    cotangent,
    seq_lengths,
    token_mask,
    step_count,
    attn_master,
    attn_first,
    attn_second,
    up_master,
    up_first,
    up_second,
    down_master,
    down_first,
    down_second,
    small_master,
    small_first,
    small_second,
):
    core = lax.axis_index("dp")
    peers = lax.axis_size("bal")
    seq_count, length, model_width = tokens.shape
    rows_total = seq_count * length
    spots = place_table(peers, core)
    shard = attn_master.shape[2]
    attn_half = lax.dynamic_slice_in_dim(attn_master, core * (model_width // 2), model_width // 2, 3)
    attn_half = attn_half.astype(jnp.bfloat16).transpose(0, 2, 1, 3).reshape(2, shard, -1)
    small_half = lax.dynamic_slice_in_dim(small_master.reshape(24, shard), core * 12, 12, 0)
    small_half = jnp.pad(small_half.astype(jnp.bfloat16).T, ((0, 0), (0, LANES - 12)))
    wide = attn_half.shape[2]
    first_piece = gather(
        jnp.concatenate([attn_half[0], small_half], axis=1), spots, peers, True
    )
    up_low, down_low = [None, None], [None, None]
    up_low[0] = gather(half_of(up_master[0], core).astype(jnp.bfloat16), spots, peers, False)
    down_low[0] = gather(half_of(down_master[0], core).astype(jnp.bfloat16), spots, peers, False)
    attn_low = [first_piece[:, :, :wide], gather(attn_half[1], spots, peers, True)]
    up_low[1] = gather(half_of(up_master[1], core).astype(jnp.bfloat16), spots, peers, False)
    down_low[1] = gather(half_of(down_master[1], core).astype(jnp.bfloat16), spots, peers, False)
    small_vals = first_piece[:, :, wide : wide + 12].transpose(0, 2, 1).astype(jnp.float32)
    flat_low = tokens.reshape(rows_total, model_width)
    attended_one, kept_attend_one = attend_forward(
        flat_low.astype(jnp.float32), flat_low, attn_low[0], small_vals[0], seq_lengths
    )
    layer_one, kept_feed_one = feed_forward(attended_one, up_low[0], down_low[0], small_vals[0])
    attended_two, kept_attend_two = attend_forward(
        layer_one, layer_one.astype(jnp.bfloat16), attn_low[1], small_vals[1], seq_lengths
    )
    cot_flat = cotangent.reshape(rows_total, model_width).astype(jnp.float32)
    select_rows = row_select(token_mask, MCAP)
    rows_in = join_low(forward_product(select_rows, split_low(attended_two, 3)), 3)
    d_rows_out = forward_product(select_rows, cotangent.reshape(rows_total, model_width))
    out_rows, kept_feed_two = feed_forward(rows_in, up_low[1], down_low[1], small_vals[1])
    d_in_rows, d_up_two, d_down_two, feed_small_two = feed_backward(
        d_rows_out, kept_feed_two, up_low[1], down_low[1], small_vals[1], core
    )
    flat_mask = token_mask.reshape(-1, 1) == 1
    output_flat = jnp.where(
        flat_mask,
        weight_grad(select_rows, out_rows.astype(jnp.bfloat16)),
        attended_two,
    )
    d_attended_two = jnp.where(
        flat_mask, join_low(weight_grad(select_rows, split_low(d_in_rows, 2)), 2), cot_flat
    )
    owned = {}
    owned["up1"] = scatter(*d_up_two, spots, peers)
    owned["down1"] = scatter(*d_down_two, spots, peers)
    d_layer_one, own_attn, far_attn, attn_small_two = attend_backward(
        d_attended_two, kept_attend_two, attn_low[1], small_vals[1], seq_lengths, core
    )
    owned["attn1"] = scatter(far_attn, own_attn, spots, peers)
    d_attended_one, d_up_one, d_down_one, feed_small_one = feed_backward(
        d_layer_one, kept_feed_one, up_low[0], down_low[0], small_vals[0], core
    )
    owned["down0"] = scatter(*d_down_one, spots, peers)
    owned["up0"] = scatter(*d_up_one, spots, peers)
    d_tokens, own_attn, far_attn, attn_small_one = attend_backward(
        d_attended_one, kept_attend_one, attn_low[0], small_vals[0], seq_lengths, core
    )
    small_grads = jnp.stack(
        [
            jnp.concatenate([attn_small_one, feed_small_one], axis=0),
            jnp.concatenate([attn_small_two, feed_small_two], axis=0),
        ]
    )

    def with_small(grads, side):
        picked = lax.dynamic_index_in_dim(small_grads, side, 0, False).T
        picked = jnp.pad(picked, ((0, 0), (0, LANES - 12)))
        return jnp.concatenate([grads, picked], axis=1)

    owned["attn0"] = scatter(
        with_small(far_attn, 1 - core), with_small(own_attn, core), spots, peers
    )
    partial_squares = sum(jnp.sum(jnp.square(owned[name].astype(jnp.float32))) for name in owned)
    square_total = sum_all(partial_squares, peers)
    both = {name: both_sides(owned[name], core) for name in owned}

    def attn_rows(name):
        sides = jnp.stack([part[:, :wide] for part in both[name]])
        return sides.reshape(2, shard, 4, -1).transpose(2, 1, 0, 3).reshape(4, shard, model_width)

    def wide_rows(name):
        return jnp.concatenate(both[name], axis=1)

    reduced = (
        jnp.stack([attn_rows("attn0"), attn_rows("attn1")]).astype(jnp.float32),
        jnp.stack([wide_rows("up0"), wide_rows("up1")]).astype(jnp.float32),
        jnp.stack([wide_rows("down0"), wide_rows("down1")]).astype(jnp.float32),
        jnp.stack([part[:, wide : wide + 12].T for part in both["attn0"]]).astype(jnp.float32),
    )
    grad_norm = jnp.sqrt(square_total).reshape(1)
    clip_scale = jnp.minimum(1.0, CLIP_NORM / (grad_norm[0] + 1e-06))
    step_value = step_count[0].astype(jnp.float32)
    attn_new = adam_update(
        attn_master,
        attn_first,
        attn_second,
        reduced[0],
        clip_scale,
        step_value,
        WEIGHT_DECAY,
        LEARN_RATE,
    )
    up_new = adam_update(
        up_master, up_first, up_second, reduced[1], clip_scale, step_value, WEIGHT_DECAY, LEARN_RATE
    )
    down_new = adam_update(
        down_master,
        down_first,
        down_second,
        reduced[2],
        clip_scale,
        step_value,
        WEIGHT_DECAY,
        LEARN_RATE,
    )
    small_new = adam_update(
        small_master, small_first, small_second, reduced[3], clip_scale, step_value, 0.0, SMALL_RATE
    )
    output = output_flat.reshape(seq_count, length, model_width).astype(jnp.bfloat16)
    input_grad = d_tokens.reshape(seq_count, length, model_width).astype(jnp.bfloat16)
    return (output, input_grad, grad_norm) + attn_new + up_new + down_new + small_new


def solution(mesh):
    return jax.shard_map(
        per_device,
        mesh=mesh,
        in_specs=(
            P(("dp", "bal"), None, None),
            P(("dp", "bal"), None, None),
            P(("dp", "bal")),
            P(("dp", "bal"), None),
            P(),
            P(None, None, "bal", None),
            P(None, None, "bal", None),
            P(None, None, "bal", None),
            P(None, "bal", None),
            P(None, "bal", None),
            P(None, "bal", None),
            P(None, "bal", None),
            P(None, "bal", None),
            P(None, "bal", None),
            P(None, None, "bal"),
            P(None, None, "bal"),
            P(None, None, "bal"),
        ),
        out_specs=(
            P(("dp", "bal"), None, None),
            P(("dp", "bal"), None, None),
            P(),
            P(None, None, "bal", None),
            P(None, None, "bal", None),
            P(None, None, "bal", None),
            P(None, None, "bal", None),
            P(None, "bal", None),
            P(None, "bal", None),
            P(None, "bal", None),
            P(None, "bal", None),
            P(None, "bal", None),
            P(None, "bal", None),
            P(None, "bal", None),
            P(None, "bal", None),
            P(None, None, "bal"),
            P(None, None, "bal"),
            P(None, None, "bal"),
            P(None, None, "bal"),
        ),
        check_vma=False,
    )
```

time: 1160 us -> 844 us (0.73)
  waiting for transfers between devices: 558 us -> 259 us
  Pallas kernels: 0 us -> 174 us
  matrix products: 348 us -> 190 us
  starting transfers between devices: 14.3 us -> 75 us
  other arithmetic: 114 us -> 68 us
  local copies, waits for them, and re-layouts: 86.4 us -> 57.5 us
    reduce_scatter x5 -> x0, waiting for transfers between devices: 265 us -> none  [scatter_rows(): lax.psum_scatter(rows, ('bal', 'dp'), scatter_dimension=0, tiled=True)]
    ppermute x13 -> x79, waiting for transfers between devices: 7.49 us -> 259 us  [the longest x48 255 us: shift(): return lax.ppermute(value, ('dp', 'bal'), pairs)]
    all_gather x6 -> x0, waiting for transfers between devices: 186 us -> none  [gather_rows(): return lax.all_gather(mine, ('bal', 'dp'), axis=0, tiled=True)]
    pallas_call x0 -> x16, Pallas kernels: none -> 174 us  [the longest x2 55 us: attend_core_back(): pl.pallas_call(attend_back_kernel, out_shape=jax.ShapeDtypeStruct((2, tot...]
    dot_general x12 -> x0, matrix products: 134 us -> none  [the longest x2 40.4 us: attend_backward(): jnp.einsum('sqhd,skhd->shqk', d_mixed, value_heads, preferred_element_typ...]
    unnamed x13 -> x0, waiting for transfers between devices: 99.3 us -> none
    ppermute x13 -> x79, starting transfers between devices: 13.5 us -> 75 us  [the longest x48 52.5 us: shift(): return lax.ppermute(value, ('dp', 'bal'), pairs)]
    convert_element_type x9 -> x3, other arithmetic: 42.2 us -> 1.47 us  [the longest x1 0.91 us: feed_forward(): rows_low = rows_in.astype(jnp.bfloat16)]
  transfers between devices with their start and end apart: 25 -> 79, of which waited for: 13 -> 31; matrix products, arithmetic and copies ran while one was open for 44% -> 9% of each run, Pallas kernels for 0% -> 8%
where the time goes in v2:
time: 844 us; the launch traced here: 837 us
  waiting for transfers between devices  259 us (31%)
  matrix products  190 us (23%)
  Pallas kernels  174 us (21%)
  starting transfers between devices  75 us (9%)
  other arithmetic  68 us (8%)
  local copies, waits for them, and re-layouts  57.5 us (7%)
  between operations  14.1 us (2%)
    ppermute x48, waiting for transfers between devices, shift(): return lax.ppermute(value, ('dp', 'bal'), pairs)  255 us
    dot_general x15, matrix products, forward_product(): return jnp.dot(left_side, right_side, preferred_element_type=jnp.float32)  74 us
    dot_general x18, matrix products, weight_grad(): lax.dot_general(left_side, right_side, (((0,), (0,)), ((), ())), preferre...  69.6 us
    pallas_call x2, Pallas kernels, attend_core_back(): pl.pallas_call(attend_back_kernel, out_shape=jax.ShapeDtypeStruct((2, tot...  55 us
    ppermute x48, starting transfers between devices, shift(): return lax.ppermute(value, ('dp', 'bal'), pairs)  52.5 us
    pallas_call x2, Pallas kernels, attend_core(): pl.pallas_call(attend_kernel, out_shape=(jax.ShapeDtypeStruct((total, wid...  47.5 us
    dot_general x12, matrix products, back_product(): lax.dot_general(left_side, right_side, (((1,), (1,)), ((), ())), preferre...  46.5 us
    pallas_call x6, Pallas kernels, fold(): pl.pallas_call(fold_kernel, out_shape=(shape, shape), grid_spec=pltpu.Pre...  42.7 us
  transfers between devices with their start and end apart: 79, of which 31 were waited for; matrix products, arithmetic and copies ran while one was open for 9% of the time, Pallas kernels for 8%

profile of v2, /device:TPU:0, one launch (start us, length us, event | category | flops | bytes accessed | tf_op | source)
XLA Modules:
  0.0 837.5 jit_solution(534983255268970312)
XLA Ops:
  19.9 9.3 %collective-permute-done.18 = bf16[1,48,1536]{2,1,0:T(8,128)(2,1)S(1)} collective-permute-done((bf16[1,48,1536]{2,1,0:T(8,128)(2,1)S(1)}, bf16[1,48,1536]{2,1,0:T(8,128)(2,1)S(1)}, u32[]{:S(2)}, u32[]{:S(2)}) %collective-permute-start.18) | collective-permute-done | bytes 147488 | tf_op jit(solution)/shard_map/ppermute | solution.py:413
  38.6 30.9 %collective-permute-done.13 = bf16[2,192,384]{2,1,0:T(8,128)(2,1)S(1)} collective-permute-done((bf16[2,192,384]{2,1,0:T(8,128)(2,1)S(1)}, bf16[2,192,384]{2,1,0:T(8,128)(2,1)S(1)}, u32[]{:S(2)}, u32[]{:S(2)}) %collective-permute-start.13) | collective-permute-done | bytes 294944 | tf_op jit(solution)/shard_map/ppermute | solution.py:413
  71.2 8.1 collective-permute-done.19
  101.2 11.1 %collective-permute-done.26 = bf16[4,48,1536]{2,1,0:T(8,128)(2,1)S(1)} collective-permute-done((bf16[4,48,1536]{2,1,0:T(8,128)(2,1)S(1)}, bf16[4,48,1536]{2,1,0:T(8,128)(2,1)S(1)}, u32[]{:S(2)}, u32[]{:S(2)}) %collective-permute-start.26) | collective-permute-done | bytes 589856 | tf_op jit(solution)/shard_map/ppermute | solution.py:413
  114.0 11.0 %collective-permute-done.32 = bf16[4,192,384]{2,1,0:T(8,128)(2,1)S(1)} collective-permute-done((bf16[4,192,384]{2,1,0:T(8,128)(2,1)S(1)}, bf16[4,192,384]{2,1,0:T(8,128)(2,1)S(1)}, u32[]{:S(2)}, u32[]{:S(2)}) %collective-permute-start.32) | collective-permute-done | bytes 589856 | tf_op jit(solution)/shard_map/ppermute | solution.py:413
  125.0 13.7 %collective-permute-done.2 = bf16[4,48,1664]{2,1,0:T(8,128)(2,1)S(1)} collective-permute-done((bf16[4,48,1664]{2,1,0:T(8,128)(2,1)S(1)}, bf16[4,48,1664]{2,1,0:T(8,128)(2,1)S(1)}, u32[]{:S(2)}, u32[]{:S(2)}) %collective-permute-start.2) | collective-permute-done | bytes 639008 | tf_op jit(solution)/shard_map/ppermute | solution.py:413
  146.2 9.3 %collective-permute-done.21.own_hi = bf16[8,48,1536]{2,1,0:T(8,128)(2,1)S(1)} collective-permute-done((bf16[8,48,1536]{2,1,0:T(8,128)(2,1)S(1)}, bf16[8,48,1536]{2,1,0:T(8,128)(2,1)S(1)}, u32[]{:S(2)}, u32[]{:S(2)}) %collective-permute-start.21) | collective-permute-done | bytes 1179680 | tf_op jit(solution)/shard_map/ppermute | solution.py:413
  158.5 9.7 %collective-permute-done.27.own_hi = bf16[8,48,1536]{2,1,0:T(8,128)(2,1)} collective-permute-done((bf16[8,48,1536]{2,1,0:T(8,128)(2,1)S(1)}, bf16[8,48,1536]{2,1,0:T(8,128)(2,1)}, u32[]{:S(2)}, u32[]{:S(2)}) %collective-permute-start.27) | collective-permute-done | bytes 1179680 | tf_op jit(solution)/shard_map/ppermute | solution.py:413
  170.8 23.8 %collective-permute-done.33.own_hi = bf16[8,192,384]{2,1,0:T(8,128)(2,1)} collective-permute-done((bf16[8,192,384]{2,1,0:T(8,128)(2,1)}, bf16[8,192,384]{2,1,0:T(8,128)(2,1)}, u32[]{:S(2)}, u32[]{:S(2)}) %collective-permute-start.33) | collective-permute-done | bytes 1179680 | tf_op jit(solution)/shard_map/ppermute | solution.py:413
  215.2 8.1 place.9
  236.4 8.0 place.6
  254.6 23.8 %attend.2 = (bf16[1024,768]{1,0:T(8,128)(2,1)S(1)}, f32[2,16,512]{2,1,0:T(8,128)S(1)}) custom-call(s32[2]{0:T(128)S(1)} %copy-done.35, bf16[1024,1152]{1,0:T(8,128)(2,1)S(1)} %fusion.39.qkv_lo, bf16[1024,1152]{1,0:T(8,128)(2,1)S(1)} %fusion.40.qkv_hi), custom_call_target="tpu_custom_call" | custom-call | flops 6442450944 | bytes 6291456 | tf_op jit(solution)/shard_map/attend/pallas_call | solution.py:135
  288.6 33.0 %fusion.2 = (bf16[1024,3072]{1,0:T(8,128)(2,1)S(1)}, f32[1024,3072]{1,0:T(8,128)}) fusion(f32[3072]{0:T(1024)S(1)} %add.484, bf16[1024,768]{1,0:T(8,128)(2,1)S(1)} %bitcast.330, bf16[768,3072]{1,0:T(8,128)(2,1)S(1)} %bitcast.282), kind=kOutput, calls=%fused_computation.4 | convolution fusion | flops 5039456256 | bytes 25178112 | tf_op jit(solution)/shard_map/dot_general | solution.py:30
  332.7 23.7 %attend.3 = (bf16[1024,768]{1,0:T(8,128)(2,1)S(1)}, f32[2,16,512]{2,1,0:T(8,128)S(1)}) custom-call(s32[2]{0:T(128)S(1)} %copy-done.36, bf16[1024,1152]{1,0:T(8,128)(2,1)S(1)} %add_convert_fusion.1.qkv_lo, bf16[1024,1152]{1,0:T(8,128)(2,1)S(1)} %add_convert_fusion.qkv_hi), custom_call_target="tpu_custom_call" | custom-call | flops 6442450944 | bytes 6291456 | tf_op jit(solution)/shard_map/attend/pallas_call | solution.py:135
  365.1 15.0 %fusion.18 = (bf16[384,3072]{1,0:T(8,128)(2,1)S(1)}, f32[384,3072]{1,0:T(8,128)S(1)}) fusion(f32[3072]{0:T(1024)S(1)} %add.509, bf16[768,3072]{1,0:T(8,128)(2,1)} %bitcast.292, f32[384,768]{1,0:T(8,128)} %slice_add_fusion.1), kind=kOutput, calls=%fused_computation.33 | convolution fusion | flops 1890091008 | bytes 12988416 | tf_op jit(solution)/shard_map/dot_general | solution.py:30
  399.1 27.5 %attend_back.2 = bf16[2,1024,1152]{2,1,0:T(8,128)(2,1)S(1)} custom-call(s32[2]{0:T(128)S(1)} %copy-done.36, bf16[1024,1152]{1,0:T(8,128)(2,1)S(1)} %copy-done.46, bf16[1024,1152]{1,0:T(8,128)(2,1)S(1)} %copy-done.44, bf16[1024,768]{1,0:T(8,128)(2,1)S(1)} %add_convert_fusion.6.d_mixed_ref, f32[2,16,512]{2,1,0:T(8,128)S(1)} %get-tuple-element.37.lse_ref), custom_call_target="tpu_custom_call" | custom-call | flops 16106127360 | bytes 11010048 | tf_op jit(solution)/shard_map/attend_back/pallas_call | solution.py:222
  439.9 8.3 convolution_convert_fusion.2
  448.3 13.5 %convert_reduce_fusion = (bf16[3072]{0:T(1024)(128)(2,1)S(1)}, bf16[1024,3072]{1,0:T(8,128)(2,1)}) fusion(f32[1024,3072]{1,0:T(8,128)} %get-tuple-element.211, f32[3072]{0:T(1024)S(1)} %add.484, bf16[1024,768]{1,0:T(8,128)(2,1)S(1)} %get-tuple-element.144, bf16[3072,768]{1,0:T(8,128)(2,1)S(1)} %bitcast.291), kind=kOutput, calls=%fused_computation.11 | convolution fusion | flops 4872729600 | bytes 25184256 | tf_op jit(solution)/shard_map/dot_general | solution.py:40
  467.8 8.0 multiply_reduce_fusion.2
  482.5 27.5 %attend_back.3 = bf16[2,1024,1152]{2,1,0:T(8,128)(2,1)S(1)} custom-call(s32[2]{0:T(128)S(1)} %copy-done.36, bf16[1024,1152]{1,0:T(8,128)(2,1)S(1)} %copy-done.42, bf16[1024,1152]{1,0:T(8,128)(2,1)S(1)} %copy-done.40, bf16[1024,768]{1,0:T(8,128)(2,1)S(1)} %add_convert_fusion.5.d_mixed_ref, f32[2,16,512]{2,1,0:T(8,128)S(1)} %get-tuple-element.38.lse_ref), custom_call_target="tpu_custom_call" | custom-call | flops 16106127360 | bytes 11010048 | tf_op jit(solution)/shard_map/attend_back/pallas_call | solution.py:222
  548.6 8.5 %convolution_convert_fusion.3 = bf16[3072,384]{1,0:T(8,128)(2,1)} fusion(bf16[1024,3072]{1,0:T(8,128)(2,1)} %copy-done.128, bf16[1024,768]{1,0:T(8,128)(2,1)S(1)} %copy-done.81, s32[]{:T(128)S(6)} %select_n.124), kind=kOutput, calls=%fused_computation.73 | convolution fusion | flops 2417098752 | bytes 9437188 | tf_op jit(solution)/shard_map/dot_general | solution.py:34
  644.9 14.1 %collective-permute-done.37 = bf16[8,48,1536]{2,1,0:T(8,128)(2,1)} collective-permute-done((bf16[8,48,1536]{2,1,0:T(8,128)(2,1)}, bf16[8,48,1536]{2,1,0:T(8,128)(2,1)}, u32[]{:S(2)}, u32[]{:S(2)}) %collective-permute-start.37) | collective-permute-done | bytes 1179680 | tf_op jit(solution)/shard_map/ppermute | solution.py:413
  662.1 24.2 %collective-permute-done.62 = bf16[8,48,1664]{2,1,0:T(8,128)(2,1)S(1)} collective-permute-done((bf16[8,48,1664]{2,1,0:T(8,128)(2,1)}, bf16[8,48,1664]{2,1,0:T(8,128)(2,1)S(1)}, u32[]{:S(2)}, u32[]{:S(2)}) %collective-permute-start.62) | collective-permute-done | bytes 1277984 | tf_op jit(solution)/shard_map/ppermute | solution.py:413
  696.4 32.7 %collective-permute-done.59 = bf16[2,48,1536]{2,1,0:T(8,128)(2,1)S(1)} collective-permute-done((bf16[2,48,1536]{2,1,0:T(8,128)(2,1)S(1)}, bf16[2,48,1536]{2,1,0:T(8,128)(2,1)S(1)}, u32[]{:S(2)}, u32[]{:S(2)}) %collective-permute-start.59) | collective-permute-done | bytes 294944 | tf_op jit(solution)/shard_map/ppermute | solution.py:413
  (707 shorter events, 420.4 us)
Async XLA Ops:
  32.4 46.9 %collective-permute-start.19 = (bf16[2,48,1536]{2,1,0:T(8,128)(2,1)S(1)}, bf16[2,48,1536]{2,1,0:T(8,128)(2,1)S(1)}, u32[]{:S(2)}, u32[]{:S(2)}) collective-permute-start(bf16[2,48,1536]{2,1,0:T(8,128)(2,1)S(1)} %pad_maximum_fusion.21), channel_id=1, source_target_pairs={{0,8},{1,9},{2,10},{3,11},{4,12},{5,13},{6,14},{7,15},{8,0},{9,1},... | collective-permute-start | bytes 884744 | tf_op jit(solution)/shard_map/ppermute | solution.py:413
  34.6 51.0 %collective-permute-start.25 = (bf16[2,48,1536]{2,1,0:T(8,128)(2,1)S(1)}, bf16[2,48,1536]{2,1,0:T(8,128)(2,1)S(1)}, u32[]{:S(2)}, u32[]{:S(2)}) collective-permute-start(bf16[2,48,1536]{2,1,0:T(8,128)(2,1)S(1)} %pad_maximum_fusion.22), channel_id=1, source_target_pairs={{0,8},{1,9},{2,10},{3,11},{4,12},{5,13},{6,14},{7,15},{8,0},{9,1},... | collective-permute-start | bytes 884744 | tf_op jit(solution)/shard_map/ppermute | solution.py:413
  35.5 56.5 %collective-permute-start.31 = (bf16[2,192,384]{2,1,0:T(8,128)(2,1)S(1)}, bf16[2,192,384]{2,1,0:T(8,128)(2,1)S(1)}, u32[]{:S(2)}, u32[]{:S(2)}) collective-permute-start(bf16[2,192,384]{2,1,0:T(8,128)(2,1)S(1)} %pad_maximum_fusion.23), channel_id=1, source_target_pairs={{0,8},{1,9},{2,10},{3,11},{4,12},{5,13},{6,14},{7,15},{8,0},{9,1},... | collective-permute-start | bytes 884744 | tf_op jit(solution)/shard_map/ppermute | solution.py:413
  37.7 58.6 %collective-permute-start.1 = (bf16[2,48,1664]{2,1,0:T(8,128)(2,1)S(1)}, bf16[2,48,1664]{2,1,0:T(8,128)(2,1)S(1)}, u32[]{:S(2)}, u32[]{:S(2)}) collective-permute-start(bf16[2,48,1664]{2,1,0:T(8,128)(2,1)S(1)} %pad_maximum_fusion.18), channel_id=1, source_target_pairs={{0,8},{1,9},{2,10},{3,11},{4,12},{5,13},{6,14},{7,15},{8,0},{9,1},... | collective-permute-start | bytes 958472 | tf_op jit(solution)/shard_map/ppermute | solution.py:413
  93.7 47.8 %collective-permute-start.9 = (bf16[8,48,1536]{2,1,0:T(8,128)(2,1)S(1)}, bf16[8,48,1536]{2,1,0:T(8,128)(2,1)S(1)}, u32[]{:S(2)}, u32[]{:S(2)}) collective-permute-start(bf16[8,48,1536]{2,1,0:T(8,128)(2,1)S(1)} %pad_maximum_fusion.5.own_lo), channel_id=1, source_target_pairs={{0,1},{1,0},{2,3},{3,2},{4,5},{5,4},{6,7},{7,6},{8,9},{9,8},{10,11... | collective-permute-start | bytes 3538952 | tf_op jit(solution)/shard_map/ppermute | solution.py:413
  95.3 46.3 %collective-permute-start.10 = (bf16[8,48,1536]{2,1,0:T(8,128)(2,1)S(1)}, bf16[8,48,1536]{2,1,0:T(8,128)(2,1)S(1)}, u32[]{:S(2)}, u32[]{:S(2)}) collective-permute-start(bf16[8,48,1536]{2,1,0:T(8,128)(2,1)S(1)} %pad_maximum_fusion.5.own_lo), channel_id=1, source_target_pairs={{0,16},{16,0},{1,17},{17,1},{2,18},{18,2},{3,19},{19,3},{4,20},{20... | collective-permute-start | bytes 3538952 | tf_op jit(solution)/shard_map/ppermute | solution.py:417
  96.3 46.3 %collective-permute-start.15 = (bf16[8,192,384]{2,1,0:T(8,128)(2,1)S(1)}, bf16[8,192,384]{2,1,0:T(8,128)(2,1)S(1)}, u32[]{:S(2)}, u32[]{:S(2)}) collective-permute-start(bf16[8,192,384]{2,1,0:T(8,128)(2,1)S(1)} %pad_maximum_fusion.6.own_lo), channel_id=1, source_target_pairs={{0,1},{1,0},{2,3},{3,2},{4,5},{5,4},{6,7},{7,6},{8,9},{9,8},{10,11... | collective-permute-start | bytes 3538952 | tf_op jit(solution)/shard_map/ppermute | solution.py:413
  144.4 50.2 %collective-permute-start.3 = (bf16[8,48,1664]{2,1,0:T(8,128)(2,1)S(1)}, bf16[8,48,1664]{2,1,0:T(8,128)(2,1)}, u32[]{:S(2)}, u32[]{:S(2)}) collective-permute-start(bf16[8,48,1664]{2,1,0:T(8,128)(2,1)S(1)} %pad_maximum_fusion.4.own_lo), channel_id=1, source_target_pairs={{0,1},{1,0},{2,3},{3,2},{4,5},{5,4},{6,7},{7,6},{8,9},{9,8},{10,11... | collective-permute-start | bytes 3833864 | tf_op jit(solution)/shard_map/ppermute | solution.py:413
  194.6 41.8 %collective-permute-start.4 = (bf16[8,48,1664]{2,1,0:T(8,128)(2,1)S(1)}, bf16[8,48,1664]{2,1,0:T(8,128)(2,1)}, u32[]{:S(2)}, u32[]{:S(2)}) collective-permute-start(bf16[8,48,1664]{2,1,0:T(8,128)(2,1)S(1)} %pad_maximum_fusion.4.own_lo), channel_id=1, source_target_pairs={{0,16},{16,0},{1,17},{17,1},{2,18},{18,2},{3,19},{19,3},{4,20},{20... | collective-permute-start | bytes 3833864 | tf_op jit(solution)/shard_map/ppermute | solution.py:417
  194.6 41.8 %collective-permute-start.5 = (bf16[8,48,1664]{2,1,0:T(8,128)(2,1)}, bf16[8,48,1664]{2,1,0:T(8,128)(2,1)}, u32[]{:S(2)}, u32[]{:S(2)}) collective-permute-start(bf16[8,48,1664]{2,1,0:T(8,128)(2,1)} %collective-permute-done.3.own_hi), channel_id=1, source_target_pairs={{0,16},{16,0},{1,17},{17,1},{2,18},{18,2},{3,19},{19,3},{4,20},{20... | collective-permute-start | bytes 3833864 | tf_op jit(solution)/shard_map/ppermute | solution.py:417
  543.3 51.2 %collective-permute-start.46 = (bf16[16,48,1536]{2,1,0:T(8,128)(2,1)}, bf16[16,48,1536]{2,1,0:T(8,128)(2,1)}, u32[]{:S(2)}, u32[]{:S(2)}) collective-permute-start(bf16[16,48,1536]{2,1,0:T(8,128)(2,1)} %pad_maximum_fusion.3), channel_id=1, source_target_pairs={{0,16},{16,0},{1,17},{17,1},{2,18},{18,2},{3,19},{19,3},{4,20},{20... | collective-permute-start | bytes 7077896 | tf_op jit(solution)/shard_map/ppermute | solution.py:417
  561.8 64.3 %collective-permute-start.61 = (bf16[16,48,1664]{2,1,0:T(8,128)(2,1)}, bf16[16,48,1664]{2,1,0:T(8,128)(2,1)}, u32[]{:S(2)}, u32[]{:S(2)}) collective-permute-start(bf16[16,48,1664]{2,1,0:T(8,128)(2,1)} %pad_maximum_fusion.1), channel_id=1, source_target_pairs={{0,16},{16,0},{1,17},{17,1},{2,18},{18,2},{3,19},{19,3},{4,20},{20... | collective-permute-start | bytes 7667720 | tf_op jit(solution)/shard_map/ppermute | solution.py:417
  562.3 45.0 %collective-permute-start.41 = (bf16[16,192,384]{2,1,0:T(8,128)(2,1)}, bf16[16,192,384]{2,1,0:T(8,128)(2,1)}, u32[]{:S(2)}, u32[]{:S(2)}) collective-permute-start(bf16[16,192,384]{2,1,0:T(8,128)(2,1)} %bitcast.41), channel_id=1, source_target_pairs={{0,16},{16,0},{1,17},{17,1},{2,18},{18,2},{3,19},{19,3},{4,20},{20... | collective-permute-start | bytes 7077896 | tf_op jit(solution)/shard_map/ppermute | solution.py:417
  567.6 51.4 %collective-permute-start.36 = (bf16[16,48,1536]{2,1,0:T(8,128)(2,1)}, bf16[16,48,1536]{2,1,0:T(8,128)(2,1)}, u32[]{:S(2)}, u32[]{:S(2)}) collective-permute-start(bf16[16,48,1536]{2,1,0:T(8,128)(2,1)} %bitcast.38), channel_id=1, source_target_pairs={{0,16},{16,0},{1,17},{17,1},{2,18},{18,2},{3,19},{19,3},{4,20},{20... | collective-permute-start | bytes 7077896 | tf_op jit(solution)/shard_map/ppermute | solution.py:417
  579.0 56.5 %collective-permute-start.57 = (bf16[8,48,1536]{2,1,0:T(8,128)(2,1)}, bf16[8,48,1536]{2,1,0:T(8,128)(2,1)}, u32[]{:S(2)}, u32[]{:S(2)}) collective-permute-start(bf16[8,48,1536]{2,1,0:T(8,128)(2,1)} %get-tuple-element.48), channel_id=1, source_target_pairs={{0,1},{1,0},{2,3},{3,2},{4,5},{5,4},{6,7},{7,6},{8,9},{9,8},{10,11... | collective-permute-start | bytes 3538952 | tf_op jit(solution)/shard_map/ppermute | solution.py:413
  594.5 43.0 %collective-permute-start.52 = (bf16[8,192,384]{2,1,0:T(8,128)(2,1)}, bf16[8,192,384]{2,1,0:T(8,128)(2,1)}, u32[]{:S(2)}, u32[]{:S(2)}) collective-permute-start(bf16[8,192,384]{2,1,0:T(8,128)(2,1)} %get-tuple-element.46), channel_id=1, source_target_pairs={{0,1},{1,0},{2,3},{3,2},{4,5},{5,4},{6,7},{7,6},{8,9},{9,8},{10,11... | collective-permute-start | bytes 3538952 | tf_op jit(solution)/shard_map/ppermute | solution.py:413
  635.5 50.8 %collective-permute-start.62 = (bf16[8,48,1664]{2,1,0:T(8,128)(2,1)}, bf16[8,48,1664]{2,1,0:T(8,128)(2,1)S(1)}, u32[]{:S(2)}, u32[]{:S(2)}) collective-permute-start(bf16[8,48,1664]{2,1,0:T(8,128)(2,1)} %get-tuple-element.50), channel_id=1, source_target_pairs={{0,1},{1,0},{2,3},{3,2},{4,5},{5,4},{6,7},{7,6},{8,9},{9,8},{10,11... | collective-permute-start | bytes 3833864 | tf_op jit(solution)/shard_map/ppermute | solution.py:413
  637.5 50.6 %collective-permute-start.58 = (bf16[4,48,1536]{2,1,0:T(8,128)(2,1)S(1)}, bf16[4,48,1536]{2,1,0:T(8,128)(2,1)S(1)}, u32[]{:S(2)}, u32[]{:S(2)}) collective-permute-start(bf16[4,48,1536]{2,1,0:T(8,128)(2,1)S(1)} %slice.559), channel_id=1, source_target_pairs={{0,2},{1,3},{2,0},{3,1},{4,6},{5,7},{6,4},{7,5},{8,10},{9,11},{10,... | collective-permute-start | bytes 1769480 | tf_op jit(solution)/shard_map/ppermute | solution.py:413
  640.7 48.3 %collective-permute-start.53 = (bf16[4,192,384]{2,1,0:T(8,128)(2,1)S(1)}, bf16[4,192,384]{2,1,0:T(8,128)(2,1)S(1)}, u32[]{:S(2)}, u32[]{:S(2)}) collective-permute-start(bf16[4,192,384]{2,1,0:T(8,128)(2,1)S(1)} %slice.553), channel_id=1, source_target_pairs={{0,2},{1,3},{2,0},{3,1},{4,6},{5,7},{6,4},{7,5},{8,10},{9,11},{10,... | collective-permute-start | bytes 1769480 | tf_op jit(solution)/shard_map/ppermute | solution.py:413
  641.8 47.5 %collective-permute-start.48 = (bf16[4,48,1536]{2,1,0:T(8,128)(2,1)S(1)}, bf16[4,48,1536]{2,1,0:T(8,128)(2,1)S(1)}, u32[]{:S(2)}, u32[]{:S(2)}) collective-permute-start(bf16[4,48,1536]{2,1,0:T(8,128)(2,1)S(1)} %slice.547), channel_id=1, source_target_pairs={{0,2},{1,3},{2,0},{3,1},{4,6},{5,7},{6,4},{7,5},{8,10},{9,11},{10,... | collective-permute-start | bytes 1769480 | tf_op jit(solution)/shard_map/ppermute | solution.py:413
  688.2 63.5 %collective-permute-start.63 = (bf16[4,48,1664]{2,1,0:T(8,128)(2,1)S(1)}, bf16[4,48,1664]{2,1,0:T(8,128)(2,1)S(1)}, u32[]{:S(2)}, u32[]{:S(2)}) collective-permute-start(bf16[4,48,1664]{2,1,0:T(8,128)(2,1)S(1)} %slice.569), channel_id=1, source_target_pairs={{0,2},{1,3},{2,0},{3,1},{4,6},{5,7},{6,4},{7,5},{8,10},{9,11},{10,... | collective-permute-start | bytes 1916936 | tf_op jit(solution)/shard_map/ppermute | solution.py:413
  689.3 46.2 %collective-permute-start.54 = (bf16[2,192,384]{2,1,0:T(8,128)(2,1)S(1)}, bf16[2,192,384]{2,1,0:T(8,128)(2,1)S(1)}, u32[]{:S(2)}, u32[]{:S(2)}) collective-permute-start(bf16[2,192,384]{2,1,0:T(8,128)(2,1)S(1)} %slice.555), channel_id=1, source_target_pairs={{0,8},{1,9},{2,10},{3,11},{4,12},{5,13},{6,14},{7,15},{8,0},{9,1},... | collective-permute-start | bytes 884744 | tf_op jit(solution)/shard_map/ppermute | solution.py:413
  692.4 49.4 %collective-permute-start.49 = (bf16[2,48,1536]{2,1,0:T(8,128)(2,1)S(1)}, bf16[2,48,1536]{2,1,0:T(8,128)(2,1)S(1)}, u32[]{:S(2)}, u32[]{:S(2)}) collective-permute-start(bf16[2,48,1536]{2,1,0:T(8,128)(2,1)S(1)} %slice.549), channel_id=1, source_target_pairs={{0,8},{1,9},{2,10},{3,11},{4,12},{5,13},{6,14},{7,15},{8,0},{9,1},... | collective-permute-start | bytes 884744 | tf_op jit(solution)/shard_map/ppermute | solution.py:413
  696.2 51.9 %collective-permute-start.44 = (bf16[2,192,384]{2,1,0:T(8,128)(2,1)S(1)}, bf16[2,192,384]{2,1,0:T(8,128)(2,1)S(1)}, u32[]{:S(2)}, u32[]{:S(2)}) collective-permute-start(bf16[2,192,384]{2,1,0:T(8,128)(2,1)S(1)} %slice.543), channel_id=1, source_target_pairs={{0,8},{1,9},{2,10},{3,11},{4,12},{5,13},{6,14},{7,15},{8,0},{9,1},... | collective-permute-start | bytes 884744 | tf_op jit(solution)/shard_map/ppermute | solution.py:413
  (208 other events, 3001.3 us)

commit v3 on v2

--- a/solution.py
+++ b/solution.py
@@ -1,3 +1,4 @@
+import functools
 import math
 
 import jax
@@ -13,6 +14,7 @@
 MCAP = 384
 LANES = 128
 QUERY_BLOCK = 256
+HIDDEN_BLOCK = 512
 
 
 LN_EPS = 1e-06
@@ -90,11 +92,11 @@
     return ref[:, pl.ds(at, LANES)].astype(jnp.float32)
 
 
-def attend_kernel(len_ref, qkv_lo, qkv_hi, mixed_ref, lse_ref, ot_ref):
+def attend_kernel(seq, len_ref, qkv_lo, qkv_hi, mixed_ref, lse_ref, ot_ref):
     rows = mixed_ref.shape[0]
     width = qkv_lo.shape[1] // 3
     pairs = width // LANES
-    real = len_ref[pl.program_id(0)]
+    real = len_ref[seq]
     lane = lax.broadcasted_iota(jnp.int32, (rows, LANES), 1)
     place_key = lax.broadcasted_iota(jnp.int32, (rows, LANES), 0)
     bias = jnp.where(place_key < real, 0.0, NEG_FILL)
@@ -125,37 +127,44 @@
         lax.fori_loop(0, pairs, one_pair, 0)
 
 
-def attend_core(qkv_lo, qkv_hi, seq_lengths):
+def attend_core(qkv_lo, qkv_hi, seq_lengths, seq, filled=None):
     total, wide = qkv_lo.shape
     seqs = seq_lengths.shape[0]
     rows, width = total // seqs, 2 * wide // 3
     heads = width // HEAD_DIM
     lse_rows = -(-heads // 8) * 8
-    side = pl.BlockSpec((rows, wide), lambda seq, lens: (seq, 0))
+    side = pl.BlockSpec((rows, wide), lambda at, lens: (seq, 0))
+    kept = [] if filled is None else list(filled)
+    anywhere = pl.BlockSpec(memory_space=pl.ANY)
+
+    def kernel(len_ref, lo_ref, hi_ref, *rest):
+        attend_kernel(seq, len_ref, lo_ref, hi_ref, *rest[len(kept) :])
+
     return pl.pallas_call(
-        attend_kernel,
+        kernel,
         out_shape=(
             jax.ShapeDtypeStruct((total, width), jnp.bfloat16),
             jax.ShapeDtypeStruct((seqs, lse_rows, rows), jnp.float32),
         ),
         grid_spec=pltpu.PrefetchScalarGridSpec(
             num_scalar_prefetch=1,
-            grid=(seqs,),
-            in_specs=[side, side],
+            grid=(1,),
+            in_specs=[side, side] + [anywhere] * len(kept),
             out_specs=[
-                pl.BlockSpec((rows, width), lambda seq, lens: (seq, 0)),
-                pl.BlockSpec((None, lse_rows, rows), lambda seq, lens: (seq, 0, 0)),
+                pl.BlockSpec((rows, width), lambda at, lens: (seq, 0)),
+                pl.BlockSpec((None, lse_rows, rows), lambda at, lens: (seq, 0, 0)),
             ],
             scratch_shapes=[pltpu.VMEM((LANES, rows), jnp.float32)],
         ),
-        compiler_params=pltpu.CompilerParams(vmem_limit_bytes=32 << 20),
+        input_output_aliases={3 + at: at for at in range(len(kept))},
+        compiler_params=pltpu.CompilerParams(vmem_limit_bytes=24 << 20),
         cost_estimate=pl.CostEstimate(
-            flops=16 * total * rows * width,
-            bytes_accessed=8 * total * width,
-            transcendentals=total * rows * heads,
+            flops=16 * rows * rows * width,
+            bytes_accessed=8 * rows * width,
+            transcendentals=rows * rows * heads,
         ),
         name="attend",
-    )(seq_lengths, qkv_lo, qkv_hi)
+    )(seq_lengths, qkv_lo, qkv_hi, *kept)
 
 
 def attend_back_kernel(
@@ -253,91 +262,158 @@
     return lax.dynamic_slice_in_dim(rows, side * width, width, 1)
 
 
-def attend_forward(flat_rows, flat_low, attn_layer, small_layer, seq_lengths):
-    model_width = flat_rows.shape[1]
-    third = model_width // 2
+def project_in(flat_low, in_layer, small_layer):
+    third = flat_low.shape[1] // 2
     qkv = []
     for side in range(2):
         cols = slice(side * third, (side + 1) * third)
         bias = jnp.concatenate(
             [small_layer[0, cols], jnp.zeros((third,), jnp.float32), small_layer[1, cols]]
         )
-        part = forward_product(flat_low, attn_layer[side, :, : 3 * third]) + bias
+        part = forward_product(flat_low, in_layer[side]) + bias
         qkv.append(part.astype(jnp.bfloat16))
-    mixed_heads, lse = attend_core(qkv[0], qkv[1], seq_lengths)
-    branch = jnp.concatenate(
-        [
-            forward_product(mixed_heads, attn_layer[side, :, 3 * third : 4 * third])
-            for side in range(2)
-        ],
-        axis=1,
-    )
-    normed, normal_part, inv_std = norm_forward(
-        flat_rows + branch + small_layer[2], small_layer[3], small_layer[4]
-    )
-    return (normed, (flat_low, qkv, lse, mixed_heads, normal_part, inv_std))
-
-
-def attend_backward(d_normed, kept_state, attn_layer, small_layer, seq_lengths, core):
-    flat_low, qkv, lse, mixed_heads, normal_part, inv_std = kept_state
-    row_count, model_width = flat_low.shape
-    third = model_width // 2
+    return qkv
+
+
+def project_out(flat_rows, mixed_heads, out_layer, small_layer):
+    branch = forward_product(mixed_heads, out_layer)
+    return norm_forward(flat_rows + branch + small_layer[2], small_layer[3], small_layer[4])
+
+
+def project_out_back(d_normed, normal_part, inv_std, out_layer, small_layer):
     d_resid, d_gain, d_shift = norm_backward(d_normed, normal_part, inv_std, small_layer[3])
     d_branch = d_resid.astype(jnp.bfloat16)
     d_out_bias = jnp.sum(d_branch.astype(jnp.float32), axis=0)
-    d_mixed = sum(
-        back_product(
-            d_branch[:, side * third : (side + 1) * third],
-            attn_layer[side, :, 3 * third : 4 * third],
+    d_mixed = back_product(d_branch, out_layer).astype(jnp.bfloat16)
+    return (d_resid, d_branch, d_mixed, (d_out_bias, d_gain, d_shift))
+
+
+def project_in_back(d_resid, d_qkv, in_layer):
+    return d_resid + sum(back_product(d_qkv[side], in_layer[side]) for side in range(2))
+
+
+def attn_small(d_qkv, sums_out):
+    third = d_qkv.shape[2] // 3
+    sums = jnp.sum(d_qkv.astype(jnp.float32), axis=1)
+    return jnp.stack(
+        [sums[:, :third].reshape(-1), sums[:, 2 * third :].reshape(-1)] + list(sums_out)
+    )
+
+
+def attn_grads_kernel(core, x_ref, mixed_ref, d_qkv_ref, d_branch_ref, *rest):
+    small_ref = rest[0] if len(rest) == 5 else None
+    far_ref, own_ref, xt_ref, mixed_t_ref = rest[-4:]
+    third = d_branch_ref.shape[1]
+
+    @pl.when(pl.program_id(0) == 0)
+    def _():
+        xt_ref[...] = x_ref[...].T
+        mixed_t_ref[...] = mixed_ref[...].T
+
+    def fill(out_ref):
+        out_ref[:, : 3 * third] = forward_product(xt_ref[...], d_qkv_ref[...]).astype(jnp.bfloat16)
+        out_ref[:, 3 * third : 4 * third] = forward_product(
+            mixed_t_ref[...], d_branch_ref[...]
+        ).astype(jnp.bfloat16)
+        if small_ref is not None:
+            out_ref[:, 4 * third :] = small_ref[...]
+
+    @pl.when(pl.program_id(0) == 0)
+    def _():
+        fill(far_ref)
+
+    @pl.when(pl.program_id(0) == 1)
+    def _():
+        fill(own_ref)
+
+
+def attn_grads(core, x_low, mixed_heads, d_qkv, d_branch, small=None):
+    total, width = x_low.shape
+    third = width // 2
+    extra = 0 if small is None else small.shape[2]
+
+    def side(at, core):
+        return jnp.where(at == 0, 1 - core[0], core[0])
+
+    specs = [pl.BlockSpec((total, width), lambda at, core: (0, 0))] * 2 + [
+        pl.BlockSpec((None, total, 3 * third), lambda at, core: (side(at, core), 0, 0)),
+        pl.BlockSpec((total, third), lambda at, core: (0, side(at, core))),
+    ]
+    given = [x_low, mixed_heads, d_qkv, d_branch]
+    if small is not None:
+        specs.append(
+            pl.BlockSpec((None, width, extra), lambda at, core: (side(at, core), 0, 0))
         )
-        for side in range(2)
-    ).astype(jnp.bfloat16)
-    d_qkv = attend_core_back(qkv[0], qkv[1], d_mixed, lse, seq_lengths)
-
-    def weights_of(side):
-        return jnp.concatenate(
-            [
-                weight_grad(flat_low, lax.dynamic_index_in_dim(d_qkv, side, 0, False)),
-                weight_grad(mixed_heads, half_of(d_branch, side)),
-            ],
-            axis=1,
-        )
-
-    far = weights_of(1 - core)
-    own = weights_of(core)
-    d_hidden = d_resid + sum(
-        back_product(d_qkv[side], attn_layer[side, :, : 3 * third]) for side in range(2)
-    )
-    sums = jnp.sum(d_qkv.astype(jnp.float32), axis=1)
-    small_rows = jnp.stack(
-        [
-            sums[:, :third].reshape(model_width),
-            sums[:, 2 * third :].reshape(model_width),
-            d_out_bias,
-            d_gain,
-            d_shift,
-        ]
-    )
-    return (d_hidden, own, far, small_rows)
-
-
-def feed_forward(rows_in, up_layer, down_layer, small_layer):
+        given.append(small)
+    shape = jax.ShapeDtypeStruct((width, 4 * third + extra), jnp.bfloat16)
+    return pl.pallas_call(
+        attn_grads_kernel,
+        out_shape=(shape, shape),
+        grid_spec=pltpu.PrefetchScalarGridSpec(
+            num_scalar_prefetch=1,
+            grid=(2,),
+            in_specs=specs,
+            out_specs=[pl.BlockSpec(shape.shape, lambda at, core: (0, 0))] * 2,
+            scratch_shapes=[pltpu.VMEM((width, total), jnp.bfloat16)] * 2,
+        ),
+        compiler_params=pltpu.CompilerParams(vmem_limit_bytes=36 << 20),
+        cost_estimate=pl.CostEstimate(
+            flops=8 * total * width * width,
+            bytes_accessed=2 * (8 * total * width + 4 * width * width),
+            transcendentals=0,
+        ),
+        name="attn_grads",
+    )(core.reshape(1).astype(jnp.int32), *given)
+
+
+def feed_up_kernel(rows_ref, up_ref, bias_ref, act_ref, slope_ref):
+    low_rows = rows_ref[...]
+    for at in range(0, up_ref.shape[1], HIDDEN_BLOCK):
+        cols = slice(at, at + HIDDEN_BLOCK)
+        pre_act = forward_product(low_rows, up_ref[:, cols]) + bias_ref[:, cols]
+        below = 0.5 * (1.0 + lax.erf(pre_act * 0.7071067811865476))
+        density = jnp.exp(-0.5 * pre_act * pre_act) * 0.3989422804014327
+        act_ref[:, cols] = (pre_act * below).astype(jnp.bfloat16)
+        slope_ref[:, cols] = (below + pre_act * density).astype(jnp.bfloat16)
+
+
+def feed_up(rows_in, up_layer, small_layer):
     rows_low = rows_in.astype(jnp.bfloat16)
-    pre_act = forward_product(rows_low, up_layer) + small_layer[5:9].reshape(-1)
-    act_low = jax.nn.gelu(pre_act, approximate=False).astype(jnp.bfloat16)
+    total, width = rows_low.shape
+    hidden = up_layer.shape[1]
+    block = math.gcd(total, 256)
+    bias = small_layer[5:9].reshape(1, hidden)
+    shape = jax.ShapeDtypeStruct((total, hidden), jnp.bfloat16)
+    act_low, slope = pl.pallas_call(
+        feed_up_kernel,
+        out_shape=(shape, shape),
+        grid=(total // block,),
+        in_specs=[
+            pl.BlockSpec((block, width), lambda at: (at, 0)),
+            pl.BlockSpec((width, hidden), lambda at: (0, 0)),
+            pl.BlockSpec((1, hidden), lambda at: (0, 0)),
+        ],
+        out_specs=[pl.BlockSpec((block, hidden), lambda at: (at, 0))] * 2,
+        compiler_params=pltpu.CompilerParams(vmem_limit_bytes=32 << 20),
+        cost_estimate=pl.CostEstimate(
+            flops=2 * total * width * hidden,
+            bytes_accessed=2 * (width * hidden + 2 * total * hidden),
+            transcendentals=2 * total * hidden,
+        ),
+        name="feed_up",
+    )(rows_low, up_layer, bias)
+    return (rows_low, act_low, slope)
+
+
+def feed_down(rows_in, act_low, down_layer, small_layer):
     branch = forward_product(act_low, down_layer) + small_layer[9]
-    normed, normal_part, inv_std = norm_forward(rows_in + branch, small_layer[10], small_layer[11])
-    return (normed, (rows_low, pre_act, act_low, normal_part, inv_std))
-
-
-def feed_backward(d_normed, kept_state, up_layer, down_layer, small_layer, core):
-    rows_low, pre_act, act_low, normal_part, inv_std = kept_state
+    return norm_forward(rows_in + branch, small_layer[10], small_layer[11])
+
+
+def feed_down_back(d_normed, normal_part, inv_std, slope, down_layer, small_layer):
     d_resid, d_gain, d_shift = norm_backward(d_normed, normal_part, inv_std, small_layer[10])
     d_branch = d_resid.astype(jnp.bfloat16)
-    d_down = [weight_grad(act_low, half_of(d_branch, side)) for side in (1 - core, core)]
-    d_pre = (back_product(d_branch, down_layer) * gelu_slope(pre_act)).astype(jnp.bfloat16)
-    d_up = [weight_grad(rows_low, half_of(d_pre, side)) for side in (1 - core, core)]
-    d_rows = d_resid + back_product(d_pre, up_layer)
+    d_pre = (back_product(d_branch, down_layer) * slope.astype(jnp.float32)).astype(jnp.bfloat16)
     model_width = d_resid.shape[1]
     small_rows = jnp.concatenate(
         [
@@ -346,7 +422,91 @@
         ],
         axis=0,
     )
-    return (d_rows, d_up, d_down, small_rows)
+    return (d_resid, d_branch, d_pre, small_rows)
+
+
+def feed_grads_kernel(shard, core, low_ref, d_pre_ref, act_ref, d_branch_ref, *rest):
+    far_ref, own_ref, low_t_ref, down_ref = rest
+    at = pl.program_id(0)
+    width = low_ref.shape[1]
+    third = width // 2
+
+    @pl.when(at == 0)
+    def _():
+        low_t_ref[...] = low_ref[...].T
+
+    for step in range(4):
+
+        @pl.when(at == step)
+        def _(step=step):
+            out_ref = far_ref if step < 2 else own_ref
+            cols = slice((step % 2) * width, (step % 2 + 1) * width)
+            out_ref[:, cols] = forward_product(low_t_ref[...], d_pre_ref[...]).astype(jnp.bfloat16)
+
+    @pl.when(at >= 4)
+    def _():
+        down_ref[...] = weight_grad(act_ref[...], d_branch_ref[...])
+        blocks = width // (4 * shard)
+        for out_ref, side in ((far_ref, 1 - core[0]), (own_ref, core[0])):
+            from_cols = pl.ds(pl.multiple_of(side * third, LANES), third)
+            for block in range(blocks):
+                row = pl.multiple_of(((at - 4) * blocks + block) * shard, 16)
+                for part in range(4):
+                    start = (block * 4 + part) * shard
+                    cols = slice(2 * width + part * third, 2 * width + (part + 1) * third)
+                    out_ref[pl.ds(row, shard), cols] = down_ref[
+                        start : start + shard, from_cols
+                    ].astype(jnp.bfloat16)
+
+
+def feed_grads_plain(core, rows_low, d_pre, act_low, d_branch, shard):
+    sides = []
+    width = rows_low.shape[1]
+    for side in (1 - core, core):
+        d_up = weight_grad(rows_low, half_of(d_pre, side))
+        d_down = weight_grad(act_low, half_of(d_branch, side))
+        d_down = d_down.reshape(-1, 4, shard, width // 2).transpose(0, 2, 1, 3)
+        sides.append(jnp.concatenate([d_up, d_down.reshape(width, -1)], axis=1))
+    return [part.astype(jnp.bfloat16) for part in sides]
+
+
+def feed_grads(core, rows_low, d_pre, act_low, d_branch, shard):
+    total, width = rows_low.shape
+    hidden = act_low.shape[1]
+    if shard % 16 or hidden != 4 * width:
+        return feed_grads_plain(core, rows_low, d_pre, act_low, d_branch, shard)
+
+    def pre_at(at, core):
+        step = jnp.minimum(at, 3)
+        return (0, jnp.where(step < 2, 1 - core[0], core[0]) * 2 + step % 2)
+
+    shape = jax.ShapeDtypeStruct((width, hidden), jnp.bfloat16)
+    return pl.pallas_call(
+        functools.partial(feed_grads_kernel, shard),
+        out_shape=(shape, shape),
+        grid_spec=pltpu.PrefetchScalarGridSpec(
+            num_scalar_prefetch=1,
+            grid=(8,),
+            in_specs=[
+                pl.BlockSpec((total, width), lambda at, core: (0, 0)),
+                pl.BlockSpec((total, width), pre_at),
+                pl.BlockSpec((total, width), lambda at, core: (0, jnp.maximum(at - 4, 0))),
+                pl.BlockSpec((total, width), lambda at, core: (0, 0)),
+            ],
+            out_specs=[pl.BlockSpec((width, hidden), lambda at, core: (0, 0))] * 2,
+            scratch_shapes=[
+                pltpu.VMEM((width, total), jnp.bfloat16),
+                pltpu.VMEM((width, width), jnp.float32),
+            ],
+        ),
+        compiler_params=pltpu.CompilerParams(vmem_limit_bytes=40 << 20),
+        cost_estimate=pl.CostEstimate(
+            flops=4 * total * width * hidden,
+            bytes_accessed=2 * (4 * total * hidden + 2 * width * hidden),
+            transcendentals=0,
+        ),
+        name="feed_grads",
+    )(core.reshape(1).astype(jnp.int32), rows_low, d_pre, act_low, d_branch)
 
 
 def row_select(token_mask, capacity):
@@ -400,7 +560,7 @@
     rest = bits - deep
     x_bits = [1 << at for at in range(rest - rest // 2)]
     y_bits = [1 << at for at in range(rest - rest // 2, rest)]
-    z_bits = [1 << at for at in range(rest, bits)]
+    z_bits = [1 << at for at in reversed(range(rest, bits))]
     first = z_bits + y_bits + x_bits
     second = z_bits + x_bits + y_bits
     return (first, second if len(x_bits) == len(y_bits) else first)
@@ -429,111 +589,181 @@
     return jnp.concatenate([mine ^ own, mine ^ far, core.reshape(1).astype(jnp.int32)])
 
 
-def place_kernel(spots, own_lo, own_hi, far_lo, far_hi, out, held, in_sems, out_sems):
-    half, rows, width = own_lo.shape
+def place_kernel(plan, spots, *refs):
+    parts, outs = refs[:4], refs[4:]
+    half, rows, _ = parts[0].shape
     core = spots[4 * half]
-    loads = []
-    for number, part in enumerate((own_lo, own_hi, far_lo, far_hi)):
-        loads.append(pltpu.make_async_copy(part, held.at[number], in_sems.at[number]))
-        loads[-1].start()
-    stores = []
-    for number, load in enumerate(loads):
-        load.wait()
+
+    for number, part in enumerate(parts):
         side = core if number < 2 else 1 - core
-        for at in range(half):
+
+        def one_block(at, carry, number=number, part=part, side=side):
             spot = spots[number * half + at]
-            if len(out.shape) == 4:
-                target = out.at[side, spot]
-            else:
-                target = out.at[spot, :, pl.ds(pl.multiple_of(side * width, LANES), width)]
-            stores.append(
-                pltpu.make_async_copy(held.at[number, at], target, out_sems.at[number, at])
-            )
-            stores[-1].start()
-    for store in stores:
-        store.wait()
-
-
-def place(spots, parts, stacked):
-    half, rows, width = parts[0].shape
+            for (start, width, kind), out in zip(plan, outs):
+                cols = pl.ds(pl.multiple_of(side * width, LANES), width)
+                if kind == "stack":
+                    out[side, spot] = part[at, :, start : start + width]
+                elif kind == "wide":
+                    out[spot, :, cols] = part[at, :, start : start + width]
+                else:
+                    for piece in range(4):
+                        begin = start + piece * width
+                        out[spot, piece * rows : (piece + 1) * rows, cols] = part[
+                            at, :, begin : begin + width
+                        ]
+            return carry
+
+        lax.fori_loop(0, half, one_block, 0)
+
+
+def place(spots, parts, plan):
+    half, rows, whole = parts[0].shape
     peers = 2 * half
-    shape = (2, peers, rows, width) if stacked else (peers, rows, 2 * width)
-    return pl.pallas_call(
-        place_kernel,
-        out_shape=jax.ShapeDtypeStruct(shape, parts[0].dtype),
+    kinds = [
+        (start, 4 * width, "stack") if kind == "down" and rows % 16 else (start, width, kind)
+        for start, width, kind in plan
+    ]
+    shapes = {
+        "stack": lambda width: (2, peers, rows, width),
+        "wide": lambda width: (peers, rows, 2 * width),
+        "down": lambda width: (peers, 4 * rows, 2 * width),
+    }
+    local = pl.BlockSpec(memory_space=pltpu.VMEM)
+    placed = pl.pallas_call(
+        functools.partial(place_kernel, kinds),
+        out_shape=[
+            jax.ShapeDtypeStruct(shapes[kind](width), parts[0].dtype) for _, width, kind in kinds
+        ],
         grid_spec=pltpu.PrefetchScalarGridSpec(
             num_scalar_prefetch=1,
             grid=(),
-            in_specs=[pl.BlockSpec(memory_space=pl.ANY)] * 4,
-            out_specs=pl.BlockSpec(memory_space=pl.ANY),
-            scratch_shapes=[
-                pltpu.VMEM((4, half, rows, width), parts[0].dtype),
-                pltpu.SemaphoreType.DMA((4,)),
-                pltpu.SemaphoreType.DMA((4, half)),
-            ],
-        ),
-        compiler_params=pltpu.CompilerParams(vmem_limit_bytes=16 << 20),
+            in_specs=[local] * 4,
+            out_specs=[local] * len(kinds),
+        ),
+        compiler_params=pltpu.CompilerParams(vmem_limit_bytes=40 << 20),
         cost_estimate=pl.CostEstimate(
-            flops=0, bytes_accessed=8 * peers * rows * width, transcendentals=0
+            flops=0, bytes_accessed=8 * peers * rows * whole, transcendentals=0
         ),
         name="place",
     )(spots, *parts)
-
-
-def gather(mine, spots, peers, stacked):
-    buffer = mine[None]
-    steps = peers.bit_length() - 1
-    for step in range(steps - 1):
-        buffer = jnp.concatenate([buffer, shift(buffer, step, peers)], axis=0)
-    moved = shift(buffer, steps - 1, peers)
-    whole = place(spots, (buffer, moved, swap(buffer), swap(moved)), stacked)
-    if stacked:
-        return whole.reshape(2, -1, whole.shape[-1])
-    return whole.reshape(-1, whole.shape[-1])
-
-
-def fold_kernel(spots, own_a, far_a, own_b, far_b, keep, send):
-    keep[...] = (own_a[...].astype(jnp.float32) + far_a[...].astype(jnp.float32)).astype(keep.dtype)
-    send[...] = (own_b[...].astype(jnp.float32) + far_b[...].astype(jnp.float32)).astype(send.dtype)
+    results = []
+    for part, (_, width, kind), (_, _, asked) in zip(placed, kinds, plan):
+        if kind != asked:
+            part = part.reshape(2, peers, rows, 4, width // 4).transpose(1, 3, 2, 0, 4)
+            results.append(part.reshape(peers * rows * 4, width // 2))
+        elif kind == "stack":
+            results.append(part.reshape(2, peers * rows, width))
+        else:
+            results.append(part.reshape(-1, 2 * width))
+    return results
+
+
+class Gather:
+    def __init__(self, mine, spots, peers, plan):
+        self.kept = [mine[None]]
+        self.spots, self.peers, self.plan = spots, peers, plan
+        self.step, self.last = 0, peers.bit_length()
+
+    def launch(self):
+        if self.step < self.last - 1:
+            return [shift(self.kept[0], self.step, self.peers)]
+        return [swap(part) for part in self.kept]
+
+    def land(self, moved):
+        if self.step < self.last - 2:
+            self.kept = [jnp.concatenate([self.kept[0], moved[0]], axis=0)]
+        else:
+            self.kept = self.kept + moved
+        self.step += 1
+
+    def result(self):
+        return place(self.spots, self.kept, self.plan)
+
+
+class Scatter:
+    def __init__(self, far, own, spots, peers):
+        self.kept = [grads.reshape(peers, -1, grads.shape[1]) for grads in (own, far)]
+        self.spots, self.peers = spots, peers
+        self.step, self.last = 0, peers.bit_length()
+
+    def launch(self):
+        if self.step == 0:
+            return [swap(self.kept[1])]
+        return [shift(self.kept[1], self.last - 1 - self.step, self.peers)]
+
+    def land(self, moved):
+        if self.step == 0:
+            self.kept = list(fold(self.spots, self.kept[0], moved[0]))
+        else:
+            total = self.kept[0].astype(jnp.float32) + moved[0].astype(jnp.float32)
+            half = total.shape[0] // 2
+            low_sum = total.astype(jnp.bfloat16)
+            self.kept = [low_sum[:half], low_sum[half:]] if half else [low_sum]
+        self.step += 1
+
+    def result(self):
+        return self.kept[0][0]
+
+
+class Lanes:
+    def __init__(self):
+        self.flying = {}
+
+    def launch(self, *moves):
+        for move in moves:
+            if move.step < move.last:
+                self.flying[move] = move.launch()
+
+    def meet(self, work, *landing, ready=()):
+        moves = [move for move in landing if move in self.flying]
+        flown = [self.flying.pop(move) for move in moves]
+        waiting = [move.kept for move in ready]
+        work, flown, waiting = lax.optimization_barrier((work, flown, waiting))
+        for move, moved in zip(moves, flown):
+            move.land(moved)
+        for move, kept in zip(ready, waiting):
+            move.kept = kept
+        return work
+
+    def finish(self, work, *moves):
+        work = self.meet(work, *moves)
+        while any(move.step < move.last for move in moves):
+            self.launch(*moves)
+            work = self.meet(work, *moves)
+        return work
+
+
+def fold_kernel(spots, own, far, keep, send):
+    half = keep.shape[0]
+
+    def one_block(at, carry):
+        for out, spot in ((keep, spots[at]), (send, spots[half + at])):
+            out[at] = (own[spot].astype(jnp.float32) + far[spot].astype(jnp.float32)).astype(
+                out.dtype
+            )
+        return carry
+
+    lax.fori_loop(0, half, one_block, 0)
 
 
 def fold(spots, own, far):
     peers, rows, width = own.shape
-    half = peers // 2
-    near = pl.BlockSpec((1, rows, width), lambda at, spots: (spots[at], 0, 0))
-    apart = pl.BlockSpec((1, rows, width), lambda at, spots: (spots[at + half], 0, 0))
-    there = pl.BlockSpec((1, rows, width), lambda at, spots: (at, 0, 0))
-    shape = jax.ShapeDtypeStruct((half, rows, width), own.dtype)
+    shape = jax.ShapeDtypeStruct((peers // 2, rows, width), own.dtype)
+    local = pl.BlockSpec(memory_space=pltpu.VMEM)
     return pl.pallas_call(
         fold_kernel,
         out_shape=(shape, shape),
         grid_spec=pltpu.PrefetchScalarGridSpec(
-            num_scalar_prefetch=1,
-            grid=(half,),
-            in_specs=[near, near, apart, apart],
-            out_specs=[there, there],
-        ),
+            num_scalar_prefetch=1, grid=(), in_specs=[local, local], out_specs=[local, local]
+        ),
+        compiler_params=pltpu.CompilerParams(vmem_limit_bytes=32 << 20),
         cost_estimate=pl.CostEstimate(
             flops=peers * rows * width,
             bytes_accessed=6 * peers * rows * width,
             transcendentals=0,
         ),
         name="fold",
-    )(spots, own, far, own, far)
-
-
-def scatter(far, own, spots, peers):
-    def blocks(grads):
-        return grads.astype(jnp.bfloat16).reshape(peers, -1, grads.shape[1])
-
-    keep, send = fold(spots, blocks(own), swap(blocks(far)))
-    for step in range(peers.bit_length() - 2, -1, -1):
-        total = keep.astype(jnp.float32) + shift(send, step, peers).astype(jnp.float32)
-        half = total.shape[0] // 2
-        if step == 0:
-            return total[0].astype(jnp.bfloat16)
-        keep = total[:half].astype(jnp.bfloat16)
-        send = total[half:].astype(jnp.bfloat16)
+    )(spots, own, far)
 
 
 def both_sides(own, core):
@@ -589,56 +819,142 @@
     small_half = lax.dynamic_slice_in_dim(small_master.reshape(24, shard), core * 12, 12, 0)
     small_half = jnp.pad(small_half.astype(jnp.bfloat16).T, ((0, 0), (0, LANES - 12)))
     wide = attn_half.shape[2]
-    first_piece = gather(
-        jnp.concatenate([attn_half[0], small_half], axis=1), spots, peers, True
-    )
-    up_low, down_low = [None, None], [None, None]
-    up_low[0] = gather(half_of(up_master[0], core).astype(jnp.bfloat16), spots, peers, False)
-    down_low[0] = gather(half_of(down_master[0], core).astype(jnp.bfloat16), spots, peers, False)
-    attn_low = [first_piece[:, :, :wide], gather(attn_half[1], spots, peers, True)]
-    up_low[1] = gather(half_of(up_master[1], core).astype(jnp.bfloat16), spots, peers, False)
-    down_low[1] = gather(half_of(down_master[1], core).astype(jnp.bfloat16), spots, peers, False)
-    small_vals = first_piece[:, :, wide : wide + 12].transpose(0, 2, 1).astype(jnp.float32)
+    lanes = Lanes()
+    third = model_width // 2
+    hidden_half = up_master.shape[2] // 2
+
+    def down_half(layer):
+        half = half_of(down_master[layer], core).astype(jnp.bfloat16)
+        return [half[part * shard : (part + 1) * shard] for part in range(4)]
+
+    up_half = [half_of(up_master[layer], core).astype(jnp.bfloat16) for layer in range(2)]
+    in_one = Gather(
+        jnp.concatenate([attn_half[0, :, : 3 * third], small_half], axis=1),
+        spots,
+        peers,
+        [(0, 3 * third, "stack"), (3 * third, LANES, "stack")],
+    )
+    out_up_one = Gather(
+        jnp.concatenate([attn_half[0, :, 3 * third :], up_half[0]], axis=1),
+        spots,
+        peers,
+        [(0, third, "wide"), (third, hidden_half, "wide")],
+    )
+    down_one = Gather(
+        jnp.concatenate(down_half(0), axis=1), spots, peers, [(0, third, "down")]
+    )
+    attn_two = Gather(
+        attn_half[1], spots, peers, [(0, 3 * third, "stack"), (3 * third, third, "wide")]
+    )
+    feed_two = Gather(
+        jnp.concatenate([up_half[1]] + down_half(1), axis=1),
+        spots,
+        peers,
+        [(0, hidden_half, "wide"), (hidden_half, third, "down")],
+    )
     flat_low = tokens.reshape(rows_total, model_width)
-    attended_one, kept_attend_one = attend_forward(
-        flat_low.astype(jnp.float32), flat_low, attn_low[0], small_vals[0], seq_lengths
-    )
-    layer_one, kept_feed_one = feed_forward(attended_one, up_low[0], down_low[0], small_vals[0])
-    attended_two, kept_attend_two = attend_forward(
-        layer_one, layer_one.astype(jnp.bfloat16), attn_low[1], small_vals[1], seq_lengths
-    )
-    cot_flat = cotangent.reshape(rows_total, model_width).astype(jnp.float32)
+    cot_flat = cotangent.reshape(rows_total, model_width)
     select_rows = row_select(token_mask, MCAP)
+    flat_mask = token_mask.reshape(-1, 1) == 1
+
+    lanes.launch(in_one)
+    lanes.meet((), in_one)
+    lanes.launch(in_one)
+    lanes.meet((), in_one, ready=(out_up_one,))
+    lanes.launch(in_one, out_up_one)
+    lanes.meet((), in_one, out_up_one)
+    lanes.launch(in_one, out_up_one)
+    lanes.meet((), in_one, out_up_one, ready=(down_one,))
+    lanes.launch(in_one, out_up_one, down_one)
+    lanes.finish((), in_one)
+    first = in_one.result()
+    (w_in_one, small_rows), = lanes.meet((first,), out_up_one, down_one, ready=(attn_two,))
+    small_vals = small_rows[:, :, :12].transpose(0, 2, 1).astype(jnp.float32)
+    lanes.launch(out_up_one, down_one, attn_two)
+    qkv_one = project_in(flat_low, w_in_one, small_vals[0])
+    seqs = seq_lengths.shape[0]
+    attended = attend_core(qkv_one[0], qkv_one[1], seq_lengths, 0)
+    attended = lanes.meet(attended, out_up_one, down_one, attn_two, ready=(feed_two,))
+    lanes.launch(out_up_one, down_one, attn_two)
+    for seq in range(1, seqs):
+        attended = attend_core(qkv_one[0], qkv_one[1], seq_lengths, seq, attended)
+    attended = lanes.meet(attended, out_up_one, down_one, attn_two)
+    mixed_one, lse_one = lanes.finish(attended, out_up_one)
+    lanes.launch(down_one, feed_two)
+    w_out_one, w_up_one = out_up_one.result()
+    attended_one = project_out(flat_low.astype(jnp.float32), mixed_one, w_out_one, small_vals[0])
+    attended_one, attn_xhat_one, attn_inv_one = lanes.meet(attended_one, down_one)
+    lanes.launch(down_one, attn_two)
+    act_one = feed_up(attended_one, w_up_one, small_vals[0])
+    act_one = lanes.meet(act_one, down_one, attn_two, feed_two)
+    low_one, act_one, slope_one = lanes.finish(act_one, down_one)
+    lanes.launch(attn_two, feed_two)
+    (w_down_one,) = down_one.result()
+    layer_one = feed_down(attended_one, act_one, w_down_one, small_vals[0])
+    layer_one = lanes.meet(layer_one, attn_two, feed_two)
+    lanes.launch(attn_two, feed_two)
+    layer_one, feed_xhat_one, feed_inv_one = lanes.finish(layer_one, attn_two)
+    w_in_two, w_out_two = attn_two.result()
+    layer_low = layer_one.astype(jnp.bfloat16)
+    qkv_two = project_in(layer_low, w_in_two, small_vals[1])
+    attended = attend_core(qkv_two[0], qkv_two[1], seq_lengths, 0)
+    attended = lanes.meet(attended, feed_two)
+    lanes.launch(feed_two)
+    for seq in range(1, seqs):
+        attended = attend_core(qkv_two[0], qkv_two[1], seq_lengths, seq, attended)
+    mixed_two, lse_two = attended
+    attended_two = project_out(layer_one, mixed_two, w_out_two, small_vals[1])
+    attended_two = lanes.meet((attended_two, mixed_two, lse_two), feed_two)
+    (attended_two, attn_xhat_two, attn_inv_two), mixed_two, lse_two = attended_two
+    lanes.launch(feed_two)
     rows_in = join_low(forward_product(select_rows, split_low(attended_two, 3)), 3)
-    d_rows_out = forward_product(select_rows, cotangent.reshape(rows_total, model_width))
-    out_rows, kept_feed_two = feed_forward(rows_in, up_low[1], down_low[1], small_vals[1])
-    d_in_rows, d_up_two, d_down_two, feed_small_two = feed_backward(
-        d_rows_out, kept_feed_two, up_low[1], down_low[1], small_vals[1], core
-    )
-    flat_mask = token_mask.reshape(-1, 1) == 1
-    output_flat = jnp.where(
+    d_rows_out = forward_product(select_rows, cot_flat)
+    rows_in = lanes.finish(rows_in, feed_two)
+    w_up_two, w_down_two = feed_two.result()
+    rows_low, act_two, slope_two = feed_up(rows_in, w_up_two, small_vals[1])
+    out_rows, feed_xhat_two, feed_inv_two = feed_down(rows_in, act_two, w_down_two, small_vals[1])
+    d_resid, d_branch, d_pre, feed_small_two = feed_down_back(
+        d_rows_out, feed_xhat_two, feed_inv_two, slope_two, w_down_two, small_vals[1]
+    )
+    grads = feed_grads(core, rows_low, d_pre, act_two, d_branch, shard)
+    grads, d_resid, d_pre = lanes.meet((grads, d_resid, d_pre))
+    g_feed_two = Scatter(*grads, spots, peers)
+    lanes.launch(g_feed_two)
+    d_in_rows = d_resid + back_product(d_pre, w_up_two)
+    d_attended_two = jnp.where(
         flat_mask,
-        weight_grad(select_rows, out_rows.astype(jnp.bfloat16)),
-        attended_two,
-    )
-    d_attended_two = jnp.where(
-        flat_mask, join_low(weight_grad(select_rows, split_low(d_in_rows, 2)), 2), cot_flat
-    )
-    owned = {}
-    owned["up1"] = scatter(*d_up_two, spots, peers)
-    owned["down1"] = scatter(*d_down_two, spots, peers)
-    d_layer_one, own_attn, far_attn, attn_small_two = attend_backward(
-        d_attended_two, kept_attend_two, attn_low[1], small_vals[1], seq_lengths, core
-    )
-    owned["attn1"] = scatter(far_attn, own_attn, spots, peers)
-    d_attended_one, d_up_one, d_down_one, feed_small_one = feed_backward(
-        d_layer_one, kept_feed_one, up_low[0], down_low[0], small_vals[0], core
-    )
-    owned["down0"] = scatter(*d_down_one, spots, peers)
-    owned["up0"] = scatter(*d_up_one, spots, peers)
-    d_tokens, own_attn, far_attn, attn_small_one = attend_backward(
-        d_attended_one, kept_attend_one, attn_low[0], small_vals[0], seq_lengths, core
-    )
+        join_low(weight_grad(select_rows, split_low(d_in_rows, 2)), 2),
+        cot_flat.astype(jnp.float32),
+    )
+    back = project_out_back(d_attended_two, attn_xhat_two, attn_inv_two, w_out_two, small_vals[1])
+    d_resid, d_branch, d_mixed, sums_out = lanes.meet(back, g_feed_two)
+    lanes.launch(g_feed_two)
+    d_qkv = attend_core_back(qkv_two[0], qkv_two[1], d_mixed, lse_two, seq_lengths)
+    d_qkv = lanes.meet(d_qkv, g_feed_two)
+    lanes.launch(g_feed_two)
+    grads = attn_grads(core, layer_low, mixed_two, d_qkv, d_branch)
+    d_layer_one = project_in_back(d_resid, d_qkv, w_in_two)
+    attn_small_two = attn_small(d_qkv, sums_out)
+    grads, d_layer_one = lanes.meet((grads, d_layer_one), g_feed_two)
+    g_attn_two = Scatter(*grads, spots, peers)
+    lanes.launch(g_attn_two, g_feed_two)
+    back = feed_down_back(
+        d_layer_one, feed_xhat_one, feed_inv_one, slope_one, w_down_one, small_vals[0]
+    )
+    d_resid, d_branch, d_pre, feed_small_one = lanes.meet(back, g_attn_two, g_feed_two)
+    lanes.launch(g_attn_two, g_feed_two)
+    grads = feed_grads(core, low_one, d_pre, act_one, d_branch, shard)
+    grads = lanes.meet(grads, g_attn_two, g_feed_two)
+    g_feed_one = Scatter(*grads, spots, peers)
+    lanes.launch(g_feed_one, g_attn_two)
+    d_attended_one = d_resid + back_product(d_pre, w_up_one)
+    back = project_out_back(d_attended_one, attn_xhat_one, attn_inv_one, w_out_one, small_vals[0])
+    d_resid, d_branch, d_mixed, sums_out = lanes.meet(back, g_feed_one, g_attn_two)
+    lanes.launch(g_feed_one, g_attn_two)
+    d_qkv = attend_core_back(qkv_one[0], qkv_one[1], d_mixed, lse_one, seq_lengths)
+    d_qkv = lanes.meet(d_qkv, g_feed_one, g_attn_two)
+    lanes.launch(g_feed_one, g_attn_two)
+    attn_small_one = attn_small(d_qkv, sums_out)
     small_grads = jnp.stack(
         [
             jnp.concatenate([attn_small_one, feed_small_one], axis=0),
@@ -646,29 +962,56 @@
         ]
     )
 
-    def with_small(grads, side):
-        picked = lax.dynamic_index_in_dim(small_grads, side, 0, False).T
-        picked = jnp.pad(picked, ((0, 0), (0, LANES - 12)))
-        return jnp.concatenate([grads, picked], axis=1)
-
-    owned["attn0"] = scatter(
-        with_small(far_attn, 1 - core), with_small(own_attn, core), spots, peers
-    )
+    small_cols = jnp.pad(
+        small_grads.astype(jnp.bfloat16).transpose(0, 2, 1), ((0, 0), (0, 0), (0, LANES - 12))
+    )
+    grads = attn_grads(core, flat_low, mixed_one, d_qkv, d_branch, small_cols)
+    grads, d_resid, d_qkv = lanes.meet((grads, d_resid, d_qkv), g_feed_one, g_attn_two)
+    g_attn_one = Scatter(*grads, spots, peers)
+    lanes.launch(g_attn_one, g_feed_one)
+    d_tokens = project_in_back(d_resid, d_qkv, w_in_one).astype(jnp.bfloat16)
+    d_tokens = lanes.meet(d_tokens, g_attn_one)
+    lanes.launch(g_attn_one)
+    output_flat = jnp.where(
+        flat_mask,
+        weight_grad(select_rows, out_rows.astype(jnp.bfloat16)),
+        attended_two,
+    ).astype(jnp.bfloat16)
+    output_flat = lanes.meet(output_flat, g_attn_one, g_feed_one)
+    lanes.launch(g_attn_one, g_feed_one)
+    lanes.meet((), g_attn_one)
+    lanes.launch(g_attn_one)
+    lanes.meet((), g_attn_one, g_feed_one)
+    lanes.finish((), g_attn_one, g_feed_one, g_attn_two, g_feed_two)
+    owned = {
+        "attn0": g_attn_one.result(),
+        "feed0": g_feed_one.result(),
+        "attn1": g_attn_two.result(),
+        "feed1": g_feed_two.result(),
+    }
     partial_squares = sum(jnp.sum(jnp.square(owned[name].astype(jnp.float32))) for name in owned)
+    both = {name: both_sides(owned[name], core) for name in owned}
     square_total = sum_all(partial_squares, peers)
-    both = {name: both_sides(owned[name], core) for name in owned}
-
-    def attn_rows(name):
-        sides = jnp.stack([part[:, :wide] for part in both[name]])
-        return sides.reshape(2, shard, 4, -1).transpose(2, 1, 0, 3).reshape(4, shard, model_width)
-
-    def wide_rows(name):
-        return jnp.concatenate(both[name], axis=1)
+
+    def joined(name, start, width):
+        return jnp.concatenate([part[:, start : start + width] for part in both[name]], axis=1)
+
+    def down_rows(name):
+        return jnp.concatenate(
+            [joined(name, hidden_half + part * third, third) for part in range(4)], axis=0
+        )
 
     reduced = (
-        jnp.stack([attn_rows("attn0"), attn_rows("attn1")]).astype(jnp.float32),
-        jnp.stack([wide_rows("up0"), wide_rows("up1")]).astype(jnp.float32),
-        jnp.stack([wide_rows("down0"), wide_rows("down1")]).astype(jnp.float32),
+        jnp.stack(
+            [
+                jnp.stack([joined(name, part * third, third) for part in range(4)])
+                for name in ("attn0", "attn1")
+            ]
+        ).astype(jnp.float32),
+        jnp.stack([joined(name, 0, hidden_half) for name in ("feed0", "feed1")]).astype(
+            jnp.float32
+        ),
+        jnp.stack([down_rows(name) for name in ("feed0", "feed1")]).astype(jnp.float32),
         jnp.stack([part[:, wide : wide + 12].T for part in both["attn0"]]).astype(jnp.float32),
     )
     grad_norm = jnp.sqrt(square_total).reshape(1)
@@ -700,8 +1043,8 @@
     small_new = adam_update(
         small_master, small_first, small_second, reduced[3], clip_scale, step_value, 0.0, SMALL_RATE
     )
-    output = output_flat.reshape(seq_count, length, model_width).astype(jnp.bfloat16)
-    input_grad = d_tokens.reshape(seq_count, length, model_width).astype(jnp.bfloat16)
+    output = output_flat.reshape(seq_count, length, model_width)
+    input_grad = d_tokens.reshape(seq_count, length, model_width)
     return (output, input_grad, grad_norm) + attn_new + up_new + down_new + small_new
 
 

time: 844 us -> 569 us (0.67)
  waiting for transfers between devices: 259 us -> 112 us
  matrix products: 190 us -> 69.1 us
  starting transfers between devices: 75 us -> 63.5 us
  Pallas kernels: 174 us -> 184 us
  local copies, waits for them, and re-layouts: 57.5 us -> 47.7 us
    ppermute x48 -> x36, waiting for transfers between devices: 255 us -> 109 us  [shift(): return lax.ppermute(value, ('dp', 'bal'), pairs)]
    dot_general x18 -> x2, matrix products: 69.6 us -> 6.22 us  [weight_grad(): lax.dot_general(left_side, right_side, (((0,), (0,)), ((), ())), preferre...]
    dot_general x15 -> x11, matrix products: 74 us -> 29 us  [forward_product(): return jnp.dot(left_side, right_side, preferred_element_type=jnp.float32)]
    pallas_call x8 -> x15, Pallas kernels: 76.2 us -> 119 us  [the longest x4 48.6 us: attend_core(): pl.pallas_call(kernel, out_shape=(jax.ShapeDtypeStruct((total, width), jn...]
    pallas_call x6 -> x4, Pallas kernels: 42.7 us -> 10.1 us  [fold(): pl.pallas_call(fold_kernel, out_shape=(shape, shape), grid_spec=pltpu.Pre...]
    dot_general x12 -> x10, matrix products: 46.5 us -> 33.9 us  [back_product(): lax.dot_general(left_side, right_side, (((1,), (1,)), ((), ())), preferre...]
    concatenate x22 -> x13, other arithmetic: 12.4 us -> 2.28 us  [the longest x11 1.64 us: land(): self.kept = [jnp.concatenate([self.kept[0], moved[0]], axis=0)]]
    convert_element_type x3 -> x17, other arithmetic: 1.47 us -> 11.3 us  [the longest x12 8.36 us: land(): low_sum = total.astype(jnp.bfloat16)]
  transfers between devices with their start and end apart: 79 -> 61, of which waited for: 31 -> 24; matrix products, arithmetic and copies ran while one was open for 9% -> 23% of each run, Pallas kernels for 8% -> 28%
where the time goes in v3:
time: 569 us; the launch traced here: 558 us
  Pallas kernels  184 us (32%)
  waiting for transfers between devices  112 us (20%)
  other arithmetic  69.6 us (12%)
  matrix products  69.1 us (12%)
  starting transfers between devices  63.5 us (11%)
  local copies, waits for them, and re-layouts  47.7 us (8%)
  between operations  12.3 us (2%)
    ppermute x36, waiting for transfers between devices, shift(): return lax.ppermute(value, ('dp', 'bal'), pairs)  109 us
    pallas_call x2, Pallas kernels, attend_core_back(): pl.pallas_call(attend_back_kernel, out_shape=jax.ShapeDtypeStruct((2, tot...  54.6 us
    pallas_call x4, Pallas kernels, attend_core(): pl.pallas_call(kernel, out_shape=(jax.ShapeDtypeStruct((total, width), jn...  48.6 us
    ppermute x36, starting transfers between devices, shift(): return lax.ppermute(value, ('dp', 'bal'), pairs)  43 us
    dot_general x10, matrix products, back_product(): lax.dot_general(left_side, right_side, (((1,), (1,)), ((), ())), preferre...  33.9 us
    dot_general x11, matrix products, forward_product(): return jnp.dot(left_side, right_side, preferred_element_type=jnp.float32)  29 us
    pallas_call x2, Pallas kernels, feed_grads(): pl.pallas_call(functools.partial(feed_grads_kernel, shard), out_shape=(sh...  27.8 us
    unnamed x287, local copies, waits for them, and re-layouts  26.3 us
  transfers between devices with their start and end apart: 61, of which 24 were waited for; matrix products, arithmetic and copies ran while one was open for 23% of the time, Pallas kernels for 28%

profile of v3, /device:TPU:0, one launch (start us, length us, event | category | flops | bytes accessed | tf_op | source)
XLA Modules:
  0.0 558.4 jit_solution(5339721466591600327)
XLA Ops:
  14.5 6.4 %collective-permute-done.1 = bf16[2,48,1280]{2,1,0:T(8,128)(2,1)S(1)} collective-permute-done((bf16[2,48,1280]{2,1,0:T(8,128)(2,1)S(1)}, bf16[2,48,1280]{2,1,0:T(8,128)(2,1)S(1)}, u32[]{:S(2)}, u32[]{:S(2)}) %collective-permute-start.1) | collective-permute-done | bytes 245792 | tf_op jit(solution)/shard_map/ppermute | solution.py:573
  25.8 7.9 %collective-permute-done.3 = bf16[1,48,1920]{2,1,0:T(8,128)(2,1)S(1)} collective-permute-done((bf16[1,48,1920]{2,1,0:T(8,128)(2,1)S(1)}, bf16[1,48,1920]{2,1,0:T(8,128)(2,1)S(1)}, u32[]{:S(2)}, u32[]{:S(2)}) %collective-permute-start.3) | collective-permute-done | bytes 184352 | tf_op jit(solution)/shard_map/ppermute | solution.py:573
  35.8 9.6 %collective-permute-done.5 = bf16[2,48,1920]{2,1,0:T(8,128)(2,1)S(1)} collective-permute-done((bf16[2,48,1920]{2,1,0:T(8,128)(2,1)S(1)}, bf16[2,48,1920]{2,1,0:T(8,128)(2,1)S(1)}, u32[]{:S(2)}, u32[]{:S(2)}) %collective-permute-start.5) | collective-permute-done | bytes 368672 | tf_op jit(solution)/shard_map/ppermute | solution.py:573
  74.1 12.0 %attend.4 = (bf16[1024,768]{1,0:T(8,128)(2,1)S(1)}, f32[2,16,512]{2,1,0:T(8,128)S(1)}) custom-call(s32[2]{0:T(128)S(1)} %copy-done.21, bf16[1024,1152]{1,0:T(8,128)(2,1)S(1)} %fusion.7.lo_ref.qkv_lo, bf16[1024,1152]{1,0:T(8,128)(2,1)S(1)} %fusion.8.hi_ref.qkv_hi), custom_call_target="tpu_custom_call" | custom-call | flops 3221225472 | bytes 3145728 | tf_op jit(solution)/shard_map/attend/pallas_call | solution.py:143
  88.8 12.0 %attend.5 = (bf16[1024,768]{1,0:T(8,128)(2,1)S(1)}, f32[2,16,512]{2,1,0:T(8,128)S(1)}) custom-call(s32[2]{0:T(128)S(1)} %copy-done.21, bf16[1024,1152]{1,0:T(8,128)(2,1)S(1)} %fusion.7.lo_ref.qkv_lo, bf16[1024,1152]{1,0:T(8,128)(2,1)S(1)} %fusion.8.hi_ref.qkv_hi, ...), custom_call_target="tpu_custom_call", output_to_operand_aliasing={{0}: (3, {}), {1}: (4, {})} | custom-call | flops 3221225472 | bytes 3145728 | tf_op jit(solution)/shard_map/attend/pallas_call | solution.py:143
  110.1 7.3 %collective-permute-done.17.refs_1_ = bf16[8,48,1536]{2,1,0:T(8,128)(2,1)S(1)} collective-permute-done((bf16[8,48,1536]{2,1,0:T(8,128)(2,1)S(1)}, bf16[8,48,1536]{2,1,0:T(8,128)(2,1)S(1)}, u32[]{:S(2)}, u32[]{:S(2)}) %collective-permute-start.17) | collective-permute-done | bytes 1179680 | tf_op jit(solution)/shard_map/ppermute | solution.py:573
  120.6 10.6 %feed_up.2 = (bf16[1024,3072]{1,0:T(8,128)(2,1)S(1)}, bf16[1024,3072]{1,0:T(8,128)(2,1)S(1)}) custom-call(bf16[1024,768]{1,0:T(8,128)(2,1)S(1)} %convert_element_type.363.rows_ref.low_ref, bf16[768,3072]{1,0:T(8,128)(2,1)S(1)} %bitcast.249, f32[1,3072]{1,0:T(1,128)S(1)} %bitcast.248), custom_call_target="tpu_custom_call" | custom-call | flops 4831838208 | bytes 17301504 | tf_op jit(solution)/shard_map/feed_up/pallas_call | solution.py:387
  140.0 8.8 %fusion.107 = (f32[1024]{0:T(1024)S(1)}, f32[1024,768]{1,0:T(8,128)S(1)}) fusion(f32[1024,768]{1,0:T(8,128)} %copy-done.43, f32[768]{0:T(1024)S(1)} %get-tuple-element.383, bf16[1024,3072]{1,0:T(8,128)(2,1)S(1)} %bitcast.267, bf16[3072,768]{1,0:T(8,128)(2,1)S(1)} %bitcast.234), kind=kOutput, calls=%fused_computation.325 | convolution fusion | flops 4834196480 | bytes 17308672 | tf_op jit(solution)/shard_map/dot_general | solution.py:32
  163.4 12.0 %attend.6 = (bf16[1024,768]{1,0:T(8,128)(2,1)S(1)}, f32[2,16,512]{2,1,0:T(8,128)S(1)}) custom-call(s32[2]{0:T(128)S(1)} %copy-done.21, bf16[1024,1152]{1,0:T(8,128)(2,1)S(1)} %add_convert_fusion.3.lo_ref.qkv_lo, bf16[1024,1152]{1,0:T(8,128)(2,1)S(1)} %add_convert_fusion.2.hi_ref.qkv_hi), custom_call_target="tpu_custom_call" | custom-call | flops 3221225472 | bytes 3145728 | tf_op jit(solution)/shard_map/attend/pallas_call | solution.py:143
  176.8 12.4 %attend.7 = (bf16[1024,768]{1,0:T(8,128)(2,1)S(1)}, f32[2,16,512]{2,1,0:T(8,128)S(1)}) custom-call(s32[2]{0:T(128)S(1)} %copy-done.21, bf16[1024,1152]{1,0:T(8,128)(2,1)S(1)} %add_convert_fusion.3.lo_ref.qkv_lo, bf16[1024,1152]{1,0:T(8,128)(2,1)S(1)} %add_convert_fusion.2.hi_ref.qkv_hi, ...), custom_call_target="tpu_custom_call", output_to_operand_aliasing={{0}: (3, {}), {1}: (4, {})} | custom-call | flops 3221225472 | bytes 3145728 | tf_op jit(solution)/shard_map/attend/pallas_call | solution.py:143
  194.6 9.9 %collective-permute-done.27.refs_1_ = bf16[8,48,3072]{2,1,0:T(8,128)(2,1)} collective-permute-done((bf16[8,48,3072]{2,1,0:T(8,128)(2,1)S(1)}, bf16[8,48,3072]{2,1,0:T(8,128)(2,1)}, u32[]{:S(2)}, u32[]{:S(2)}) %collective-permute-start.27) | collective-permute-done | bytes 2359328 | tf_op jit(solution)/shard_map/ppermute | solution.py:573
  212.5 6.8 %place.9 = (bf16[16,48,3072]{2,1,0:T(8,128)(2,1)S(1)}, bf16[16,192,768]{2,1,0:T(8,128)(2,1)}) custom-call(s32[33]{0:T(128)S(1)} %pad_add_fusion.spots, bf16[8,48,3072]{2,1,0:T(8,128)(2,1)S(1)} %constant_dynamic-update-slice_fusion.16.refs_0_, bf16[8,48,3072]{2,1,0:T(8,128)(2,1)} %collective-permute-done.27.refs_1_, ...), custom_call_target="tpu_custom_call" | custom-call | bytes 18874368 | tf_op jit(solution)/shard_map/place/pallas_call | solution.py:632
  231.2 11.4 %feed_grads.2 = (bf16[768,3072]{1,0:T(8,128)(2,1)}, bf16[768,3072]{1,0:T(8,128)(2,1)}) custom-call(s32[1]{0:T(128)} %bitcast.4.core, bf16[384,768]{1,0:T(8,128)(2,1)S(1)} %convert_element_type.370.rows_ref.low_ref, bf16[384,3072]{1,0:T(8,128)(2,1)S(1)} %get-tuple-element.250.d_pre_ref, bf16[384,3072]{1,0:T(8,128)(2,1)S(1)} %get-tuple-element.240.act_ref, ...), custom_call_target="tpu_custom_call" | custom-call | flops 3623878656 | bytes 18874368 | tf_op jit(solution)/shard_map/feed_grads/pallas_call | solution.py:484
  256.8 27.3 %attend_back.2.d_qkv_ref = bf16[2,1024,1152]{2,1,0:T(8,128)(2,1)S(1)} custom-call(s32[2]{0:T(128)S(1)} %copy-done.21, bf16[1024,1152]{1,0:T(8,128)(2,1)S(1)} %copy-done.31, bf16[1024,1152]{1,0:T(8,128)(2,1)S(1)} %copy-done.29, bf16[1024,768]{1,0:T(8,128)(2,1)S(1)} %convolution_convert_fusion.1.d_mixed_ref, f32[2,16,512]{2,1,0:T(8,128)S(1)} %copy-done.39), custom_call_target="tpu_custom_call" | custom-call | flops 16106127360 | bytes 11010048 | tf_op jit(solution)/shard_map/attend_back/pallas_call | solution.py:231
  289.9 8.1 %attn_grads.2 = (bf16[768,1536]{1,0:T(8,128)(2,1)}, bf16[768,1536]{1,0:T(8,128)(2,1)S(1)}) custom-call(s32[1]{0:T(128)} %bitcast.4.core, bf16[1024,768]{1,0:T(8,128)(2,1)S(1)} %copy-done.12, bf16[1024,768]{1,0:T(8,128)(2,1)S(1)} %copy-done.23, bf16[2,1024,1152]{2,1,0:T(8,128)(2,1)S(1)} %attend_back.2.d_qkv_ref, ...), custom_call_target="tpu_custom_call" | custom-call | flops 4831838208 | bytes 17301504 | tf_op jit(solution)/shard_map/attn_grads/pallas_call | solution.py:349
  311.7 7.1 %convert_reduce_fusion = (bf16[3072]{0:T(1024)(128)(2,1)S(1)}, bf16[1024,3072]{1,0:T(8,128)(2,1)}) fusion(bf16[1024,3072]{1,0:T(8,128)(2,1)S(1)} %bitcast.269, bf16[1024,768]{1,0:T(8,128)(2,1)S(1)} %get-tuple-element.274.d_branch_ref, bf16[3072,768]{1,0:T(8,128)(2,1)S(1)} %bitcast.237), kind=kOutput, calls=%fused_computation | convolution fusion | flops 4847563776 | bytes 18880512 | tf_op jit(solution)/shard_map/dot_general | solution.py:42
  332.7 16.4 %feed_grads.3 = (bf16[768,3072]{1,0:T(8,128)(2,1)}, bf16[768,3072]{1,0:T(8,128)(2,1)S(1)}) custom-call(s32[1]{0:T(128)} %bitcast.4.core, bf16[1024,768]{1,0:T(8,128)(2,1)S(1)} %copy-done.10, bf16[1024,3072]{1,0:T(8,128)(2,1)} %get-tuple-element.271.d_pre_ref, bf16[1024,3072]{1,0:T(8,128)(2,1)} %copy-done.34, bf16[1024,768]{1,0:T(8,128)(2,1)S(1)} %copy-done.8), custom_call_target="tpu_custom_call" | custom-call | flops 9663676416 | bytes 34603008 | tf_op jit(solution)/shard_map/feed_grads/pallas_call | solution.py:484
  365.9 8.7 %fusion.111 = f32[1024,768]{1,0:T(8,128)S(1)} fusion(bf16[1024,3072]{1,0:T(8,128)(2,1)} %get-tuple-element.271.d_pre_ref, bf16[768,3072]{1,0:T(8,128)(2,1)} %bitcast.250), kind=kOutput, calls=%fused_computation.329 | convolution fusion | flops 4831838208 | bytes 14155776 | tf_op jit(solution)/shard_map/dot_general | solution.py:42
  396.2 27.3 %attend_back.3.d_qkv_ref = bf16[2,1024,1152]{2,1,0:T(8,128)(2,1)S(1)} custom-call(s32[2]{0:T(128)S(1)} %copy-done.21, bf16[1024,1152]{1,0:T(8,128)(2,1)S(1)} %copy-done.27, bf16[1024,1152]{1,0:T(8,128)(2,1)S(1)} %copy-done.25, bf16[1024,768]{1,0:T(8,128)(2,1)S(1)} %convolution_convert_fusion.d_mixed_ref, f32[2,16,512]{2,1,0:T(8,128)S(1)} %copy-done.37), custom_call_target="tpu_custom_call" | custom-call | flops 16106127360 | bytes 11010048 | tf_op jit(solution)/shard_map/attend_back/pallas_call | solution.py:231
  441.0 6.5 %attn_grads.3 = (bf16[768,1664]{1,0:T(8,128)(2,1)S(1)}, bf16[768,1664]{1,0:T(8,128)(2,1)S(1)}) custom-call(s32[1]{0:T(128)} %bitcast.4.core, bf16[1024,768]{1,0:T(8,128)(2,1)S(1)} %bitcast.261, bf16[1024,768]{1,0:T(8,128)(2,1)S(1)} %copy-done.33, bf16[2,1024,1152]{2,1,0:T(8,128)(2,1)S(1)} %copy-done.4, bf16[1024,768]{1,0:T(8,128)(2,1)S(1)} %copy-done.6, ...), custom_call_target="tpu_custom_call" | custom-call | flops 4831838208 | bytes 17301504 | tf_op jit(solution)/shard_map/attn_grads/pallas_call | solution.py:349
  464.1 14.4 %collective-permute-done.45 = bf16[2,48,3072]{2,1,0:T(8,128)(2,1)S(1)} collective-permute-done((bf16[2,48,3072]{2,1,0:T(8,128)(2,1)S(1)}, bf16[2,48,3072]{2,1,0:T(8,128)(2,1)S(1)}, u32[]{:S(2)}, u32[]{:S(2)}) %collective-permute-start.45) | collective-permute-done | bytes 589856 | tf_op jit(solution)/shard_map/ppermute | solution.py:573
  481.1 8.3 %collective-permute-done.46 = bf16[4,48,1664]{2,1,0:T(8,128)(2,1)S(1)} collective-permute-done((bf16[4,48,1664]{2,1,0:T(8,128)(2,1)S(1)}, bf16[4,48,1664]{2,1,0:T(8,128)(2,1)S(1)}, u32[]{:S(2)}, u32[]{:S(2)}) %collective-permute-start.46) | collective-permute-done | bytes 639008 | tf_op jit(solution)/shard_map/ppermute | solution.py:573
  494.7 6.7 %collective-permute-done.47 = bf16[2,48,1664]{2,1,0:T(8,128)(2,1)S(1)} collective-permute-done((bf16[2,48,1664]{2,1,0:T(8,128)(2,1)S(1)}, bf16[2,48,1664]{2,1,0:T(8,128)(2,1)S(1)}, u32[]{:S(2)}, u32[]{:S(2)}) %collective-permute-start.47) | collective-permute-done | bytes 319520 | tf_op jit(solution)/shard_map/ppermute | solution.py:573
  503.8 7.1 %collective-permute-done.49 = bf16[1,48,1664]{2,1,0:T(8,128)(2,1)S(1)} collective-permute-done((bf16[1,48,1664]{2,1,0:T(8,128)(2,1)S(1)}, bf16[1,48,1664]{2,1,0:T(8,128)(2,1)S(1)}, u32[]{:S(2)}, u32[]{:S(2)}) %collective-permute-start.49) | collective-permute-done | bytes 159776 | tf_op jit(solution)/shard_map/ppermute | solution.py:573
  (606 shorter events, 280.6 us)
Async XLA Ops:
  59.7 41.1 %collective-permute-start.13 = (bf16[8,48,1920]{2,1,0:T(8,128)(2,1)S(1)}, bf16[8,48,1920]{2,1,0:T(8,128)(2,1)}, u32[]{:S(2)}, u32[]{:S(2)}) collective-permute-start(bf16[8,48,1920]{2,1,0:T(8,128)(2,1)S(1)} %constant_dynamic-update-slice_fusion.refs_0_), channel_id=1, source_target_pairs={{0,16},{16,0},{1,17},{17,1},{2,18},{18,2},{3,19},{19,3},{4,20},{20... | collective-permute-start | bytes 4423688 | tf_op jit(solution)/shard_map/ppermute | solution.py:577
  59.8 26.4 %collective-permute-start.10 = (bf16[8,48,1920]{2,1,0:T(8,128)(2,1)S(1)}, bf16[8,48,1920]{2,1,0:T(8,128)(2,1)}, u32[]{:S(2)}, u32[]{:S(2)}) collective-permute-start(bf16[8,48,1920]{2,1,0:T(8,128)(2,1)S(1)} %constant_dynamic-update-slice_fusion.refs_0_), channel_id=1, source_target_pairs={{0,1},{1,0},{2,3},{3,2},{4,5},{5,4},{6,7},{7,6},{8,9},{9,8},{10,11... | collective-permute-start | bytes 4423688 | tf_op jit(solution)/shard_map/ppermute | solution.py:573
  62.8 23.3 %collective-permute-start.12 = (bf16[1,48,1536]{2,1,0:T(8,128)(2,1)S(1)}, bf16[1,48,1536]{2,1,0:T(8,128)(2,1)S(1)}, u32[]{:S(2)}, u32[]{:S(2)}) collective-permute-start(bf16[1,48,1536]{2,1,0:T(8,128)(2,1)S(1)} %bitcast.274), channel_id=1, source_target_pairs={{0,8},{1,9},{2,10},{3,11},{4,12},{5,13},{6,14},{7,15},{8,0},{9,1},... | collective-permute-start | bytes 442376 | tf_op jit(solution)/shard_map/ppermute | solution.py:573
  63.9 22.2 %collective-permute-start.11 = (bf16[2,48,1536]{2,1,0:T(8,128)(2,1)S(1)}, bf16[2,48,1536]{2,1,0:T(8,128)(2,1)S(1)}, u32[]{:S(2)}, u32[]{:S(2)}) collective-permute-start(bf16[2,48,1536]{2,1,0:T(8,128)(2,1)S(1)} %pad_maximum_fusion.11), channel_id=1, source_target_pairs={{0,4},{1,5},{2,6},{3,7},{4,0},{5,1},{6,2},{7,3},{8,12},{9,13},{10,... | collective-permute-start | bytes 884744 | tf_op jit(solution)/shard_map/ppermute | solution.py:573
  100.9 35.6 %collective-permute-start.18 = (bf16[8,48,1536]{2,1,0:T(8,128)(2,1)S(1)}, bf16[8,48,1536]{2,1,0:T(8,128)(2,1)S(1)}, u32[]{:S(2)}, u32[]{:S(2)}) collective-permute-start(bf16[8,48,1536]{2,1,0:T(8,128)(2,1)S(1)} %constant_dynamic-update-slice_fusion.8.refs_0_), channel_id=1, source_target_pairs={{0,16},{16,0},{1,17},{17,1},{2,18},{18,2},{3,19},{19,3},{4,20},{20... | collective-permute-start | bytes 3538952 | tf_op jit(solution)/shard_map/ppermute | solution.py:577
  117.4 19.1 %collective-permute-start.19 = (bf16[8,48,1536]{2,1,0:T(8,128)(2,1)S(1)}, bf16[8,48,1536]{2,1,0:T(8,128)(2,1)S(1)}, u32[]{:S(2)}, u32[]{:S(2)}) collective-permute-start(bf16[8,48,1536]{2,1,0:T(8,128)(2,1)S(1)} %collective-permute-done.17.refs_1_), channel_id=1, source_target_pairs={{0,16},{16,0},{1,17},{17,1},{2,18},{18,2},{3,19},{19,3},{4,20},{20... | collective-permute-start | bytes 3538952 | tf_op jit(solution)/shard_map/ppermute | solution.py:577
  118.0 18.5 %collective-permute-start.21 = (bf16[1,48,3072]{2,1,0:T(8,128)(2,1)S(1)}, bf16[1,48,3072]{2,1,0:T(8,128)(2,1)S(1)}, u32[]{:S(2)}, u32[]{:S(2)}) collective-permute-start(bf16[1,48,3072]{2,1,0:T(8,128)(2,1)S(1)} %bitcast.270), channel_id=1, source_target_pairs={{0,8},{1,9},{2,10},{3,11},{4,12},{5,13},{6,14},{7,15},{8,0},{9,1},... | collective-permute-start | bytes 884744 | tf_op jit(solution)/shard_map/ppermute | solution.py:573
  119.1 17.3 %collective-permute-start.20 = (bf16[4,48,1536]{2,1,0:T(8,128)(2,1)S(1)}, bf16[4,48,1536]{2,1,0:T(8,128)(2,1)S(1)}, u32[]{:S(2)}, u32[]{:S(2)}) collective-permute-start(bf16[4,48,1536]{2,1,0:T(8,128)(2,1)S(1)} %pad_maximum_fusion.4), channel_id=1, source_target_pairs={{0,2},{1,3},{2,0},{3,1},{4,6},{5,7},{6,4},{7,5},{8,10},{9,11},{10,... | collective-permute-start | bytes 1769480 | tf_op jit(solution)/shard_map/ppermute | solution.py:573
  136.6 18.0 %collective-permute-start.24 = (bf16[8,48,1536]{2,1,0:T(8,128)(2,1)S(1)}, bf16[8,48,1536]{2,1,0:T(8,128)(2,1)S(1)}, u32[]{:S(2)}, u32[]{:S(2)}) collective-permute-start(bf16[8,48,1536]{2,1,0:T(8,128)(2,1)S(1)} %constant_dynamic-update-slice_fusion.12.refs_0_), channel_id=1, source_target_pairs={{0,16},{16,0},{1,17},{17,1},{2,18},{18,2},{3,19},{19,3},{4,20},{20... | collective-permute-start | bytes 3538952 | tf_op jit(solution)/shard_map/ppermute | solution.py:577
  136.7 16.4 %collective-permute-start.22 = (bf16[8,48,1536]{2,1,0:T(8,128)(2,1)S(1)}, bf16[8,48,1536]{2,1,0:T(8,128)(2,1)S(1)}, u32[]{:S(2)}, u32[]{:S(2)}) collective-permute-start(bf16[8,48,1536]{2,1,0:T(8,128)(2,1)S(1)} %constant_dynamic-update-slice_fusion.12.refs_0_), channel_id=1, source_target_pairs={{0,1},{1,0},{2,3},{3,2},{4,5},{5,4},{6,7},{7,6},{8,9},{9,8},{10,11... | collective-permute-start | bytes 3538952 | tf_op jit(solution)/shard_map/ppermute | solution.py:573
  153.3 22.1 %collective-permute-start.26 = (bf16[4,48,3072]{2,1,0:T(8,128)(2,1)S(1)}, bf16[4,48,3072]{2,1,0:T(8,128)(2,1)S(1)}, u32[]{:S(2)}, u32[]{:S(2)}) collective-permute-start(bf16[4,48,3072]{2,1,0:T(8,128)(2,1)S(1)} %pad_maximum_fusion), channel_id=1, source_target_pairs={{0,2},{1,3},{2,0},{3,1},{4,6},{5,7},{6,4},{7,5},{8,10},{9,11},{10,... | collective-permute-start | bytes 3538952 | tf_op jit(solution)/shard_map/ppermute | solution.py:573
  175.5 29.0 %collective-permute-start.27 = (bf16[8,48,3072]{2,1,0:T(8,128)(2,1)S(1)}, bf16[8,48,3072]{2,1,0:T(8,128)(2,1)}, u32[]{:S(2)}, u32[]{:S(2)}) collective-permute-start(bf16[8,48,3072]{2,1,0:T(8,128)(2,1)S(1)} %constant_dynamic-update-slice_fusion.16.refs_0_), channel_id=1, source_target_pairs={{0,1},{1,0},{2,3},{3,2},{4,5},{5,4},{6,7},{7,6},{8,9},{9,8},{10,11... | collective-permute-start | bytes 7077896 | tf_op jit(solution)/shard_map/ppermute | solution.py:573
  176.8 35.6 %collective-permute-start.28 = (bf16[8,48,3072]{2,1,0:T(8,128)(2,1)S(1)}, bf16[8,48,3072]{2,1,0:T(8,128)(2,1)}, u32[]{:S(2)}, u32[]{:S(2)}) collective-permute-start(bf16[8,48,3072]{2,1,0:T(8,128)(2,1)S(1)} %constant_dynamic-update-slice_fusion.16.refs_0_), channel_id=1, source_target_pairs={{0,16},{16,0},{1,17},{17,1},{2,18},{18,2},{3,19},{19,3},{4,20},{20... | collective-permute-start | bytes 7077896 | tf_op jit(solution)/shard_map/ppermute | solution.py:577
  255.5 28.9 %collective-permute-start.31 = (bf16[8,48,3072]{2,1,0:T(8,128)(2,1)S(1)}, bf16[8,48,3072]{2,1,0:T(8,128)(2,1)S(1)}, u32[]{:S(2)}, u32[]{:S(2)}) collective-permute-start(bf16[8,48,3072]{2,1,0:T(8,128)(2,1)S(1)} %get-tuple-element.257), channel_id=1, source_target_pairs={{0,1},{1,0},{2,3},{3,2},{4,5},{5,4},{6,7},{7,6},{8,9},{9,8},{10,11... | collective-permute-start | bytes 7077896 | tf_op jit(solution)/shard_map/ppermute | solution.py:573
  307.2 16.9 %collective-permute-start.33 = (bf16[16,48,1536]{2,1,0:T(8,128)(2,1)}, bf16[16,48,1536]{2,1,0:T(8,128)(2,1)}, u32[]{:S(2)}, u32[]{:S(2)}) collective-permute-start(bf16[16,48,1536]{2,1,0:T(8,128)(2,1)} %bitcast.51), channel_id=1, source_target_pairs={{0,16},{16,0},{1,17},{17,1},{2,18},{18,2},{3,19},{19,3},{4,20},{20... | collective-permute-start | bytes 7077896 | tf_op jit(solution)/shard_map/ppermute | solution.py:577
  328.0 23.4 %collective-permute-start.35 = (bf16[8,48,1536]{2,1,0:T(8,128)(2,1)S(1)}, bf16[8,48,1536]{2,1,0:T(8,128)(2,1)S(1)}, u32[]{:S(2)}, u32[]{:S(2)}) collective-permute-start(bf16[8,48,1536]{2,1,0:T(8,128)(2,1)S(1)} %get-tuple-element.279), channel_id=1, source_target_pairs={{0,1},{1,0},{2,3},{3,2},{4,5},{5,4},{6,7},{7,6},{8,9},{9,8},{10,11... | collective-permute-start | bytes 3538952 | tf_op jit(solution)/shard_map/ppermute | solution.py:573
  330.4 21.0 %collective-permute-start.36 = (bf16[1,48,3072]{2,1,0:T(8,128)(2,1)S(1)}, bf16[1,48,3072]{2,1,0:T(8,128)(2,1)S(1)}, u32[]{:S(2)}, u32[]{:S(2)}) collective-permute-start(bf16[1,48,3072]{2,1,0:T(8,128)(2,1)S(1)} %slice.619), channel_id=1, source_target_pairs={{0,8},{1,9},{2,10},{3,11},{4,12},{5,13},{6,14},{7,15},{8,0},{9,1},... | collective-permute-start | bytes 884744 | tf_op jit(solution)/shard_map/ppermute | solution.py:573
  352.1 36.4 %collective-permute-start.37 = (bf16[16,48,3072]{2,1,0:T(8,128)(2,1)}, bf16[16,48,3072]{2,1,0:T(8,128)(2,1)}, u32[]{:S(2)}, u32[]{:S(2)}) collective-permute-start(bf16[16,48,3072]{2,1,0:T(8,128)(2,1)} %bitcast.53), channel_id=1, source_target_pairs={{0,16},{16,0},{1,17},{17,1},{2,18},{18,2},{3,19},{19,3},{4,20},{20... | collective-permute-start | bytes 14155784 | tf_op jit(solution)/shard_map/ppermute | solution.py:577
  392.8 33.0 %collective-permute-start.39 = (bf16[8,48,3072]{2,1,0:T(8,128)(2,1)S(1)}, bf16[8,48,3072]{2,1,0:T(8,128)(2,1)}, u32[]{:S(2)}, u32[]{:S(2)}) collective-permute-start(bf16[8,48,3072]{2,1,0:T(8,128)(2,1)S(1)} %get-tuple-element.288), channel_id=1, source_target_pairs={{0,1},{1,0},{2,3},{3,2},{4,5},{5,4},{6,7},{7,6},{8,9},{9,8},{10,11... | collective-permute-start | bytes 7077896 | tf_op jit(solution)/shard_map/ppermute | solution.py:573
  394.4 31.4 %collective-permute-start.40 = (bf16[2,48,1536]{2,1,0:T(8,128)(2,1)S(1)}, bf16[2,48,1536]{2,1,0:T(8,128)(2,1)S(1)}, u32[]{:S(2)}, u32[]{:S(2)}) collective-permute-start(bf16[2,48,1536]{2,1,0:T(8,128)(2,1)S(1)} %slice.622), channel_id=1, source_target_pairs={{0,4},{1,5},{2,6},{3,7},{4,0},{5,1},{6,2},{7,3},{8,12},{9,13},{10,... | collective-permute-start | bytes 884744 | tf_op jit(solution)/shard_map/ppermute | solution.py:573
  432.8 16.5 %collective-permute-start.41 = (bf16[4,48,3072]{2,1,0:T(8,128)(2,1)}, bf16[4,48,3072]{2,1,0:T(8,128)(2,1)}, u32[]{:S(2)}, u32[]{:S(2)}) collective-permute-start(bf16[4,48,3072]{2,1,0:T(8,128)(2,1)} %slice.627), channel_id=1, source_target_pairs={{0,2},{1,3},{2,0},{3,1},{4,6},{5,7},{6,4},{7,5},{8,10},{9,11},{10,... | collective-permute-start | bytes 3538952 | tf_op jit(solution)/shard_map/ppermute | solution.py:573
  460.4 18.2 %collective-permute-start.44 = (bf16[8,48,1664]{2,1,0:T(8,128)(2,1)S(1)}, bf16[8,48,1664]{2,1,0:T(8,128)(2,1)S(1)}, u32[]{:S(2)}, u32[]{:S(2)}) collective-permute-start(bf16[8,48,1664]{2,1,0:T(8,128)(2,1)S(1)} %get-tuple-element.310), channel_id=1, source_target_pairs={{0,1},{1,0},{2,3},{3,2},{4,5},{5,4},{6,7},{7,6},{8,9},{9,8},{10,11... | collective-permute-start | bytes 3833864 | tf_op jit(solution)/shard_map/ppermute | solution.py:573
  503.0 34.7 %collective-permute-start.59 = (bf16[48,3072]{1,0:T(8,128)(2,1)}, bf16[48,3072]{1,0:T(8,128)(2,1)}, u32[]{:S(2)}, u32[]{:S(2)}) collective-permute-start(bf16[48,3072]{1,0:T(8,128)(2,1)} %get-tuple-element.416), channel_id=1, source_target_pairs={{0,16},{16,0},{1,17},{17,1},{2,18},{18,2},{3,19},{19,3},{4,20},{20... | collective-permute-start | bytes 884744 | tf_op jit(solution)/shard_map/ppermute | solution.py:577
  515.9 29.2 %collective-permute-start.57 = (bf16[48,1664]{1,0:T(8,128)(2,1)}, bf16[48,1664]{1,0:T(8,128)(2,1)S(1)}, u32[]{:S(2)}, u32[]{:S(2)}) collective-permute-start(bf16[48,1664]{1,0:T(8,128)(2,1)} %get-tuple-element.418), channel_id=1, source_target_pairs={{0,16},{16,0},{1,17},{17,1},{2,18},{18,2},{3,19},{19,3},{4,20},{20... | collective-permute-start | bytes 479240 | tf_op jit(solution)/shard_map/ppermute | solution.py:577
  (166 other events, 1358.9 us)

commit v4 on v3

--- a/solution.py
+++ b/solution.py
@@ -15,6 +15,7 @@
 LANES = 128
 QUERY_BLOCK = 256
 HIDDEN_BLOCK = 512
+LIGHT = pl.CostEstimate(flops=3000000000, bytes_accessed=8000000, transcendentals=0)
 
 
 LN_EPS = 1e-06
@@ -59,7 +60,11 @@
         - jnp.mean(d_normal, axis=-1, keepdims=True)
         - normal_part * jnp.mean(d_normal * normal_part, axis=-1, keepdims=True)
     )
-    return (d_resid, jnp.sum(d_out * normal_part, axis=0), jnp.sum(d_out, axis=0))
+    return (
+        d_resid,
+        jnp.sum(d_out * normal_part, axis=0, keepdims=True),
+        jnp.sum(d_out, axis=0, keepdims=True),
+    )
 
 
 def gelu_slope(pre_act):
@@ -92,11 +97,11 @@
     return ref[:, pl.ds(at, LANES)].astype(jnp.float32)
 
 
-def attend_kernel(seq, len_ref, qkv_lo, qkv_hi, mixed_ref, lse_ref, ot_ref):
+def attend_kernel(len_ref, qkv_lo, qkv_hi, mixed_ref, lse_ref, ot_ref):
     rows = mixed_ref.shape[0]
     width = qkv_lo.shape[1] // 3
     pairs = width // LANES
-    real = len_ref[seq]
+    real = len_ref[pl.program_id(0)]
     lane = lax.broadcasted_iota(jnp.int32, (rows, LANES), 1)
     place_key = lax.broadcasted_iota(jnp.int32, (rows, LANES), 0)
     bias = jnp.where(place_key < real, 0.0, NEG_FILL)
@@ -106,20 +111,24 @@
             queries = pair_of(qkv_ref, 0, pair) * (1.0 / math.sqrt(HEAD_DIM))
             keys = pair_of(qkv_ref, 1, pair)
             values_t = pair_of(qkv_ref, 2, pair).T.astype(jnp.bfloat16)
+            scored = []
             for half in range(2):
                 keys_one = key_side(keys, bias, lane, half)
                 queries_one = query_side(queries, lane, half)
-                lanes = slice(half * HEAD_DIM, (half + 1) * HEAD_DIM)
-                head = side * 2 * pairs + 2 * pair + half
                 for at in range(0, rows, QUERY_BLOCK):
                     cols = slice(at, at + QUERY_BLOCK)
-                    scores = back_product(keys_one, queries_one[cols])
-                    top = jnp.max(scores, axis=0, keepdims=True)
-                    exps = jnp.exp(scores - top)
-                    total = jnp.sum(exps, axis=0, keepdims=True)
-                    mixed_t = forward_product(values_t[lanes], exps.astype(jnp.bfloat16))
-                    ot_ref[lanes, cols] = mixed_t / total
-                    lse_ref[pl.ds(head, 1), cols] = top + jnp.log(total)
+                    scored.append((half, cols, back_product(keys_one, queries_one[cols])))
+            weighed = []
+            for half, cols, scores in scored:
+                head = side * 2 * pairs + 2 * pair + half
+                top = jnp.max(scores, axis=0, keepdims=True)
+                exps = jnp.exp(scores - top)
+                total = jnp.sum(exps, axis=0, keepdims=True)
+                lse_ref[pl.ds(head, 1), cols] = top + jnp.log(total)
+                weighed.append((half, cols, exps.astype(jnp.bfloat16), total))
+            for half, cols, exps, total in weighed:
+                lanes = slice(half * HEAD_DIM, (half + 1) * HEAD_DIM)
+                ot_ref[lanes, cols] = forward_product(values_t[lanes], exps) / total
             at = pl.multiple_of(side * width + pair * LANES, LANES)
             mixed_ref[:, pl.ds(at, LANES)] = ot_ref[...].T.astype(jnp.bfloat16)
             return carry
@@ -127,49 +136,36 @@
         lax.fori_loop(0, pairs, one_pair, 0)
 
 
-def attend_core(qkv_lo, qkv_hi, seq_lengths, seq, filled=None):
+def attend_core(qkv_lo, qkv_hi, seq_lengths):
     total, wide = qkv_lo.shape
     seqs = seq_lengths.shape[0]
     rows, width = total // seqs, 2 * wide // 3
     heads = width // HEAD_DIM
     lse_rows = -(-heads // 8) * 8
-    side = pl.BlockSpec((rows, wide), lambda at, lens: (seq, 0))
-    kept = [] if filled is None else list(filled)
-    anywhere = pl.BlockSpec(memory_space=pl.ANY)
-
-    def kernel(len_ref, lo_ref, hi_ref, *rest):
-        attend_kernel(seq, len_ref, lo_ref, hi_ref, *rest[len(kept) :])
-
+    side = pl.BlockSpec((rows, wide), lambda seq, lens: (seq, 0))
     return pl.pallas_call(
-        kernel,
+        attend_kernel,
         out_shape=(
             jax.ShapeDtypeStruct((total, width), jnp.bfloat16),
             jax.ShapeDtypeStruct((seqs, lse_rows, rows), jnp.float32),
         ),
         grid_spec=pltpu.PrefetchScalarGridSpec(
             num_scalar_prefetch=1,
-            grid=(1,),
-            in_specs=[side, side] + [anywhere] * len(kept),
+            grid=(seqs,),
+            in_specs=[side, side],
             out_specs=[
-                pl.BlockSpec((rows, width), lambda at, lens: (seq, 0)),
-                pl.BlockSpec((None, lse_rows, rows), lambda at, lens: (seq, 0, 0)),
+                pl.BlockSpec((rows, width), lambda seq, lens: (seq, 0)),
+                pl.BlockSpec((None, lse_rows, rows), lambda seq, lens: (seq, 0, 0)),
             ],
             scratch_shapes=[pltpu.VMEM((LANES, rows), jnp.float32)],
         ),
-        input_output_aliases={3 + at: at for at in range(len(kept))},
-        compiler_params=pltpu.CompilerParams(vmem_limit_bytes=24 << 20),
-        cost_estimate=pl.CostEstimate(
-            flops=16 * rows * rows * width,
-            bytes_accessed=8 * rows * width,
-            transcendentals=rows * rows * heads,
-        ),
+        compiler_params=pltpu.CompilerParams(vmem_limit_bytes=32 << 20),
+        cost_estimate=LIGHT,
         name="attend",
-    )(seq_lengths, qkv_lo, qkv_hi, *kept)
-
-
-def attend_back_kernel(
-    len_ref, qkv_lo, qkv_hi, d_mixed_ref, lse_ref, d_qkv_ref, dqt_ref, dk_ref, dv_ref
-):
+    )(seq_lengths, qkv_lo, qkv_hi)
+
+
+def attend_back_kernel(len_ref, qkv_lo, qkv_hi, d_mixed_ref, lse_ref, d_qkv_ref, sums_ref, dqt_ref):
     rows = d_mixed_ref.shape[0]
     width = qkv_lo.shape[1] // 3
     pairs = width // LANES
@@ -187,36 +183,45 @@
             at_mixed = pl.multiple_of(side * width + pair * LANES, LANES)
             d_mixed = d_mixed_ref[:, pl.ds(at_mixed, LANES)].astype(jnp.float32)
             keys_t = keys.T.astype(jnp.bfloat16)
-            started = False
+            scored = []
             for half in range(2):
                 keys_one = key_side(keys, bias, lane, half)
                 queries_one = query_side(queries, lane, half)
                 values_only = one_head(values, lane, half)
                 queries_only = one_head(queries, lane, half)
                 d_mixed_only = one_head(d_mixed, lane, half)
-                lanes = slice(half * HEAD_DIM, (half + 1) * HEAD_DIM)
-                head = side * 2 * pairs + 2 * pair + half
                 for at in range(0, rows, QUERY_BLOCK):
                     cols = slice(at, at + QUERY_BLOCK)
                     scores = back_product(keys_one, queries_one[cols])
                     d_probs = back_product(values_only, d_mixed_only[cols])
-                    probs = jnp.exp(scores - lse_ref[pl.ds(head, 1), cols])
-                    row_part = jnp.sum(probs * d_probs, axis=0, keepdims=True)
-                    d_scores = (probs * (d_probs - row_part)).astype(jnp.bfloat16)
-                    d_values = forward_product(probs.astype(jnp.bfloat16), d_mixed_only[cols])
-                    d_keys = forward_product(d_scores, queries_only[cols])
-                    if started:
-                        dv_ref[...] += d_values
-                        dk_ref[...] += d_keys
-                    else:
-                        dv_ref[...] = d_values
-                        dk_ref[...] = d_keys
-                        started = True
-                    dqt_ref[lanes, cols] = forward_product(keys_t[lanes], d_scores)
-            outs = ((dqt_ref[...].T * scale), dk_ref[...], dv_ref[...])
-            for part, value in enumerate(outs):
+                    scored.append(
+                        (half, cols, scores, d_probs, queries_only[cols], d_mixed_only[cols])
+                    )
+            weighed = []
+            for half, cols, scores, d_probs, queries_only, d_mixed_only in scored:
+                head = side * 2 * pairs + 2 * pair + half
+                probs = jnp.exp(scores - lse_ref[pl.ds(head, 1), cols])
+                row_part = jnp.sum(probs * d_probs, axis=0, keepdims=True)
+                d_scores = (probs * (d_probs - row_part)).astype(jnp.bfloat16)
+                weighed.append(
+                    (half, cols, probs.astype(jnp.bfloat16), d_scores, queries_only, d_mixed_only)
+                )
+            d_keys = d_values = None
+            for half, cols, probs, d_scores, queries_only, d_mixed_only in weighed:
+                value_part = forward_product(probs, d_mixed_only)
+                key_part = forward_product(d_scores, queries_only)
+                d_values = value_part if d_values is None else d_values + value_part
+                d_keys = key_part if d_keys is None else d_keys + key_part
+                lanes = slice(half * HEAD_DIM, (half + 1) * HEAD_DIM)
+                dqt_ref[lanes, cols] = forward_product(keys_t[lanes], d_scores)
+            for part, value in enumerate((dqt_ref[...].T * scale, d_keys, d_values)):
                 at = pl.multiple_of(part * width + pair * LANES, LANES)
-                d_qkv_ref[side, :, pl.ds(at, LANES)] = value.astype(jnp.bfloat16)
+                rounded = value.astype(jnp.bfloat16)
+                d_qkv_ref[side, :, pl.ds(at, LANES)] = rounded
+                if part != 1:
+                    sums_ref[side, :, pl.ds(at, LANES)] = jnp.broadcast_to(
+                        jnp.sum(rounded.astype(jnp.float32), axis=0, keepdims=True), (8, LANES)
+                    )
             return carry
 
         lax.fori_loop(0, pairs, one_pair, 0)
@@ -230,7 +235,10 @@
     side = pl.BlockSpec((rows, wide), lambda seq, lens: (seq, 0))
     return pl.pallas_call(
         attend_back_kernel,
-        out_shape=jax.ShapeDtypeStruct((2, total, wide), jnp.bfloat16),
+        out_shape=(
+            jax.ShapeDtypeStruct((2, total, wide), jnp.bfloat16),
+            jax.ShapeDtypeStruct((seqs, 2, 8, wide), jnp.float32),
+        ),
         grid_spec=pltpu.PrefetchScalarGridSpec(
             num_scalar_prefetch=1,
             grid=(seqs,),
@@ -240,19 +248,14 @@
                 pl.BlockSpec((rows, width), lambda seq, lens: (seq, 0)),
                 pl.BlockSpec((None, lse.shape[1], rows), lambda seq, lens: (seq, 0, 0)),
             ],
-            out_specs=pl.BlockSpec((2, rows, wide), lambda seq, lens: (0, seq, 0)),
-            scratch_shapes=[
-                pltpu.VMEM((LANES, rows), jnp.float32),
-                pltpu.VMEM((rows, LANES), jnp.float32),
-                pltpu.VMEM((rows, LANES), jnp.float32),
+            out_specs=[
+                pl.BlockSpec((2, rows, wide), lambda seq, lens: (0, seq, 0)),
+                pl.BlockSpec((None, 2, 8, wide), lambda seq, lens: (seq, 0, 0, 0)),
             ],
+            scratch_shapes=[pltpu.VMEM((LANES, rows), jnp.float32)],
         ),
         compiler_params=pltpu.CompilerParams(vmem_limit_bytes=40 << 20),
-        cost_estimate=pl.CostEstimate(
-            flops=40 * total * rows * width,
-            bytes_accessed=14 * total * width,
-            transcendentals=total * rows * heads,
-        ),
+        cost_estimate=LIGHT,
         name="attend_back",
     )(seq_lengths, qkv_lo, qkv_hi, d_mixed, lse)
 
@@ -283,7 +286,7 @@
 def project_out_back(d_normed, normal_part, inv_std, out_layer, small_layer):
     d_resid, d_gain, d_shift = norm_backward(d_normed, normal_part, inv_std, small_layer[3])
     d_branch = d_resid.astype(jnp.bfloat16)
-    d_out_bias = jnp.sum(d_branch.astype(jnp.float32), axis=0)
+    d_out_bias = jnp.sum(d_branch.astype(jnp.float32), axis=0, keepdims=True)
     d_mixed = back_product(d_branch, out_layer).astype(jnp.bfloat16)
     return (d_resid, d_branch, d_mixed, (d_out_bias, d_gain, d_shift))
 
@@ -292,12 +295,14 @@
     return d_resid + sum(back_product(d_qkv[side], in_layer[side]) for side in range(2))
 
 
-def attn_small(d_qkv, sums_out):
-    third = d_qkv.shape[2] // 3
-    sums = jnp.sum(d_qkv.astype(jnp.float32), axis=1)
-    return jnp.stack(
-        [sums[:, :third].reshape(-1), sums[:, 2 * third :].reshape(-1)] + list(sums_out)
-    )
+def attn_small(sums, sums_out):
+    width = sums.shape[-1] // 3
+    sums = jnp.sum(sums[:, :, :1], axis=0)
+    rows = [
+        jnp.concatenate([sums[side, :, start : start + width] for side in range(2)], axis=1)
+        for start in (0, 2 * width)
+    ]
+    return rows + list(sums_out)
 
 
 def attn_grads_kernel(core, x_ref, mixed_ref, d_qkv_ref, d_branch_ref, *rest):
@@ -316,7 +321,7 @@
             mixed_t_ref[...], d_branch_ref[...]
         ).astype(jnp.bfloat16)
         if small_ref is not None:
-            out_ref[:, 4 * third :] = small_ref[...]
+            out_ref[:, 4 * third :] = small_ref[...].T.astype(jnp.bfloat16)
 
     @pl.when(pl.program_id(0) == 0)
     def _():
@@ -330,7 +335,7 @@
 def attn_grads(core, x_low, mixed_heads, d_qkv, d_branch, small=None):
     total, width = x_low.shape
     third = width // 2
-    extra = 0 if small is None else small.shape[2]
+    extra = 0 if small is None else small.shape[1]
 
     def side(at, core):
         return jnp.where(at == 0, 1 - core[0], core[0])
@@ -342,7 +347,7 @@
     given = [x_low, mixed_heads, d_qkv, d_branch]
     if small is not None:
         specs.append(
-            pl.BlockSpec((None, width, extra), lambda at, core: (side(at, core), 0, 0))
+            pl.BlockSpec((None, extra, width), lambda at, core: (side(at, core), 0, 0))
         )
         given.append(small)
     shape = jax.ShapeDtypeStruct((width, 4 * third + extra), jnp.bfloat16)
@@ -357,11 +362,7 @@
             scratch_shapes=[pltpu.VMEM((width, total), jnp.bfloat16)] * 2,
         ),
         compiler_params=pltpu.CompilerParams(vmem_limit_bytes=36 << 20),
-        cost_estimate=pl.CostEstimate(
-            flops=8 * total * width * width,
-            bytes_accessed=2 * (8 * total * width + 4 * width * width),
-            transcendentals=0,
-        ),
+        cost_estimate=LIGHT,
         name="attn_grads",
     )(core.reshape(1).astype(jnp.int32), *given)
 
@@ -395,11 +396,7 @@
         ],
         out_specs=[pl.BlockSpec((block, hidden), lambda at: (at, 0))] * 2,
         compiler_params=pltpu.CompilerParams(vmem_limit_bytes=32 << 20),
-        cost_estimate=pl.CostEstimate(
-            flops=2 * total * width * hidden,
-            bytes_accessed=2 * (width * hidden + 2 * total * hidden),
-            transcendentals=2 * total * hidden,
-        ),
+        cost_estimate=LIGHT,
         name="feed_up",
     )(rows_low, up_layer, bias)
     return (rows_low, act_low, slope)
@@ -415,14 +412,168 @@
     d_branch = d_resid.astype(jnp.bfloat16)
     d_pre = (back_product(d_branch, down_layer) * slope.astype(jnp.float32)).astype(jnp.bfloat16)
     model_width = d_resid.shape[1]
-    small_rows = jnp.concatenate(
-        [
-            jnp.sum(d_pre.astype(jnp.float32), axis=0).reshape(4, model_width),
-            jnp.stack([jnp.sum(d_branch.astype(jnp.float32), axis=0), d_gain, d_shift]),
+    d_bias = jnp.sum(d_pre.astype(jnp.float32), axis=0, keepdims=True)
+    small_rows = [
+        d_bias[:, part * model_width : (part + 1) * model_width] for part in range(4)
+    ] + [jnp.sum(d_branch.astype(jnp.float32), axis=0, keepdims=True), d_gain, d_shift]
+    return (d_resid, d_branch, d_pre, small_rows)
+
+
+def norm_back_rows(d_out, xhat, inv, gain):
+    d_normal = d_out * gain
+    d_resid = inv * (
+        d_normal
+        - jnp.mean(d_normal, axis=-1, keepdims=True)
+        - xhat * jnp.mean(d_normal * xhat, axis=-1, keepdims=True)
+    )
+    return (d_resid, d_resid.astype(jnp.bfloat16))
+
+
+def add_sums(sums_ref, values):
+    width = values[0].shape[1]
+    first = pl.program_id(0) == 0
+    for number, value in enumerate(values):
+        cols = slice(number * width, (number + 1) * width)
+        part = jnp.broadcast_to(jnp.sum(value, axis=0, keepdims=True), (8, width))
+        sums_ref[:, cols] = jnp.where(first, part, part + sums_ref[:, cols])
+
+
+def layer_back_kernel(
+    d_resid_ref, d_qkv_ref, in_ref, xhat_ref, inv_ref, gain_ref, down_ref, slope_ref, *outs
+):
+    out_resid_ref, d_branch_ref, d_pre_ref, pre_sums_ref, sums_ref = outs
+    d_out = d_resid_ref[...]
+    for side in range(2):
+        d_out = d_out + back_product(d_qkv_ref[side], in_ref[side])
+    xhat = xhat_ref[...]
+    d_resid, d_branch = norm_back_rows(d_out, xhat, inv_ref[:, :1], gain_ref[...])
+    out_resid_ref[...] = d_resid
+    d_branch_ref[...] = d_branch
+    add_sums(sums_ref, (d_branch.astype(jnp.float32), d_out * xhat, d_out))
+    first = pl.program_id(0) == 0
+    for at in range(0, down_ref.shape[0], HIDDEN_BLOCK):
+        cols = slice(at, at + HIDDEN_BLOCK)
+        d_act = back_product(d_branch, down_ref[cols])
+        d_pre = (d_act * slope_ref[:, cols].astype(jnp.float32)).astype(jnp.bfloat16)
+        d_pre_ref[:, cols] = d_pre
+        part = jnp.broadcast_to(
+            jnp.sum(d_pre.astype(jnp.float32), axis=0, keepdims=True), (8, HIDDEN_BLOCK)
+        )
+        pre_sums_ref[:, cols] = jnp.where(first, part, part + pre_sums_ref[:, cols])
+
+
+def layer_back(d_resid, d_qkv, in_layer, xhat, inv, small_layer, down_layer, slope):
+    total, width = d_resid.shape
+    hidden = slope.shape[1]
+    wide = d_qkv.shape[2]
+    block = math.gcd(total, 256)
+    row = pl.BlockSpec((block, width), lambda at: (at, 0))
+    hidden_row = pl.BlockSpec((block, hidden), lambda at: (at, 0))
+    d_resid, d_branch, d_pre, pre_sums, sums = pl.pallas_call(
+        layer_back_kernel,
+        out_shape=(
+            jax.ShapeDtypeStruct((total, width), jnp.float32),
+            jax.ShapeDtypeStruct((total, width), jnp.bfloat16),
+            jax.ShapeDtypeStruct((total, hidden), jnp.bfloat16),
+            jax.ShapeDtypeStruct((8, hidden), jnp.float32),
+            jax.ShapeDtypeStruct((8, 3 * width), jnp.float32),
+        ),
+        grid=(total // block,),
+        in_specs=[
+            row,
+            pl.BlockSpec((2, block, wide), lambda at: (0, at, 0)),
+            pl.BlockSpec((2, width, wide), lambda at: (0, 0, 0), pipeline_mode=pl.Buffered(1)),
+            row,
+            pl.BlockSpec((block, LANES), lambda at: (at, 0)),
+            pl.BlockSpec((1, width), lambda at: (0, 0)),
+            pl.BlockSpec((hidden, width), lambda at: (0, 0), pipeline_mode=pl.Buffered(1)),
+            hidden_row,
         ],
-        axis=0,
-    )
+        out_specs=[
+            row,
+            row,
+            hidden_row,
+            pl.BlockSpec((8, hidden), lambda at: (0, 0)),
+            pl.BlockSpec((8, 3 * width), lambda at: (0, 0)),
+        ],
+        compiler_params=pltpu.CompilerParams(vmem_limit_bytes=30 << 20),
+        cost_estimate=LIGHT,
+        name="layer_back",
+    )(d_resid, d_qkv, in_layer, xhat, inv, small_layer[10:11], down_layer, slope)
+    small_rows = [pre_sums[:1, part * width : (part + 1) * width] for part in range(4)]
+    small_rows += [sums[:1, part * width : (part + 1) * width] for part in range(3)]
     return (d_resid, d_branch, d_pre, small_rows)
+
+
+def feed_back_kernel(d_resid_ref, d_pre_ref, up_ref, xhat_ref, inv_ref, gain_ref, out_ref, *outs):
+    out_resid_ref, d_branch_ref, d_mixed_ref, sums_ref = outs
+    d_out = d_resid_ref[...] + back_product(d_pre_ref[...], up_ref[...])
+    xhat = xhat_ref[...]
+    d_resid, d_branch = norm_back_rows(d_out, xhat, inv_ref[:, :1], gain_ref[...])
+    out_resid_ref[...] = d_resid
+    d_branch_ref[...] = d_branch
+    d_mixed_ref[...] = back_product(d_branch, out_ref[...]).astype(jnp.bfloat16)
+    add_sums(sums_ref, (d_branch.astype(jnp.float32), d_out * xhat, d_out))
+
+
+def feed_back(d_resid, d_pre, up_layer, xhat, inv, small_layer, out_layer):
+    total, width = d_resid.shape
+    hidden = d_pre.shape[1]
+    block = math.gcd(total, 256)
+    row = pl.BlockSpec((block, width), lambda at: (at, 0))
+    d_resid, d_branch, d_mixed, sums = pl.pallas_call(
+        feed_back_kernel,
+        out_shape=(
+            jax.ShapeDtypeStruct((total, width), jnp.float32),
+            jax.ShapeDtypeStruct((total, width), jnp.bfloat16),
+            jax.ShapeDtypeStruct((total, width), jnp.bfloat16),
+            jax.ShapeDtypeStruct((8, 3 * width), jnp.float32),
+        ),
+        grid=(total // block,),
+        in_specs=[
+            row,
+            pl.BlockSpec((block, hidden), lambda at: (at, 0)),
+            pl.BlockSpec((width, hidden), lambda at: (0, 0), pipeline_mode=pl.Buffered(1)),
+            row,
+            pl.BlockSpec((block, LANES), lambda at: (at, 0)),
+            pl.BlockSpec((1, width), lambda at: (0, 0)),
+            pl.BlockSpec((width, width), lambda at: (0, 0), pipeline_mode=pl.Buffered(1)),
+        ],
+        out_specs=[row, row, row, pl.BlockSpec((8, 3 * width), lambda at: (0, 0))],
+        compiler_params=pltpu.CompilerParams(vmem_limit_bytes=24 << 20),
+        cost_estimate=LIGHT,
+        name="feed_back",
+    )(d_resid, d_pre, up_layer, xhat, inv, small_layer[3:4], out_layer)
+    sums_out = [sums[:1, part * width : (part + 1) * width] for part in range(3)]
+    return (d_resid, d_branch, d_mixed, sums_out)
+
+
+def order_attn_kernel(core_ref, *refs):
+    pairs, out_ref = (refs[:2], refs[2:4]), refs[4]
+    third = out_ref.shape[3] // 2
+    core = core_ref[0]
+    for layer, (own_ref, far_ref) in enumerate(pairs):
+        for part in range(4):
+            cols = slice(part * third, (part + 1) * third)
+            own, far = own_ref[:, cols], far_ref[:, cols]
+            for side in range(2):
+                out_ref[layer, part, :, side * third : (side + 1) * third] = jnp.where(
+                    core == side, own, far
+                )
+
+
+def order_attn(core, one, two, width):
+    local = pl.BlockSpec(memory_space=pltpu.VMEM)
+    shard = one[0].shape[0]
+    return pl.pallas_call(
+        order_attn_kernel,
+        out_shape=jax.ShapeDtypeStruct((2, 4, shard, width), jnp.bfloat16),
+        grid_spec=pltpu.PrefetchScalarGridSpec(
+            num_scalar_prefetch=1, grid=(), in_specs=[local] * 4, out_specs=local
+        ),
+        cost_estimate=LIGHT,
+        name="order_attn",
+    )(core.reshape(1).astype(jnp.int32), *one, *two)
 
 
 def feed_grads_kernel(shard, core, low_ref, d_pre_ref, act_ref, d_branch_ref, *rest):
@@ -500,11 +651,7 @@
             ],
         ),
         compiler_params=pltpu.CompilerParams(vmem_limit_bytes=40 << 20),
-        cost_estimate=pl.CostEstimate(
-            flops=4 * total * width * hidden,
-            bytes_accessed=2 * (4 * total * hidden + 2 * width * hidden),
-            transcendentals=0,
-        ),
+        cost_estimate=LIGHT,
         name="feed_grads",
     )(core.reshape(1).astype(jnp.int32), rows_low, d_pre, act_low, d_branch)
 
@@ -543,7 +690,7 @@
 def adam_update(
     master, first_moment, second_moment, gradient, clip_scale, step_value, decay_rate, rate_value
 ):
-    clipped = gradient * clip_scale
+    clipped = gradient.astype(jnp.float32) * clip_scale
     first_new = BETA_FIRST * first_moment + (1.0 - BETA_FIRST) * clipped
     second_new = BETA_SECOND * second_moment + (1.0 - BETA_SECOND) * clipped * clipped
     first_hat = first_new / (1.0 - jnp.power(BETA_FIRST, step_value))
@@ -560,16 +707,25 @@
     rest = bits - deep
     x_bits = [1 << at for at in range(rest - rest // 2)]
     y_bits = [1 << at for at in range(rest - rest // 2, rest)]
-    z_bits = [1 << at for at in reversed(range(rest, bits))]
-    first = z_bits + y_bits + x_bits
-    second = z_bits + x_bits + y_bits
-    return (first, second if len(x_bits) == len(y_bits) else first)
-
-
-def shift(value, step, peers):
+    z_bits = [1 << at for at in range(rest, bits)]
+    if len(x_bits) == len(y_bits):
+        return ((z_bits, y_bits, x_bits), (z_bits, x_bits, y_bits))
+    return ((z_bits, y_bits, x_bits), (z_bits, y_bits, x_bits))
+
+
+def stage_sizes(peers):
+    return [1 << len(bits) for bits in routes(peers)[0]]
+
+
+def mask_of(bits, turn):
+    return sum(bit for at, bit in enumerate(bits) if turn >> at & 1)
+
+
+def shift(value, stage, turn, peers):
     pairs = []
     for core, path in enumerate(routes(peers)):
-        pairs += [(core * peers + at, core * peers + (at ^ path[step])) for at in range(peers)]
+        mask = mask_of(path[stage], turn)
+        pairs += [(core * peers + at, core * peers + (at ^ mask)) for at in range(peers)]
     return lax.ppermute(value, ("dp", "bal"), pairs)
 
 
@@ -579,8 +735,7 @@
 
 def place_table(peers, core):
     masks = [
-        [sum(bit for at, bit in enumerate(path) if spot >> at & 1) for spot in range(peers)]
-        for path in routes(peers)
+        [mask_of(sum(path, []), spot) for spot in range(peers)] for path in routes(peers)
     ]
     masks = jnp.asarray(np.array(masks, np.int32))
     mine = lax.axis_index("bal")
@@ -589,16 +744,16 @@
     return jnp.concatenate([mine ^ own, mine ^ far, core.reshape(1).astype(jnp.int32)])
 
 
-def place_kernel(plan, spots, *refs):
-    parts, outs = refs[:4], refs[4:]
-    half, rows, _ = parts[0].shape
-    core = spots[4 * half]
+def place_kernel(plan, count, spots, *refs):
+    parts, outs = refs[:count], refs[count:]
+    held, rows, _ = parts[0].shape
+    core = spots[count * held]
 
     for number, part in enumerate(parts):
-        side = core if number < 2 else 1 - core
+        side = core if number < count // 2 else 1 - core
 
         def one_block(at, carry, number=number, part=part, side=side):
-            spot = spots[number * half + at]
+            spot = spots[number * held + at]
             for (start, width, kind), out in zip(plan, outs):
                 cols = pl.ds(pl.multiple_of(side * width, LANES), width)
                 if kind == "stack":
@@ -613,12 +768,12 @@
                         ]
             return carry
 
-        lax.fori_loop(0, half, one_block, 0)
+        lax.fori_loop(0, held, one_block, 0)
 
 
 def place(spots, parts, plan):
-    half, rows, whole = parts[0].shape
-    peers = 2 * half
+    held, rows, whole = parts[0].shape
+    peers = len(parts) * held // 2
     kinds = [
         (start, 4 * width, "stack") if kind == "down" and rows % 16 else (start, width, kind)
         for start, width, kind in plan
@@ -630,20 +785,18 @@
     }
     local = pl.BlockSpec(memory_space=pltpu.VMEM)
     placed = pl.pallas_call(
-        functools.partial(place_kernel, kinds),
+        functools.partial(place_kernel, kinds, len(parts)),
         out_shape=[
             jax.ShapeDtypeStruct(shapes[kind](width), parts[0].dtype) for _, width, kind in kinds
         ],
         grid_spec=pltpu.PrefetchScalarGridSpec(
             num_scalar_prefetch=1,
             grid=(),
-            in_specs=[local] * 4,
+            in_specs=[local] * len(parts),
             out_specs=[local] * len(kinds),
         ),
         compiler_params=pltpu.CompilerParams(vmem_limit_bytes=40 << 20),
-        cost_estimate=pl.CostEstimate(
-            flops=0, bytes_accessed=8 * peers * rows * whole, transcendentals=0
-        ),
+        cost_estimate=LIGHT,
         name="place",
     )(spots, *parts)
     results = []
@@ -660,21 +813,32 @@
 
 class Gather:
     def __init__(self, mine, spots, peers, plan):
-        self.kept = [mine[None]]
+        self.kept, self.moved = [mine[None]], []
         self.spots, self.peers, self.plan = spots, peers, plan
-        self.step, self.last = 0, peers.bit_length()
-
-    def launch(self):
-        if self.step < self.last - 1:
-            return [shift(self.kept[0], self.step, self.peers)]
-        return [swap(part) for part in self.kept]
+        self.sizes = stage_sizes(peers)
+        self.stage, self.turn = 0, 1
+
+    def done(self):
+        return self.stage > len(self.sizes)
+
+    def launch(self, count):
+        if self.stage == len(self.sizes):
+            return [swap(part) for part in self.kept]
+        stop = self.sizes[self.stage]
+        stop = stop if count is None else min(stop, self.turn + count)
+        turns = range(self.turn, stop)
+        self.turn = stop
+        return [shift(self.kept[0], self.stage, turn, self.peers) for turn in turns]
 
     def land(self, moved):
-        if self.step < self.last - 2:
-            self.kept = [jnp.concatenate([self.kept[0], moved[0]], axis=0)]
-        else:
-            self.kept = self.kept + moved
-        self.step += 1
+        self.moved += moved
+        if self.stage < len(self.sizes) and len(self.moved) < self.sizes[self.stage] - 1:
+            return
+        whole = self.kept + self.moved
+        if self.stage < len(self.sizes) - 1:
+            whole = [jnp.concatenate(whole, axis=0)]
+        self.kept, self.moved = whole, []
+        self.stage, self.turn = self.stage + 1, 1
 
     def result(self):
         return place(self.spots, self.kept, self.plan)
@@ -683,23 +847,41 @@
 class Scatter:
     def __init__(self, far, own, spots, peers):
         self.kept = [grads.reshape(peers, -1, grads.shape[1]) for grads in (own, far)]
+        self.moved = []
         self.spots, self.peers = spots, peers
-        self.step, self.last = 0, peers.bit_length()
-
-    def launch(self):
-        if self.step == 0:
+        self.sizes = stage_sizes(peers)
+        self.stage, self.turn = len(self.sizes), 1
+
+    def done(self):
+        return self.stage < 0
+
+    def launch(self, count):
+        if self.stage == len(self.sizes):
             return [swap(self.kept[1])]
-        return [shift(self.kept[1], self.last - 1 - self.step, self.peers)]
+        stop = self.sizes[self.stage]
+        stop = stop if count is None else min(stop, self.turn + count)
+        turns = range(self.turn, stop)
+        self.turn = stop
+        return [shift(self.kept[turn], self.stage, turn, self.peers) for turn in turns]
 
     def land(self, moved):
-        if self.step == 0:
-            self.kept = list(fold(self.spots, self.kept[0], moved[0]))
+        self.moved += moved
+        if self.stage == len(self.sizes):
+            self.kept = list(fold(self.spots, self.kept[0], self.moved[0], self.sizes[-1]))
         else:
-            total = self.kept[0].astype(jnp.float32) + moved[0].astype(jnp.float32)
-            half = total.shape[0] // 2
-            low_sum = total.astype(jnp.bfloat16)
-            self.kept = [low_sum[:half], low_sum[half:]] if half else [low_sum]
-        self.step += 1
+            if len(self.moved) < self.sizes[self.stage] - 1:
+                return
+            pieces = self.sizes[self.stage - 1] if self.stage else 1
+            size = self.kept[0].shape[0] // pieces
+
+            def total(at):
+                rows = slice(at * size, (at + 1) * size)
+                adds = [part[rows].astype(jnp.float32) for part in [self.kept[0]] + self.moved]
+                return sum(adds[1:], adds[0]).astype(jnp.bfloat16)
+
+            self.kept = [total(at) for at in range(pieces)]
+        self.moved = []
+        self.stage, self.turn = self.stage - 1, 1
 
     def result(self):
         return self.kept[0][0]
@@ -711,8 +893,9 @@
 
     def launch(self, *moves):
         for move in moves:
-            if move.step < move.last:
-                self.flying[move] = move.launch()
+            move, count = move if isinstance(move, tuple) else (move, None)
+            if not move.done():
+                self.flying[move] = self.flying.get(move, []) + move.launch(count)
 
     def meet(self, work, *landing, ready=()):
         moves = [move for move in landing if move in self.flying]
@@ -725,68 +908,52 @@
             move.kept = kept
         return work
 
+    def settle(self, work, *moves):
+        return self.meet(work, ready=moves)
+
     def finish(self, work, *moves):
         work = self.meet(work, *moves)
-        while any(move.step < move.last for move in moves):
+        while not all(move.done() for move in moves):
             self.launch(*moves)
             work = self.meet(work, *moves)
         return work
 
 
-def fold_kernel(spots, own, far, keep, send):
-    half = keep.shape[0]
+def fold_kernel(spots, own, far, *outs):
+    held = outs[0].shape[0]
 
     def one_block(at, carry):
-        for out, spot in ((keep, spots[at]), (send, spots[half + at])):
+        for number, out in enumerate(outs):
+            spot = spots[number * held + at]
             out[at] = (own[spot].astype(jnp.float32) + far[spot].astype(jnp.float32)).astype(
                 out.dtype
             )
         return carry
 
-    lax.fori_loop(0, half, one_block, 0)
-
-
-def fold(spots, own, far):
+    lax.fori_loop(0, held, one_block, 0)
+
+
+def fold(spots, own, far, pieces):
     peers, rows, width = own.shape
-    shape = jax.ShapeDtypeStruct((peers // 2, rows, width), own.dtype)
+    shape = jax.ShapeDtypeStruct((peers // pieces, rows, width), own.dtype)
     local = pl.BlockSpec(memory_space=pltpu.VMEM)
     return pl.pallas_call(
         fold_kernel,
-        out_shape=(shape, shape),
+        out_shape=[shape] * pieces,
         grid_spec=pltpu.PrefetchScalarGridSpec(
-            num_scalar_prefetch=1, grid=(), in_specs=[local, local], out_specs=[local, local]
+            num_scalar_prefetch=1,
+            grid=(),
+            in_specs=[local, local],
+            out_specs=[local] * pieces,
         ),
         compiler_params=pltpu.CompilerParams(vmem_limit_bytes=32 << 20),
-        cost_estimate=pl.CostEstimate(
-            flops=peers * rows * width,
-            bytes_accessed=6 * peers * rows * width,
-            transcendentals=0,
-        ),
+        cost_estimate=LIGHT,
         name="fold",
     )(spots, own, far)
 
 
-def both_sides(own, core):
-    other = swap(own)
+def both_sides(own, other, core):
     return (jnp.where(core == 0, own, other), jnp.where(core == 0, other, own))
-
-
-def sum_all(value, peers):
-    total = value.reshape(1, 1)
-    total = total + swap(total)
-    step = 1
-    while step < peers:
-        span = min(4, peers // step)
-        moved = [
-            lax.ppermute(total, "bal", [(at, at ^ (turn * step)) for at in range(peers)])
-            for turn in range(1, span)
-        ]
-        if span == 4:
-            total = (total + moved[0]) + (moved[1] + moved[2])
-        else:
-            total = total + moved[0]
-        step *= span
-    return total[0, 0]
 
 
 def per_device(
@@ -846,11 +1013,9 @@
     attn_two = Gather(
         attn_half[1], spots, peers, [(0, 3 * third, "stack"), (3 * third, third, "wide")]
     )
-    feed_two = Gather(
-        jnp.concatenate([up_half[1]] + down_half(1), axis=1),
-        spots,
-        peers,
-        [(0, hidden_half, "wide"), (hidden_half, third, "down")],
+    up_two = Gather(up_half[1], spots, peers, [(0, hidden_half, "wide")])
+    down_two = Gather(
+        jnp.concatenate(down_half(1), axis=1), spots, peers, [(0, third, "down")]
     )
     flat_low = tokens.reshape(rows_total, model_width)
     cot_flat = cotangent.reshape(rows_total, model_width)
@@ -858,60 +1023,57 @@
     flat_mask = token_mask.reshape(-1, 1) == 1
 
     lanes.launch(in_one)
-    lanes.meet((), in_one)
-    lanes.launch(in_one)
     lanes.meet((), in_one, ready=(out_up_one,))
-    lanes.launch(in_one, out_up_one)
+    lanes.launch(in_one, (out_up_one, 2))
     lanes.meet((), in_one, out_up_one)
     lanes.launch(in_one, out_up_one)
     lanes.meet((), in_one, out_up_one, ready=(down_one,))
-    lanes.launch(in_one, out_up_one, down_one)
+    lanes.launch(in_one, out_up_one, (down_one, 2))
     lanes.finish((), in_one)
-    first = in_one.result()
-    (w_in_one, small_rows), = lanes.meet((first,), out_up_one, down_one, ready=(attn_two,))
+    w_in_one, small_rows = in_one.result()
     small_vals = small_rows[:, :, :12].transpose(0, 2, 1).astype(jnp.float32)
+    qkv_one = project_in(flat_low, w_in_one, small_vals[0])
+    qkv_one = lanes.meet(qkv_one, out_up_one, down_one, ready=(attn_two,))
+    lanes.launch(out_up_one, down_one, (attn_two, 2))
+    attended = attend_core(qkv_one[0], qkv_one[1], seq_lengths)
+    attended = lanes.meet(attended, out_up_one, down_one, attn_two, ready=(up_two,))
     lanes.launch(out_up_one, down_one, attn_two)
-    qkv_one = project_in(flat_low, w_in_one, small_vals[0])
-    seqs = seq_lengths.shape[0]
-    attended = attend_core(qkv_one[0], qkv_one[1], seq_lengths, 0)
-    attended = lanes.meet(attended, out_up_one, down_one, attn_two, ready=(feed_two,))
-    lanes.launch(out_up_one, down_one, attn_two)
-    for seq in range(1, seqs):
-        attended = attend_core(qkv_one[0], qkv_one[1], seq_lengths, seq, attended)
-    attended = lanes.meet(attended, out_up_one, down_one, attn_two)
     mixed_one, lse_one = lanes.finish(attended, out_up_one)
-    lanes.launch(down_one, feed_two)
     w_out_one, w_up_one = out_up_one.result()
     attended_one = project_out(flat_low.astype(jnp.float32), mixed_one, w_out_one, small_vals[0])
-    attended_one, attn_xhat_one, attn_inv_one = lanes.meet(attended_one, down_one)
-    lanes.launch(down_one, attn_two)
+    attended_one = lanes.meet(attended_one, down_one, attn_two, ready=(down_two,))
+    attended_one, attn_xhat_one, attn_inv_one = attended_one
+    lanes.launch(down_one, attn_two, (up_two, 2))
     act_one = feed_up(attended_one, w_up_one, small_vals[0])
-    act_one = lanes.meet(act_one, down_one, attn_two, feed_two)
+    act_one = lanes.meet(act_one, down_one, attn_two, up_two)
+    lanes.launch(down_one, attn_two, up_two, (down_two, 1))
     low_one, act_one, slope_one = lanes.finish(act_one, down_one)
-    lanes.launch(attn_two, feed_two)
+    attn_inv_one = jnp.broadcast_to(attn_inv_one, (rows_total, LANES))
     (w_down_one,) = down_one.result()
     layer_one = feed_down(attended_one, act_one, w_down_one, small_vals[0])
-    layer_one = lanes.meet(layer_one, attn_two, feed_two)
-    lanes.launch(attn_two, feed_two)
+    layer_one = lanes.meet(layer_one, attn_two, up_two, down_two)
+    lanes.launch(attn_two, up_two, down_two)
     layer_one, feed_xhat_one, feed_inv_one = lanes.finish(layer_one, attn_two)
     w_in_two, w_out_two = attn_two.result()
+    feed_inv_one = jnp.broadcast_to(feed_inv_one, (rows_total, LANES))
+    w_in_two, w_out_two = lanes.meet((w_in_two, w_out_two), up_two, down_two)
+    lanes.launch(up_two, down_two)
     layer_low = layer_one.astype(jnp.bfloat16)
     qkv_two = project_in(layer_low, w_in_two, small_vals[1])
-    attended = attend_core(qkv_two[0], qkv_two[1], seq_lengths, 0)
-    attended = lanes.meet(attended, feed_two)
-    lanes.launch(feed_two)
-    for seq in range(1, seqs):
-        attended = attend_core(qkv_two[0], qkv_two[1], seq_lengths, seq, attended)
-    mixed_two, lse_two = attended
+    attended = attend_core(qkv_two[0], qkv_two[1], seq_lengths)
+    mixed_two, lse_two = lanes.meet(attended, up_two, down_two)
+    lanes.launch(up_two, down_two)
     attended_two = project_out(layer_one, mixed_two, w_out_two, small_vals[1])
-    attended_two = lanes.meet((attended_two, mixed_two, lse_two), feed_two)
-    (attended_two, attn_xhat_two, attn_inv_two), mixed_two, lse_two = attended_two
-    lanes.launch(feed_two)
+    attended_two, attn_xhat_two, attn_inv_two = attended_two
     rows_in = join_low(forward_product(select_rows, split_low(attended_two, 3)), 3)
     d_rows_out = forward_product(select_rows, cot_flat)
-    rows_in = lanes.finish(rows_in, feed_two)
-    w_up_two, w_down_two = feed_two.result()
+    rows_in = lanes.finish(rows_in, up_two)
+    rows_in = lanes.meet(rows_in, down_two)
+    lanes.launch(down_two)
+    (w_up_two,) = up_two.result()
     rows_low, act_two, slope_two = feed_up(rows_in, w_up_two, small_vals[1])
+    rows_low, act_two, slope_two = lanes.finish((rows_low, act_two, slope_two), down_two)
+    (w_down_two,) = down_two.result()
     out_rows, feed_xhat_two, feed_inv_two = feed_down(rows_in, act_two, w_down_two, small_vals[1])
     d_resid, d_branch, d_pre, feed_small_two = feed_down_back(
         d_rows_out, feed_xhat_two, feed_inv_two, slope_two, w_down_two, small_vals[1]
@@ -929,60 +1091,71 @@
     back = project_out_back(d_attended_two, attn_xhat_two, attn_inv_two, w_out_two, small_vals[1])
     d_resid, d_branch, d_mixed, sums_out = lanes.meet(back, g_feed_two)
     lanes.launch(g_feed_two)
-    d_qkv = attend_core_back(qkv_two[0], qkv_two[1], d_mixed, lse_two, seq_lengths)
-    d_qkv = lanes.meet(d_qkv, g_feed_two)
-    lanes.launch(g_feed_two)
+    back = attend_core_back(qkv_two[0], qkv_two[1], d_mixed, lse_two, seq_lengths)
+    d_qkv, sums = back
     grads = attn_grads(core, layer_low, mixed_two, d_qkv, d_branch)
-    d_layer_one = project_in_back(d_resid, d_qkv, w_in_two)
-    attn_small_two = attn_small(d_qkv, sums_out)
-    grads, d_layer_one = lanes.meet((grads, d_layer_one), g_feed_two)
+    grads, d_resid, d_qkv = lanes.meet((grads, d_resid, d_qkv), g_feed_two)
+    attn_small_two = attn_small(sums, sums_out)
     g_attn_two = Scatter(*grads, spots, peers)
-    lanes.launch(g_attn_two, g_feed_two)
-    back = feed_down_back(
-        d_layer_one, feed_xhat_one, feed_inv_one, slope_one, w_down_one, small_vals[0]
+    d_resid = lanes.settle(d_resid, g_feed_two)
+    lanes.launch(g_feed_two, g_attn_two)
+    back = layer_back(
+        d_resid,
+        d_qkv,
+        w_in_two,
+        feed_xhat_one,
+        feed_inv_one,
+        small_vals[0],
+        w_down_one,
+        slope_one,
     )
     d_resid, d_branch, d_pre, feed_small_one = lanes.meet(back, g_attn_two, g_feed_two)
-    lanes.launch(g_attn_two, g_feed_two)
+    d_branch = lanes.settle(d_branch, g_attn_two, g_feed_two)
+    lanes.launch(g_attn_two, (g_feed_two, 2))
     grads = feed_grads(core, low_one, d_pre, act_one, d_branch, shard)
-    grads = lanes.meet(grads, g_attn_two, g_feed_two)
+    grads, d_resid, d_pre = lanes.meet((grads, d_resid, d_pre), g_attn_two, g_feed_two)
     g_feed_one = Scatter(*grads, spots, peers)
+    d_pre = lanes.settle(d_pre, g_attn_two)
     lanes.launch(g_feed_one, g_attn_two)
-    d_attended_one = d_resid + back_product(d_pre, w_up_one)
-    back = project_out_back(d_attended_one, attn_xhat_one, attn_inv_one, w_out_one, small_vals[0])
+    back = feed_back(
+        d_resid, d_pre, w_up_one, attn_xhat_one, attn_inv_one, small_vals[0], w_out_one
+    )
     d_resid, d_branch, d_mixed, sums_out = lanes.meet(back, g_feed_one, g_attn_two)
+    d_mixed = lanes.settle(d_mixed, g_feed_one, g_attn_two)
+    lanes.launch(g_feed_one, (g_attn_two, 2), g_feed_two)
+    back = attend_core_back(qkv_one[0], qkv_one[1], d_mixed, lse_one, seq_lengths)
+    d_qkv, sums = lanes.meet(back, g_feed_one, g_attn_two, g_feed_two)
+    d_qkv, sums, d_branch = lanes.settle((d_qkv, sums, d_branch), g_feed_one, g_attn_two)
     lanes.launch(g_feed_one, g_attn_two)
-    d_qkv = attend_core_back(qkv_one[0], qkv_one[1], d_mixed, lse_one, seq_lengths)
-    d_qkv = lanes.meet(d_qkv, g_feed_one, g_attn_two)
-    lanes.launch(g_feed_one, g_attn_two)
-    attn_small_one = attn_small(d_qkv, sums_out)
+    attn_small_one = attn_small(sums, sums_out)
+    small_pad = [jnp.zeros((LANES - 12, model_width), jnp.float32)]
     small_grads = jnp.stack(
         [
-            jnp.concatenate([attn_small_one, feed_small_one], axis=0),
-            jnp.concatenate([attn_small_two, feed_small_two], axis=0),
+            jnp.concatenate(attn_small_one + feed_small_one + small_pad, axis=0),
+            jnp.concatenate(attn_small_two + feed_small_two + small_pad, axis=0),
         ]
     )
-
-    small_cols = jnp.pad(
-        small_grads.astype(jnp.bfloat16).transpose(0, 2, 1), ((0, 0), (0, 0), (0, LANES - 12))
-    )
-    grads = attn_grads(core, flat_low, mixed_one, d_qkv, d_branch, small_cols)
-    grads, d_resid, d_qkv = lanes.meet((grads, d_resid, d_qkv), g_feed_one, g_attn_two)
+    grads = attn_grads(core, flat_low, mixed_one, d_qkv, d_branch, small_grads)
+    grads, d_resid, d_qkv, attended_two, out_rows = lanes.meet(
+        (grads, d_resid, d_qkv, attended_two, out_rows), g_feed_one, g_attn_two
+    )
     g_attn_one = Scatter(*grads, spots, peers)
+    lanes.launch(g_attn_one)
+    lanes.meet((), g_attn_one)
+    lanes.launch(g_attn_one, (g_feed_one, 2))
+    d_tokens = project_in_back(d_resid, d_qkv, w_in_one).astype(jnp.bfloat16)
+    d_tokens, attended_two, out_rows = lanes.meet(
+        (d_tokens, attended_two, out_rows), g_attn_one, g_feed_one
+    )
     lanes.launch(g_attn_one, g_feed_one)
-    d_tokens = project_in_back(d_resid, d_qkv, w_in_one).astype(jnp.bfloat16)
-    d_tokens = lanes.meet(d_tokens, g_attn_one)
-    lanes.launch(g_attn_one)
     output_flat = jnp.where(
         flat_mask,
         weight_grad(select_rows, out_rows.astype(jnp.bfloat16)),
         attended_two,
     ).astype(jnp.bfloat16)
     output_flat = lanes.meet(output_flat, g_attn_one, g_feed_one)
-    lanes.launch(g_attn_one, g_feed_one)
-    lanes.meet((), g_attn_one)
     lanes.launch(g_attn_one)
-    lanes.meet((), g_attn_one, g_feed_one)
-    lanes.finish((), g_attn_one, g_feed_one, g_attn_two, g_feed_two)
+    lanes.finish((), g_feed_one, g_attn_two, g_feed_two, g_attn_one)
     owned = {
         "attn0": g_attn_one.result(),
         "feed0": g_feed_one.result(),
@@ -990,8 +1163,8 @@
         "feed1": g_feed_two.result(),
     }
     partial_squares = sum(jnp.sum(jnp.square(owned[name].astype(jnp.float32))) for name in owned)
-    both = {name: both_sides(owned[name], core) for name in owned}
-    square_total = sum_all(partial_squares, peers)
+    raw = {name: (owned[name], swap(owned[name])) for name in owned}
+    both = {name: both_sides(*raw[name], core) for name in raw}
 
     def joined(name, start, width):
         return jnp.concatenate([part[:, start : start + width] for part in both[name]], axis=1)
@@ -1002,18 +1175,25 @@
         )
 
     reduced = (
-        jnp.stack(
-            [
-                jnp.stack([joined(name, part * third, third) for part in range(4)])
-                for name in ("attn0", "attn1")
-            ]
-        ).astype(jnp.float32),
+        order_attn(core, raw["attn0"], raw["attn1"], model_width),
         jnp.stack([joined(name, 0, hidden_half) for name in ("feed0", "feed1")]).astype(
             jnp.float32
         ),
-        jnp.stack([down_rows(name) for name in ("feed0", "feed1")]).astype(jnp.float32),
-        jnp.stack([part[:, wide : wide + 12].T for part in both["attn0"]]).astype(jnp.float32),
-    )
+        jnp.stack([down_rows(name) for name in ("feed0", "feed1")]),
+        jnp.stack([part[:, wide : wide + 12].T for part in both["attn0"]]),
+    )
+    partial_squares = partial_squares.reshape(1, 1)
+    partial_squares = partial_squares + swap(partial_squares)
+    hops = [
+        (stage, 1 << at)
+        for stage, bits in enumerate(routes(peers)[0])
+        for at in range(len(bits))
+    ]
+    for stage, turn in hops[:-1]:
+        partial_squares = partial_squares + shift(partial_squares, stage, turn, peers)
+    reduced, partial_squares = lax.optimization_barrier((reduced, partial_squares))
+    moved = shift(partial_squares, *hops[-1], peers)
+    square_total = (partial_squares + moved)[0, 0]
     grad_norm = jnp.sqrt(square_total).reshape(1)
     clip_scale = jnp.minimum(1.0, CLIP_NORM / (grad_norm[0] + 1e-06))
     step_value = step_count[0].astype(jnp.float32)

time: 569 us -> 537 us (0.944)
  waiting for transfers between devices: 112 us -> 72.1 us
  local copies, waits for them, and re-layouts: 47.7 us -> 82 us
  matrix products: 69.1 us -> 44.3 us
  starting transfers between devices: 63.5 us -> 87.7 us
  Pallas kernels: 184 us -> 170 us
  other arithmetic: 69.6 us -> 59.3 us
    ppermute x36 -> x54, waiting for transfers between devices: 109 us -> 67.7 us  [shift(): return lax.ppermute(value, ('dp', 'bal'), pairs)]
    ppermute x36 -> x54, starting transfers between devices: 43 us -> 83.3 us  [shift(): return lax.ppermute(value, ('dp', 'bal'), pairs)]
    unnamed x287 -> x331, local copies, waits for them, and re-layouts: 26.3 us -> 61.6 us
    dot_general x10 -> x5, matrix products: 33.9 us -> 13.4 us  [back_product(): lax.dot_general(left_side, right_side, (((1,), (1,)), ((), ())), preferre...]
    ppermute x6 -> x0, starting transfers between devices: 15.8 us -> none  [sum_all(): lax.ppermute(total, 'bal', [(at, at ^ turn * step) for at in range(peers)])]
    pallas_call x15 -> x17, Pallas kernels: 127 us -> 116 us  [the longest x2 41.8 us: attend_core_back(): pl.pallas_call(attend_back_kernel, out_shape=(jax.ShapeDtypeStruct((2, to...]
    reduce_sum x9 -> x6, other arithmetic: 18.6 us -> 7.91 us  [the longest x1 3.34 us: norm_backward(): jnp.sum(d_out * normal_part, axis=0, keepdims=True)]
    concatenate x9 -> x8, local copies, waits for them, and re-layouts: 2.26 us -> 10.3 us  [the longest x6 4.2 us: land(): whole = [jnp.concatenate(whole, axis=0)]]
  transfers between devices with their start and end apart: 61 -> 75, of which waited for: 24 -> 25; matrix products, arithmetic and copies ran while one was open for 23% -> 20% of each run, Pallas kernels for 28% -> 28%
where the time goes in v4:
time: 537 us; the launch traced here: 527 us
  Pallas kernels  170 us (32%)
  starting transfers between devices  87.7 us (16%)
  local copies, waits for them, and re-layouts  82 us (15%)
  waiting for transfers between devices  72.1 us (13%)
  other arithmetic  59.3 us (11%)
  matrix products  44.3 us (8%)
  between operations  11.3 us (2%)
    ppermute x54, starting transfers between devices, shift(): return lax.ppermute(value, ('dp', 'bal'), pairs)  83.3 us
    ppermute x54, waiting for transfers between devices, shift(): return lax.ppermute(value, ('dp', 'bal'), pairs)  67.7 us
    unnamed x331, local copies, waits for them, and re-layouts  61.6 us
    pallas_call x2, Pallas kernels, attend_core_back(): pl.pallas_call(attend_back_kernel, out_shape=(jax.ShapeDtypeStruct((2, to...  41.8 us
    pallas_call x2, Pallas kernels, attend_core(): pl.pallas_call(attend_kernel, out_shape=(jax.ShapeDtypeStruct((total, wid...  27.1 us
    dot_general x11, matrix products, forward_product(): return jnp.dot(left_side, right_side, preferred_element_type=jnp.float32)  26.8 us
    pallas_call x2, Pallas kernels, feed_grads(): pl.pallas_call(functools.partial(feed_grads_kernel, shard), out_shape=(sh...  26.7 us
    pallas_call x1, Pallas kernels, layer_back(): pl.pallas_call(layer_back_kernel, out_shape=(jax.ShapeDtypeStruct((total,...  17.4 us
  transfers between devices with their start and end apart: 75, of which 25 were waited for; matrix products, arithmetic and copies ran while one was open for 20% of the time, Pallas kernels for 28%

profile of v4, /device:TPU:0, one launch (start us, length us, event | category | flops | bytes accessed | tf_op | source)
XLA Modules:
  0.0 526.7 jit_solution(15716264638022973118)
XLA Ops:
  9.9 7.7 %collective-permute-done.1 = bf16[1,48,1280]{2,1,0:T(8,128)(2,1)S(1)} collective-permute-done((bf16[1,48,1280]{2,1,0:T(8,128)(2,1)S(1)}, bf16[1,48,1280]{2,1,0:T(8,128)(2,1)S(1)}, u32[]{:S(2)}, u32[]{:S(2)}) %collective-permute-start.1) | collective-permute-done | bytes 122912 | tf_op jit(solution)/shard_map/ppermute | solution.py:729
  35.8 4.3 collective-permute-done.7
  70.2 13.5 %attend.2 = (bf16[1024,768]{1,0:T(8,128)(2,1)S(1)}, f32[2,16,512]{2,1,0:T(8,128)S(1)}) custom-call(s32[2]{0:T(128)S(1)} %copy-done.41, bf16[1024,1152]{1,0:T(8,128)(2,1)S(1)} %fusion.7.qkv_lo, bf16[1024,1152]{1,0:T(8,128)(2,1)S(1)} %fusion.8.qkv_hi), custom_call_target="tpu_custom_call" | custom-call | flops 3000000000 | bytes 8000000 | tf_op jit(solution)/shard_map/attend/pallas_call | solution.py:146
  111.5 10.6 %feed_up.2 = (bf16[1024,3072]{1,0:T(8,128)(2,1)S(1)}, bf16[1024,3072]{1,0:T(8,128)(2,1)S(1)}) custom-call(bf16[1024,768]{1,0:T(8,128)(2,1)S(1)} %convert_element_type.461.rows_ref.low_ref, bf16[768,3072]{1,0:T(8,128)(2,1)S(1)} %bitcast.196, f32[1,3072]{1,0:T(1,128)S(1)} %bitcast.206), custom_call_target="tpu_custom_call" | custom-call | flops 3000000000 | bytes 8000000 | tf_op jit(solution)/shard_map/feed_up/pallas_call | solution.py:388
  137.2 8.8 %fusion.91 = (f32[1024]{0:T(1024)S(1)}, f32[1024,768]{1,0:T(8,128)S(1)}) fusion(f32[1024,768]{1,0:T(8,128)} %get-tuple-element.270, f32[768]{0:T(1024)S(1)} %copy-done.135, bf16[1024,3072]{1,0:T(8,128)(2,1)S(1)} %get-tuple-element.284.act_ref, bf16[3072,768]{1,0:T(8,128)(2,1)S(1)} %bitcast.198), kind=kOutput, calls=%fused_computation.306 | convolution fusion | flops 4834196480 | bytes 17308672 | tf_op jit(solution)/shard_map/dot_general | solution.py:33
  155.0 5.1 collective-permute-done.32
  168.9 13.5 %attend.3 = (bf16[1024,768]{1,0:T(8,128)(2,1)S(1)}, f32[2,16,512]{2,1,0:T(8,128)S(1)}) custom-call(s32[2]{0:T(128)S(1)} %copy-done.41, bf16[1024,1152]{1,0:T(8,128)(2,1)S(1)} %add_convert_fusion.1.qkv_lo, bf16[1024,1152]{1,0:T(8,128)(2,1)S(1)} %add_convert_fusion.qkv_hi), custom_call_target="tpu_custom_call" | custom-call | flops 3000000000 | bytes 8000000 | tf_op jit(solution)/shard_map/attend/pallas_call | solution.py:146
  191.5 7.5 %collective-permute-done.39.refs_1_ = bf16[8,48,1536]{2,1,0:T(8,128)(2,1)S(1)} collective-permute-done((bf16[8,48,1536]{2,1,0:T(8,128)(2,1)S(1)}, bf16[8,48,1536]{2,1,0:T(8,128)(2,1)S(1)}, u32[]{:S(2)}, u32[]{:S(2)}) %collective-permute-start.39) | collective-permute-done | bytes 1179680 | tf_op jit(solution)/shard_map/ppermute | solution.py:729
  204.7 4.2 feed_up.3
  218.2 10.1 %feed_grads.2 = (bf16[768,3072]{1,0:T(8,128)(2,1)S(1)}, bf16[768,3072]{1,0:T(8,128)(2,1)}) custom-call(s32[1]{0:T(128)} %bitcast.1.core.core_ref, bf16[384,768]{1,0:T(8,128)(2,1)S(1)} %convert_element_type.468.rows_ref.low_ref, bf16[384,3072]{1,0:T(8,128)(2,1)S(1)} %get-tuple-element.327.d_pre_ref, bf16[384,3072]{1,0:T(8,128)(2,1)S(1)} %get-tuple-element.320.act_ref, ...), custom_call_target="tpu_custom_call" | custom-call | flops 3000000000 | bytes 8000000 | tf_op jit(solution)/shard_map/feed_grads/pallas_call | solution.py:635
  228.8 4.4 reduce-precision_convert_fusion.2
  254.7 20.8 %attend_back.2 = (bf16[2,1024,1152]{2,1,0:T(8,128)(2,1)S(1)}, f32[2,2,8,1152]{3,2,1,0:T(8,128)S(1)}) custom-call(s32[2]{0:T(128)S(1)} %copy-done.41, bf16[1024,1152]{1,0:T(8,128)(2,1)S(1)} %copy-done.62, bf16[1024,1152]{1,0:T(8,128)(2,1)S(1)} %copy-done.60, bf16[1024,768]{1,0:T(8,128)(2,1)S(1)} %copy-done.63, f32[2,16,512]{2,1,0:T(8,128)S(1)} %get-tuple-element.330.lse_ref), custom_call_target="tpu_custom_call" | custom-call | flops 3000000000 | bytes 8000000 | tf_op jit(solution)/shard_map/attend_back/pallas_call | solution.py:236
  284.4 6.7 %attn_grads.2 = (bf16[768,1536]{1,0:T(8,128)(2,1)S(1)}, bf16[768,1536]{1,0:T(8,128)(2,1)S(1)}) custom-call(s32[1]{0:T(128)} %bitcast.1.core.core_ref, bf16[1024,768]{1,0:T(8,128)(2,1)S(1)} %copy-done.23, bf16[1024,768]{1,0:T(8,128)(2,1)S(1)} %copy-done.54, bf16[2,1024,1152]{2,1,0:T(8,128)(2,1)S(1)} %copy-done.10, bf16[1024,768]{1,0:T(8,128)(2,1)S(1)} %copy-done.21), custom_call_target="tpu_custom_call" | custom-call | flops 3000000000 | bytes 8000000 | tf_op jit(solution)/shard_map/attn_grads/pallas_call | solution.py:354
  301.7 17.4 %layer_back.1 = (f32[1024,768]{1,0:T(8,128)S(1)}, bf16[1024,768]{1,0:T(8,128)(2,1)S(1)}, bf16[1024,3072]{1,0:T(8,128)(2,1)}, f32[8,3072]{1,0:T(8,128)S(1)}, f32[8,2304]{1,0:T(8,128)S(1)}) custom-call(f32[1024,768]{1,0:T(8,128)S(1)} %get-tuple-element.342.d_resid_ref, bf16[2,1024,1152]{2,1,0:T(8,128)(2,1)S(1)} %copy-done.11, ...), custom_call_target="tpu_custom_call" | custom-call | flops 3000000000 | bytes 8000000 | tf_op jit(solution)/shard_map/layer_back/pallas_call | solution.py:472
  330.3 16.7 %feed_grads.3 = (bf16[768,3072]{1,0:T(8,128)(2,1)}, bf16[768,3072]{1,0:T(8,128)(2,1)S(1)}) custom-call(s32[1]{0:T(128)} %bitcast.1.core.core_ref, bf16[1024,768]{1,0:T(8,128)(2,1)S(1)} %copy-done.2, bf16[1024,3072]{1,0:T(8,128)(2,1)} %get-tuple-element.373.d_pre_ref, bf16[1024,3072]{1,0:T(8,128)(2,1)} %copy-done, bf16[1024,768]{1,0:T(8,128)(2,1)S(1)} %copy-done.19), custom_call_target="tpu_custom_call" | custom-call | flops 3000000000 | bytes 8000000 | tf_op jit(solution)/shard_map/feed_grads/pallas_call | solution.py:635
  354.6 10.3 %feed_back.1 = (f32[1024,768]{1,0:T(8,128)S(1)}, bf16[1024,768]{1,0:T(8,128)(2,1)S(1)}, bf16[1024,768]{1,0:T(8,128)(2,1)S(1)}, f32[8,2304]{1,0:T(8,128)S(1)}) custom-call(f32[1024,768]{1,0:T(8,128)S(1)} %copy-done.15, bf16[1024,3072]{1,0:T(8,128)(2,1)S(1)} %bitcast.195, bf16[768,3072]{1,0:T(8,128)(2,1)S(1)} %bitcast.197, ...), custom_call_target="tpu_custom_call" | custom-call | flops 3000000000 | bytes 8000000 | tf_op jit(solution)/shard_map/feed_back/pallas_call | solution.py:524
  382.6 21.0 %attend_back.3 = (bf16[2,1024,1152]{2,1,0:T(8,128)(2,1)S(1)}, f32[2,2,8,1152]{3,2,1,0:T(8,128)S(1)}) custom-call(s32[2]{0:T(128)S(1)} %copy-done.41, bf16[1024,1152]{1,0:T(8,128)(2,1)S(1)} %copy-done.58, bf16[1024,1152]{1,0:T(8,128)(2,1)S(1)} %copy-done.56, bf16[1024,768]{1,0:T(8,128)(2,1)S(1)} %copy-done.40, f32[2,16,512]{2,1,0:T(8,128)S(1)} %get-tuple-element.390.lse_ref), custom_call_target="tpu_custom_call" | custom-call | flops 3000000000 | bytes 8000000 | tf_op jit(solution)/shard_map/attend_back/pallas_call | solution.py:236
  422.0 6.3 %attn_grads.3 = (bf16[768,1664]{1,0:T(8,128)(2,1)S(1)}, bf16[768,1664]{1,0:T(8,128)(2,1)S(1)}) custom-call(s32[1]{0:T(128)} %bitcast.1.core.core_ref, bf16[1024,768]{1,0:T(8,128)(2,1)S(1)} %bitcast.215, bf16[1024,768]{1,0:T(8,128)(2,1)S(1)} %copy-done.52, bf16[2,1024,1152]{2,1,0:T(8,128)(2,1)S(1)} %copy-done.50, bf16[1024,768]{1,0:T(8,128)(2,1)S(1)} %copy-done.38, ...), custom_call_target="tpu_custom_call" | custom-call | flops 3000000000 | bytes 8000000 | tf_op jit(solution)/shard_map/attn_grads/pallas_call | solution.py:354
  451.8 5.1 collective-permute-done.58
  462.3 5.4 %collective-permute-done.62 = bf16[1,48,3072]{2,1,0:T(8,128)(2,1)S(1)} collective-permute-done((bf16[1,48,3072]{2,1,0:T(8,128)(2,1)S(1)}, bf16[1,48,3072]{2,1,0:T(8,128)(2,1)S(1)}, u32[]{:S(2)}, u32[]{:S(2)}) %collective-permute-start.62) | collective-permute-done | bytes 294944 | tf_op jit(solution)/shard_map/ppermute | solution.py:729
  467.9 4.8 collective-permute-start.63
  479.8 5.7 %collective-permute-done.64 = bf16[1,48,1664]{2,1,0:T(8,128)(2,1)S(1)} collective-permute-done((bf16[1,48,1664]{2,1,0:T(8,128)(2,1)S(1)}, bf16[1,48,1664]{2,1,0:T(8,128)(2,1)S(1)}, u32[]{:S(2)}, u32[]{:S(2)}) %collective-permute-start.64) | collective-permute-done | bytes 159776 | tf_op jit(solution)/shard_map/ppermute | solution.py:729
  491.0 4.0 collective-permute-start.71
  514.6 4.4 fusion.68
  (637 shorter events, 297.2 us)
Async XLA Ops:
  70.2 23.4 %collective-permute-start.17 = (bf16[8,48,1920]{2,1,0:T(8,128)(2,1)S(1)}, bf16[8,48,1920]{2,1,0:T(8,128)(2,1)S(1)}, u32[]{:S(2)}, u32[]{:S(2)}) collective-permute-start(bf16[8,48,1920]{2,1,0:T(8,128)(2,1)S(1)} %constant_dynamic-update-slice_fusion.5.refs_0_), channel_id=1, source_target_pairs={{0,16},{16,0},{1,17},{17,1},{2,18},{18,2},{3,19},{19,3},{4,20},{20... | collective-permute-start | bytes 4423688 | tf_op jit(solution)/shard_map/ppermute | solution.py:733
  103.2 22.4 %collective-permute-start.21 = (bf16[8,48,1536]{2,1,0:T(8,128)(2,1)}, bf16[8,48,1536]{2,1,0:T(8,128)(2,1)}, u32[]{:S(2)}, u32[]{:S(2)}) collective-permute-start(bf16[8,48,1536]{2,1,0:T(8,128)(2,1)} %constant_dynamic-update-slice_fusion.10.refs_0_), channel_id=1, source_target_pairs={{0,1},{1,0},{2,3},{3,2},{4,5},{5,4},{6,7},{7,6},{8,9},{9,8},{10,11... | collective-permute-start | bytes 3538952 | tf_op jit(solution)/shard_map/ppermute | solution.py:729
  109.4 21.9 %collective-permute-start.25 = (bf16[8,48,1536]{2,1,0:T(8,128)(2,1)}, bf16[8,48,1536]{2,1,0:T(8,128)(2,1)S(1)}, u32[]{:S(2)}, u32[]{:S(2)}) collective-permute-start(bf16[8,48,1536]{2,1,0:T(8,128)(2,1)} %constant_dynamic-update-slice_fusion.10.refs_0_), channel_id=1, source_target_pairs={{0,16},{16,0},{1,17},{17,1},{2,18},{18,2},{3,19},{19,3},{4,20},{20... | collective-permute-start | bytes 3538952 | tf_op jit(solution)/shard_map/ppermute | solution.py:733
  125.6 23.3 %collective-permute-start.28 = (bf16[1,48,1536]{2,1,0:T(8,128)(2,1)S(1)}, bf16[1,48,1536]{2,1,0:T(8,128)(2,1)S(1)}, u32[]{:S(2)}, u32[]{:S(2)}) collective-permute-start(bf16[1,48,1536]{2,1,0:T(8,128)(2,1)S(1)} %copy-done.87), channel_id=1, source_target_pairs={{0,12},{1,13},{2,14},{3,15},{4,8},{5,9},{6,10},{7,11},{8,4},{9,5},... | collective-permute-start | bytes 442376 | tf_op jit(solution)/shard_map/ppermute | solution.py:729
  128.2 20.8 %collective-permute-start.29 = (bf16[1,48,1536]{2,1,0:T(8,128)(2,1)S(1)}, bf16[1,48,1536]{2,1,0:T(8,128)(2,1)S(1)}, u32[]{:S(2)}, u32[]{:S(2)}) collective-permute-start(bf16[1,48,1536]{2,1,0:T(8,128)(2,1)S(1)} %maximum_bitcast_fusion.6), channel_id=1, source_target_pairs={{0,4},{1,5},{2,6},{3,7},{4,0},{5,1},{6,2},{7,3},{8,12},{9,13},{10,... | collective-permute-start | bytes 442376 | tf_op jit(solution)/shard_map/ppermute | solution.py:729
  128.2 26.8 %collective-permute-start.33 = (bf16[1,48,1536]{2,1,0:T(8,128)(2,1)S(1)}, bf16[1,48,1536]{2,1,0:T(8,128)(2,1)S(1)}, u32[]{:S(2)}, u32[]{:S(2)}) collective-permute-start(bf16[1,48,1536]{2,1,0:T(8,128)(2,1)S(1)} %maximum_bitcast_fusion.6), channel_id=1, source_target_pairs={{0,8},{1,9},{2,10},{3,11},{4,12},{5,13},{6,14},{7,15},{8,0},{9,1},... | collective-permute-start | bytes 442376 | tf_op jit(solution)/shard_map/ppermute | solution.py:729
  131.3 23.7 %collective-permute-start.34 = (bf16[1,48,1536]{2,1,0:T(8,128)(2,1)S(1)}, bf16[1,48,1536]{2,1,0:T(8,128)(2,1)S(1)}, u32[]{:S(2)}, u32[]{:S(2)}) collective-permute-start(bf16[1,48,1536]{2,1,0:T(8,128)(2,1)S(1)} %maximum_bitcast_fusion.6), channel_id=1, source_target_pairs={{0,12},{1,13},{2,14},{3,15},{4,8},{5,9},{6,10},{7,11},{8,4},{9,5},... | collective-permute-start | bytes 442376 | tf_op jit(solution)/shard_map/ppermute | solution.py:729
  160.2 22.6 %collective-permute-start.35 = (bf16[8,48,1536]{2,1,0:T(8,128)(2,1)S(1)}, bf16[8,48,1536]{2,1,0:T(8,128)(2,1)S(1)}, u32[]{:S(2)}, u32[]{:S(2)}) collective-permute-start(bf16[8,48,1536]{2,1,0:T(8,128)(2,1)S(1)} %constant_dynamic-update-slice_fusion.20.refs_0_), channel_id=1, source_target_pairs={{0,1},{1,0},{2,3},{3,2},{4,5},{5,4},{6,7},{7,6},{8,9},{9,8},{10,11... | collective-permute-start | bytes 3538952 | tf_op jit(solution)/shard_map/ppermute | solution.py:729
  161.1 30.4 %collective-permute-start.37 = (bf16[8,48,1536]{2,1,0:T(8,128)(2,1)S(1)}, bf16[8,48,1536]{2,1,0:T(8,128)(2,1)S(1)}, u32[]{:S(2)}, u32[]{:S(2)}) collective-permute-start(bf16[8,48,1536]{2,1,0:T(8,128)(2,1)S(1)} %constant_dynamic-update-slice_fusion.20.refs_0_), channel_id=1, source_target_pairs={{0,16},{16,0},{1,17},{17,1},{2,18},{18,2},{3,19},{19,3},{4,20},{20... | collective-permute-start | bytes 3538952 | tf_op jit(solution)/shard_map/ppermute | solution.py:733
  161.2 21.2 %collective-permute-start.36 = (bf16[4,48,1536]{2,1,0:T(8,128)(2,1)S(1)}, bf16[4,48,1536]{2,1,0:T(8,128)(2,1)S(1)}, u32[]{:S(2)}, u32[]{:S(2)}) collective-permute-start(bf16[4,48,1536]{2,1,0:T(8,128)(2,1)S(1)} %pad_maximum_fusion.5), channel_id=1, source_target_pairs={{0,2},{1,3},{2,0},{3,1},{4,6},{5,7},{6,4},{7,5},{8,10},{9,11},{10,... | collective-permute-start | bytes 1769480 | tf_op jit(solution)/shard_map/ppermute | solution.py:729
  183.8 25.1 %collective-permute-start.40 = (bf16[8,48,1536]{2,1,0:T(8,128)(2,1)S(1)}, bf16[8,48,1536]{2,1,0:T(8,128)(2,1)S(1)}, u32[]{:S(2)}, u32[]{:S(2)}) collective-permute-start(bf16[8,48,1536]{2,1,0:T(8,128)(2,1)S(1)} %constant_dynamic-update-slice_fusion.25.refs_0_), channel_id=1, source_target_pairs={{0,16},{16,0},{1,17},{17,1},{2,18},{18,2},{3,19},{19,3},{4,20},{20... | collective-permute-start | bytes 3538952 | tf_op jit(solution)/shard_map/ppermute | solution.py:733
  249.1 43.4 %collective-permute-start.43 = (bf16[8,48,3072]{2,1,0:T(8,128)(2,1)}, bf16[8,48,3072]{2,1,0:T(8,128)(2,1)}, u32[]{:S(2)}, u32[]{:S(2)}) collective-permute-start(bf16[8,48,3072]{2,1,0:T(8,128)(2,1)} %get-tuple-element.338), channel_id=1, source_target_pairs={{0,1},{1,0},{2,3},{3,2},{4,5},{5,4},{6,7},{7,6},{8,9},{9,8},{10,11... | collective-permute-start | bytes 7077896 | tf_op jit(solution)/shard_map/ppermute | solution.py:729
  292.5 29.4 %collective-permute-start.44 = (bf16[16,48,1536]{2,1,0:T(8,128)(2,1)S(1)}, bf16[16,48,1536]{2,1,0:T(8,128)(2,1)S(1)}, u32[]{:S(2)}, u32[]{:S(2)}) collective-permute-start(bf16[16,48,1536]{2,1,0:T(8,128)(2,1)S(1)} %bitcast.211), channel_id=1, source_target_pairs={{0,16},{16,0},{1,17},{17,1},{2,18},{18,2},{3,19},{19,3},{4,20},{20... | collective-permute-start | bytes 7077896 | tf_op jit(solution)/shard_map/ppermute | solution.py:733
  296.2 25.6 %collective-permute-start.45 = (bf16[4,48,3072]{2,1,0:T(8,128)(2,1)}, bf16[4,48,3072]{2,1,0:T(8,128)(2,1)}, u32[]{:S(2)}, u32[]{:S(2)}) collective-permute-start(bf16[4,48,3072]{2,1,0:T(8,128)(2,1)} %get-tuple-element.353), channel_id=1, source_target_pairs={{0,2},{1,3},{2,0},{3,1},{4,6},{5,7},{6,4},{7,5},{8,10},{9,11},{10,... | collective-permute-start | bytes 3538952 | tf_op jit(solution)/shard_map/ppermute | solution.py:729
  326.5 22.7 %collective-permute-start.46 = (bf16[8,48,1536]{2,1,0:T(8,128)(2,1)}, bf16[8,48,1536]{2,1,0:T(8,128)(2,1)}, u32[]{:S(2)}, u32[]{:S(2)}) collective-permute-start(bf16[8,48,1536]{2,1,0:T(8,128)(2,1)} %get-tuple-element.366), channel_id=1, source_target_pairs={{0,1},{1,0},{2,3},{3,2},{4,5},{5,4},{6,7},{7,6},{8,9},{9,8},{10,11... | collective-permute-start | bytes 3538952 | tf_op jit(solution)/shard_map/ppermute | solution.py:729
  327.6 21.6 %collective-permute-start.47 = (bf16[1,48,3072]{2,1,0:T(8,128)(2,1)}, bf16[1,48,3072]{2,1,0:T(8,128)(2,1)}, u32[]{:S(2)}, u32[]{:S(2)}) collective-permute-start(bf16[1,48,3072]{2,1,0:T(8,128)(2,1)} %get-tuple-element.367), channel_id=1, source_target_pairs={{0,4},{1,5},{2,6},{3,7},{4,0},{5,1},{6,2},{7,3},{8,12},{9,13},{10,... | collective-permute-start | bytes 884744 | tf_op jit(solution)/shard_map/ppermute | solution.py:729
  327.6 21.6 %collective-permute-start.48 = (bf16[1,48,3072]{2,1,0:T(8,128)(2,1)S(1)}, bf16[1,48,3072]{2,1,0:T(8,128)(2,1)}, u32[]{:S(2)}, u32[]{:S(2)}) collective-permute-start(bf16[1,48,3072]{2,1,0:T(8,128)(2,1)S(1)} %get-tuple-element.368), channel_id=1, source_target_pairs={{0,8},{1,9},{2,10},{3,11},{4,12},{5,13},{6,14},{7,15},{8,0},{9,1},... | collective-permute-start | bytes 884744 | tf_op jit(solution)/shard_map/ppermute | solution.py:729
  375.9 28.9 %collective-permute-start.51 = (bf16[8,48,3072]{2,1,0:T(8,128)(2,1)S(1)}, bf16[8,48,3072]{2,1,0:T(8,128)(2,1)S(1)}, u32[]{:S(2)}, u32[]{:S(2)}) collective-permute-start(bf16[8,48,3072]{2,1,0:T(8,128)(2,1)S(1)} %get-tuple-element.393), channel_id=1, source_target_pairs={{0,1},{1,0},{2,3},{3,2},{4,5},{5,4},{6,7},{7,6},{8,9},{9,8},{10,11... | collective-permute-start | bytes 7077896 | tf_op jit(solution)/shard_map/ppermute | solution.py:729
  378.1 25.5 %collective-permute-start.54 = (bf16[1,48,3072]{2,1,0:T(8,128)(2,1)S(1)}, bf16[1,48,3072]{2,1,0:T(8,128)(2,1)S(1)}, u32[]{:S(2)}, u32[]{:S(2)}) collective-permute-start(bf16[1,48,3072]{2,1,0:T(8,128)(2,1)S(1)} %copy-done.103), channel_id=1, source_target_pairs={{0,12},{1,13},{2,14},{3,15},{4,8},{5,9},{6,10},{7,11},{8,4},{9,5},... | collective-permute-start | bytes 884744 | tf_op jit(solution)/shard_map/ppermute | solution.py:729
  379.9 23.7 %collective-permute-start.52 = (bf16[1,48,1536]{2,1,0:T(8,128)(2,1)S(1)}, bf16[1,48,1536]{2,1,0:T(8,128)(2,1)S(1)}, u32[]{:S(2)}, u32[]{:S(2)}) collective-permute-start(bf16[1,48,1536]{2,1,0:T(8,128)(2,1)S(1)} %get-tuple-element.394), channel_id=1, source_target_pairs={{0,4},{1,5},{2,6},{3,7},{4,0},{5,1},{6,2},{7,3},{8,12},{9,13},{10,... | collective-permute-start | bytes 442376 | tf_op jit(solution)/shard_map/ppermute | solution.py:729
  379.9 23.7 %collective-permute-start.53 = (bf16[1,48,1536]{2,1,0:T(8,128)(2,1)S(1)}, bf16[1,48,1536]{2,1,0:T(8,128)(2,1)S(1)}, u32[]{:S(2)}, u32[]{:S(2)}) collective-permute-start(bf16[1,48,1536]{2,1,0:T(8,128)(2,1)S(1)} %get-tuple-element.395), channel_id=1, source_target_pairs={{0,8},{1,9},{2,10},{3,11},{4,12},{5,13},{6,14},{7,15},{8,0},{9,1},... | collective-permute-start | bytes 442376 | tf_op jit(solution)/shard_map/ppermute | solution.py:729
  407.3 21.0 %collective-permute-start.55 = (bf16[4,48,3072]{2,1,0:T(8,128)(2,1)}, bf16[4,48,3072]{2,1,0:T(8,128)(2,1)}, u32[]{:S(2)}, u32[]{:S(2)}) collective-permute-start(bf16[4,48,3072]{2,1,0:T(8,128)(2,1)} %get-tuple-element.424), channel_id=1, source_target_pairs={{0,2},{1,3},{2,0},{3,1},{4,6},{5,7},{6,4},{7,5},{8,10},{9,11},{10,... | collective-permute-start | bytes 3538952 | tf_op jit(solution)/shard_map/ppermute | solution.py:729
  477.0 28.5 %collective-permute-start.68 = (bf16[48,3072]{1,0:T(8,128)(2,1)S(1)}, bf16[48,3072]{1,0:T(8,128)(2,1)S(1)}, u32[]{:S(2)}, u32[]{:S(2)}) collective-permute-start(bf16[48,3072]{1,0:T(8,128)(2,1)S(1)} %get-tuple-element.548), channel_id=1, source_target_pairs={{0,16},{16,0},{1,17},{17,1},{2,18},{18,2},{3,19},{19,3},{4,20},{20... | collective-permute-start | bytes 884744 | tf_op jit(solution)/shard_map/ppermute | solution.py:733
  479.2 27.6 %collective-permute-start.67 = (bf16[48,1536]{1,0:T(8,128)(2,1)}, bf16[48,1536]{1,0:T(8,128)(2,1)S(1)}, u32[]{:S(2)}, u32[]{:S(2)}) collective-permute-start(bf16[48,1536]{1,0:T(8,128)(2,1)} %get-tuple-element.546.refs_2_), channel_id=1, source_target_pairs={{0,16},{16,0},{1,17},{17,1},{2,18},{18,2},{3,19},{19,3},{4,20},{20... | collective-permute-start | bytes 442376 | tf_op jit(solution)/shard_map/ppermute | solution.py:733
  (201 other events, 1578.1 us)
